TPU v7x, 32 devices: a whole 2x2x4 slice. The times are simulated.
32 devices in a mesh: section: 4 (over y, x), seq: 8 (over z, core).
Axes of the slice: x: 2, y: 2, z: 4, core: 2. Of those that a mesh axis runs over, the one named last changes fastest.
Arguments:
- teacher_query_array: bfloat16 [4, 2048, 4096], P('section', 'seq'), may hold values from -8 to 8
- teacher_keys: bfloat16 [4, 2048, 512], P('section', 'seq'), may hold values from -8 to 8
- teacher_value_array: bfloat16 [4, 2048, 512], P('section', 'seq'), may hold values from -6 to 6
- projection: bfloat16 [4, 8, 512, 128], P('section'), may hold values from -0.25 to 0.25
- student_query_array: bfloat16 [4, 1024, 2048], P('section', 'seq'), may hold values from -8 to 8
- student_keys: bfloat16 [4, 1024, 512], P('section', 'seq'), may hold values from -8 to 8
- student_value_array: bfloat16 [4, 1024, 512], P('section', 'seq'), may hold values from -6 to 6
Outputs:
- grad_student_q: float32 [4, 1024, 2048], P('section', 'seq')
- grad_student_keys: float32 [4, 1024, 512], P('section', 'seq')
- grad_student_values: float32 [4, 1024, 512], P('section', 'seq')
- per_token_loss: float32 [4, 1024], P('section', 'seq')
All inputs are finite; a program needn't handle non-finite values.
Results may differ from a plain program's by a relative error of at most 0.03.
Values may be sent and summed in bfloat16 or wider, within the bound.
No kernel may reach another device: no remote copies, remote signals or barrier semaphores. Data moves between devices by JAX's collectives and lax.ppermute only.
A program may use at most 128 MiB of HBM per device.

v0:
```python
import math

import jax
import jax.numpy as jnp
from jax import lax
from jax.sharding import PartitionSpec as P

HEAD_SIZE = 128
TEACHER_Q_HEADS = 64
TEACHER_KV_HEADS = 8
STUDENT_Q_HEADS = 16
STUDENT_KV_HEADS = 4


floor_score = -1e30


def partner(value, axis, apart):
    mask = 2**apart
    pairs = [(source, source ^ mask) for source in range(lax.axis_size(axis))]
    return lax.ppermute(value, axis, pairs)


def blocking(row_count):
    return math.gcd(row_count, 512)


def absorb(carried, key_block, value_block, block_start, queries, query_pos):
    row_peak, row_total, weighted = carried
    inverse_root = 1.0 / math.sqrt(queries.shape[3])
    scores = (
        jnp.einsum("qgjd,kgd->gjqk", queries, key_block, preferred_element_type=jnp.float32)
        * inverse_root
    )
    key_pos = block_start + jnp.arange(key_block.shape[0], dtype=jnp.int32)
    allowed = key_pos[None, None, None, :] <= query_pos[None, None, :, None]
    scores = jnp.where(allowed, scores, floor_score)
    new_peak = jnp.maximum(row_peak, jnp.max(scores, axis=-1))
    rescale = jnp.exp(row_peak - new_peak)
    weights = jnp.where(allowed, jnp.exp(scores - new_peak[..., None]), 0.0)
    row_total = row_total * rescale + jnp.sum(weights, axis=-1)
    weighted = weighted * jnp.transpose(rescale, (2, 0, 1))[..., None] + jnp.einsum(
        "gjqk,kgd->qgjd",
        weights.astype(jnp.bfloat16),
        value_block,
        preferred_element_type=jnp.float32,
    )
    return (new_peak, row_total, weighted)


def online_pass(carried, key_rows, value_rows, queries, query_pos):
    row_count = key_rows.shape[0]
    rows_per_block = blocking(row_count)
    count_of_blocks = row_count // rows_per_block
    heads_of_keys = queries.shape[1]
    head_width = queries.shape[3]
    blocked_keys = key_rows.reshape(count_of_blocks, rows_per_block, heads_of_keys, head_width)
    blocked_values = value_rows.reshape(count_of_blocks, rows_per_block, heads_of_keys, head_width)
    last_query = query_pos[-1]

    def online_step(status, element):
        block_index, key_block, value_block = element
        block_start = block_index * rows_per_block
        status = lax.cond(
            block_start <= last_query,
            lambda current: absorb(
                current, key_block, value_block, block_start, queries, query_pos
            ),
            lambda current: current,
            status,
        )
        return (status, None)

    status, _ = lax.scan(
        online_step,
        carried,
        (jnp.arange(count_of_blocks, dtype=jnp.int32), blocked_keys, blocked_values),
    )
    return status


def fresh_state(queries):
    row_shape = (queries.shape[1], queries.shape[2], queries.shape[0])
    return (
        jnp.full(row_shape, floor_score, jnp.float32),
        jnp.zeros(row_shape, jnp.float32),
        jnp.zeros(queries.shape, jnp.float32),
    )


def finish(status):
    row_peak, row_total, weighted = status
    return weighted / jnp.transpose(row_total, (2, 0, 1))[..., None]


def body(
    teacher_query_array,
    teacher_keys,
    teacher_value_array,
    projection,
    student_query_array,
    student_keys,
    student_value_array,
):
    section_index = lax.axis_index("section")
    pair_bit = section_index % 2
    seq_index = lax.axis_index("seq")
    rows_of_teacher = teacher_query_array.shape[1]
    queries_of_teacher = teacher_query_array[0].reshape(
        rows_of_teacher, TEACHER_KV_HEADS // 2, TEACHER_Q_HEADS // TEACHER_KV_HEADS, HEAD_SIZE
    )
    teacher_pos = seq_index * rows_of_teacher + jnp.arange(rows_of_teacher, dtype=jnp.int32)
    status = online_pass(
        fresh_state(queries_of_teacher),
        lax.all_gather(teacher_keys[0], "seq", axis=0, tiled=True),
        lax.all_gather(teacher_value_array[0], "seq", axis=0, tiled=True),
        queries_of_teacher,
        teacher_pos,
    )
    context = (
        finish(status)
        .astype(jnp.bfloat16)
        .reshape(
            rows_of_teacher, STUDENT_Q_HEADS // 2, TEACHER_Q_HEADS // STUDENT_Q_HEADS * HEAD_SIZE
        )
    )
    target = jnp.einsum(
        "thf,hfe->the", context, projection[0], preferred_element_type=jnp.float32
    ).astype(jnp.bfloat16)
    rows_of_student = rows_of_teacher // 2
    own_target = lax.dynamic_slice_in_dim(target, pair_bit * rows_of_student, rows_of_student, 0)
    other_target = lax.dynamic_slice_in_dim(
        target, (1 - pair_bit) * rows_of_student, rows_of_student, 0
    )
    other_target = partner(other_target, "section", 0)
    rows_of_target = jnp.where(
        pair_bit == 0,
        jnp.concatenate([own_target, other_target], 1),
        jnp.concatenate([other_target, own_target], 1),
    )
    rows_of_target = rows_of_target.reshape(
        rows_of_student, STUDENT_KV_HEADS, STUDENT_Q_HEADS // STUDENT_KV_HEADS, HEAD_SIZE
    )
    own_keys = student_keys[0]
    own_values = student_value_array[0]
    far_keys, far_values = partner((own_keys, own_values), "section", 0)
    block_keys = jnp.where(
        pair_bit == 0,
        jnp.concatenate([own_keys, far_keys], 0),
        jnp.concatenate([far_keys, own_keys], 0),
    )
    block_values = jnp.where(
        pair_bit == 0,
        jnp.concatenate([own_values, far_values], 0),
        jnp.concatenate([far_values, own_values], 0),
    )
    every_key, every_value = (
        lax.all_gather(block_keys, "seq", axis=0, tiled=True),
        lax.all_gather(block_values, "seq", axis=0, tiled=True),
    )
    queries_of_student = student_query_array[0].reshape(
        rows_of_student, STUDENT_KV_HEADS, STUDENT_Q_HEADS // STUDENT_KV_HEADS, HEAD_SIZE
    )
    student_pos = (
        seq_index * 2 * rows_of_student
        + pair_bit * rows_of_student
        + jnp.arange(rows_of_student, dtype=jnp.int32)
    )
    status = online_pass(
        fresh_state(queries_of_student), every_key, every_value, queries_of_student, student_pos
    )
    row_peak, row_total, weighted = status
    student_context = finish(status)
    mismatch = student_context - rows_of_target.astype(jnp.float32)
    per_token_loss = jnp.mean(jnp.square(mismatch).reshape(rows_of_student, -1), axis=1)
    grad_context = mismatch.astype(jnp.bfloat16)
    row_delta = jnp.transpose(jnp.sum(mismatch * student_context, axis=-1), (1, 2, 0))
    row_total_count = every_key.shape[0]
    rows_per_block = blocking(row_total_count)
    count_of_blocks = row_total_count // rows_per_block
    blocked_keys = every_key.reshape(count_of_blocks, rows_per_block, STUDENT_KV_HEADS, HEAD_SIZE)
    blocked_values = every_value.reshape(
        count_of_blocks, rows_per_block, STUDENT_KV_HEADS, HEAD_SIZE
    )
    inverse_root = 1.0 / math.sqrt(HEAD_SIZE)
    last_query = student_pos[-1]

    def backward_step(query_gradient, element):
        block_index, key_block, value_block = element
        block_start = block_index * rows_per_block

        def active_block(query_gradient):
            key_pos = block_start + jnp.arange(rows_per_block, dtype=jnp.int32)
            allowed = key_pos[None, None, None, :] <= student_pos[None, None, :, None]
            scores = (
                jnp.einsum(
                    "qgjd,kgd->gjqk",
                    queries_of_student,
                    key_block,
                    preferred_element_type=jnp.float32,
                )
                * inverse_root
            )
            probability = jnp.where(
                allowed, jnp.exp(scores - row_peak[..., None]) / row_total[..., None], 0.0
            )
            grad_prob = jnp.einsum(
                "qgjd,kgd->gjqk", grad_context, value_block, preferred_element_type=jnp.float32
            )
            grad_score = (probability * (grad_prob - row_delta[..., None])).astype(jnp.bfloat16)
            query_gradient = query_gradient + jnp.einsum(
                "gjqk,kgd->qgjd", grad_score, key_block, preferred_element_type=jnp.float32
            )
            grad_key = (
                jnp.einsum(
                    "gjqk,qgjd->kgd",
                    grad_score,
                    queries_of_student,
                    preferred_element_type=jnp.float32,
                )
                * inverse_root
            )
            grad_value = jnp.einsum(
                "gjqk,qgjd->kgd",
                probability.astype(jnp.bfloat16),
                grad_context,
                preferred_element_type=jnp.float32,
            )
            return (
                query_gradient,
                jnp.concatenate(
                    [grad_key.reshape(rows_per_block, -1), grad_value.reshape(rows_per_block, -1)],
                    1,
                ),
            )

        def skipped_block(query_gradient):
            return (
                query_gradient,
                jnp.zeros((rows_per_block, 2 * STUDENT_KV_HEADS * HEAD_SIZE), jnp.float32),
            )

        return lax.cond(block_start <= last_query, active_block, skipped_block, query_gradient)

    query_gradient, terms_of_keys = lax.scan(
        backward_step,
        jnp.zeros(queries_of_student.shape, jnp.float32),
        (jnp.arange(count_of_blocks, dtype=jnp.int32), blocked_keys, blocked_values),
    )
    terms_of_keys = terms_of_keys.reshape(row_total_count, 2 * STUDENT_KV_HEADS * HEAD_SIZE)
    query_gradient = (query_gradient * inverse_root).reshape(
        rows_of_student, STUDENT_Q_HEADS * HEAD_SIZE
    )
    summed = lax.psum_scatter(
        terms_of_keys.astype(jnp.bfloat16), "seq", scatter_dimension=0, tiled=True
    ).astype(jnp.float32)
    own_part = lax.dynamic_slice_in_dim(summed, pair_bit * rows_of_student, rows_of_student, 0)
    far_part = lax.dynamic_slice_in_dim(
        summed, (1 - pair_bit) * rows_of_student, rows_of_student, 0
    )
    key_grads = own_part + partner(far_part.astype(jnp.bfloat16), "section", 0).astype(
        far_part.dtype
    )
    width_of_keys = STUDENT_KV_HEADS * HEAD_SIZE
    return (
        query_gradient[None],
        key_grads[:, :width_of_keys][None],
        key_grads[:, width_of_keys:][None],
        per_token_loss[None],
    )


def solution(mesh):
    in_specs = (
        P("section", "seq", None),
        P("section", "seq", None),
        P("section", "seq", None),
        P("section", None, None, None),
        P("section", "seq", None),
        P("section", "seq", None),
        P("section", "seq", None),
    )
    out_specs = (
        P("section", "seq", None),
        P("section", "seq", None),
        P("section", "seq", None),
        P("section", "seq"),
    )
    return jax.shard_map(body, mesh=mesh, in_specs=in_specs, out_specs=out_specs, check_vma=False)
```

profile of v0, /device:TPU:0, one launch (start us, length us, event | category | flops | bytes accessed | tf_op | source)
XLA Modules:
  0.0 338.9 jit_solution(2687442060411226346)
XLA Ops:
  7.2 0.7 all-gather.11.cloned.1.call-update
  8.0 0.7 all-gather.13.cloned.1.call-update
  8.7 3.0 collective-permute-start.1
  11.7 3.7 %collective-permute-done.1 = bf16[128,512]{1,0:T(8,128)(2,1)S(1)} collective-permute-done((bf16[128,512]{1,0:T(8,128)(2,1)}, bf16[128,512]{1,0:T(8,128)(2,1)S(1)}, u32[]{:S(2)}, u32[]{:S(2)}) %collective-permute-start.1) | collective-permute-done | bytes 131104 | tf_op jit(solution)/shard_map/ppermute | solution.py:21
  15.5 1.8 maximum_select_fusion.2
  17.3 1.8 collective-permute-start
  19.1 3.4 %collective-permute-done = bf16[128,512]{1,0:T(8,128)(2,1)S(1)} collective-permute-done((bf16[128,512]{1,0:T(8,128)(2,1)}, bf16[128,512]{1,0:T(8,128)(2,1)S(1)}, u32[]{:S(2)}, u32[]{:S(2)}) %collective-permute-start) | collective-permute-done | bytes 131104 | tf_op jit(solution)/shard_map/ppermute | solution.py:21
  22.5 1.8 maximum_select_fusion.1
  25.0 3.3 copy.36
  28.3 2.4 copy.38
  30.7 10.8 %all-gather.11.cloned.1.call-done = bf16[1,2048,512]{2,1,0:T(8,128)(2,1)} async-done(((bf16[1,256,512]{2,1,0:T(8,128)(2,1)}), bf16[1,2048,512]{2,1,0:T(8,128)(2,1)}) %all-gather.11.cloned.1.call-update) | async-done | bytes 2097168 | tf_op jit(solution)/shard_map/all_gather | solution.py:115
  41.5 2.5 reshape.179
  44.1 1.7 copy.37
  45.8 25.9 %all-gather.13.cloned.1.call-done = bf16[1,2048,512]{2,1,0:T(8,128)(2,1)} async-done(((bf16[1,256,512]{2,1,0:T(8,128)(2,1)}), bf16[1,2048,512]{2,1,0:T(8,128)(2,1)}) %all-gather.13.cloned.1.call-update) | async-done | bytes 2097168 | tf_op jit(solution)/shard_map/all_gather | solution.py:116
  71.7 2.5 reshape.180
  74.2 1.7 copy.39
  75.9 2.4 broadcast_in_dim.118
  78.4 25.5 %while.47 = (s32[]{:T(128)}, f32[4,8,256]{2,1,0:T(8,128)S(1)}, f32[4,8,256]{2,1,0:T(8,128)S(1)}, f32[256,4,8,128]{3,0,2,1:T(8,128)}, s32[4]{0:T(128)S(1)}, /*ind...) while((s32[]{:T(128)}, f32[4,8,256]{2,1,0:T(8,128)S(1)}, ...), condition=%wide.region_11.12_spmd.clone, body=%wide.region_6.11_spmd.clone.sunk | while | flops 2204263168 | bytes 62924072 | solution.py:74
  80.4 17.5 %conditional.10 = ((f32[4,8,256]{2,1,0:T(8,128)S(1)}, f32[4,8,256]{2,1,0:T(8,128)S(1)}, f32[256,4,8,128]{3,0,2,1:T(8,128)})) conditional(s32[]{:T(128)} %convert_element_type.96, (f32[4,8,256]{2,1,0:T(8,128)S(1)}, f32[4,8,256]{2,1,0:T(8,128)S(1)}, f32[256,4,8,128]{3,0,2,1:T(8,128)}) %tuple.116, (s32[]{:T(128)}, s32[]{:T(128)}, ...), branch_computations={%region_7.7_spmd, %region_8.10_spmd} | conditional | flops 2204263168 | bytes 62922792 | solution.py:64
  80.5 4.3 %fusion.29 = (f32[4,8,256]{2,1,0:T(8,128)S(1)}, f32[4,512,256,8]{2,1,3,0:T(8,128)S(1)}) fusion(pred[256,512]{0,1:T(8,128)(4,1)S(1)} %broadcast_compare_fusion.1, bf16[256,4,8,128]{3,0,2,1:T(8,128)(2,1)} %get-tuple-element.381, bf16[4,512,4,128]{3,1,2,0:T(8,128)(2,1)} %get-tuple-element.379, s32[]{:T(128)} %get-tuple-element.380), kind=kOutput, calls=%fused_computation.30 | convolution fusion | flops 1086316544 | bytes 19563008 | tf_op jit(solution)/shard_map/while/body/eval_jaxpr/cond/branch_1_fun/qgjd,kgd->gjqk/dot_general | solution.py:32
  84.9 4.2 %fusion.31 = f32[4,8,256]{2,1,0:T(8,128)S(1)} fusion(f32[4,512,256,8]{2,1,3,0:T(8,128)S(1)} %get-tuple-element.656, f32[4,8,256]{2,1,0:T(8,128)S(1)} %get-tuple-element.887, pred[256,512]{0,1:T(8,128)(4,1)S(1)} %broadcast_compare_fusion.1), kind=kLoop, calls=%fused_computation.32 | loop fusion | flops 20963328 | bytes 16973824 | tf_op jit(solution)/shard_map/while/body/eval_jaxpr/cond/branch_1_fun/reduce_sum | solution.py:41
  89.1 8.7 %bitcast_add_fusion = f32[256,4,8,128]{3,0,2,1:T(8,128)} fusion(f32[256,4,8,128]{3,0,2,1:T(8,128)} %get-tuple-element.383, f32[4,512,256,8]{2,1,3,0:T(8,128)S(1)} %get-tuple-element.656, f32[4,8,256]{2,1,0:T(8,128)S(1)} %get-tuple-element.887, pred[256,512]{0,1:T(8,128)(4,1)S(1)} %broadcast_compare_fusion.1, f32[256,4,8]{0,2,1:T(8,128)S(1)} %get-tuple-element.649, ...), kind=kOutput, calls=%fused_computation.35 | convolution fusion | flops 1096810496 | bytes 25887232 | tf_op jit(solution)/shard_map/while/body/eval_jaxpr/cond/branch_1_fun/gjqk,kgd->qgjd/dot_general | solution.py:42
  103.9 5.4 %copy.40 = f32[256,4,8,128]{0,3,2,1:T(8,128)} copy(f32[256,4,8,128]{3,0,2,1:T(8,128)} %get-tuple-element.440) | data formatting | bytes 8388608 | tf_op jit(solution)/shard_map/while | solution.py:74
  109.3 2.9 divide_convert_fusion
  112.8 0.8 dynamic-slice_bitcast_fusion
  113.6 1.3 collective-permute-start.2
  115.5 1.0 copy.31
  116.6 1.3 copy.33
  117.9 2.6 reshape.178
  120.5 1.7 copy.34
  122.2 10.9 %all-gather.7.cloned.1.call-done = bf16[2048,512]{1,0:T(8,128)(2,1)} async-done(((bf16[256,512]{1,0:T(8,128)(2,1)}), bf16[2048,512]{1,0:T(8,128)(2,1)}) %all-gather.7.cloned.1.call-update) | async-done | bytes 2097168 | tf_op jit(solution)/shard_map/all_gather | solution.py:158
  133.0 4.0 %reshape.177 = bf16[4,512,4,128]{3,2,1,0:T(4,128)(2,1)} reshape(bf16[2048,512]{1,0:T(8,128)(2,1)} %all-gather.7.cloned.1.call-done) | data formatting | bytes 4194304 | tf_op jit(solution)/shard_map/reshape | solution.py:181
  137.1 2.0 copy.43
  139.1 1.1 broadcast.153.clone
  140.2 13.6 %while.46 = (s32[]{:T(128)}, f32[4,4,128]{2,1,0:T(4,128)S(1)}, f32[4,4,128]{2,1,0:T(4,128)S(1)}, f32[128,4,4,128]{3,0,2,1:T(8,128)}, s32[4]{0:T(128)S(1)}, /*ind...) while((s32[]{:T(128)}, f32[4,4,128]{2,1,0:T(4,128)S(1)}, ...), condition=%wide.region_5.6_spmd.clone, body=%wide.region_0.5_spmd.clone.sunk | while | flops 551099008 | bytes 25041768 | solution.py:74
  142.1 5.7 %conditional.9 = ((f32[4,4,128]{2,1,0:T(4,128)S(1)}, f32[4,4,128]{2,1,0:T(4,128)S(1)}, f32[128,4,4,128]{3,0,2,1:T(8,128)})) conditional(s32[]{:T(128)} %convert_element_type.95, (f32[4,4,128]{2,1,0:T(4,128)S(1)}, f32[4,4,128]{2,1,0:T(4,128)S(1)}, f32[128,4,4,128]{3,0,2,1:T(8,128)}) %tuple.113, (s32[]{:T(128)}, s32[]{:T(128)}, ...), branch_computations={%region_1.1_spmd, %region_2.4_spmd} | conditional | flops 551099008 | bytes 25040996 | solution.py:64
  142.3 0.7 fusion.6
  143.1 1.0 fusion.8
  144.1 2.7 fusion.15
  146.8 1.0 copy-done.4
  153.7 3.4 copy.35
  157.1 0.7 copy-done.6
  157.8 1.7 fusion.67
  159.5 1.5 multiply_reduce_fusion
  161.1 21.6 %while.48 = (s32[]{:T(128)}, f32[128,4,4,128]{3,0,2,1:T(8,128)S(1)}, bf16[4,512,1024]{1,2,0:T(8,128)(2,1)}, s32[4]{0:T(128)S(1)}, s32[]{:T(128)}, /*index=5*/bf1...) while((s32[]{:T(128)}, ...), condition=%wide.region_16.17_spmd.clone, body=%wide.region_13.16_spmd.clone.sunk | while | flops 1353515648 | bytes 30048556 | solution.py:245
  163.0 9.3 %conditional.11 = (f32[128,4,4,128]{3,0,2,1:T(8,128)S(1)}, bf16[1,512,1024]{1,2,0:T(8,128)(2,1)S(1)}) conditional(s32[]{:T(128)} %convert_element_type.97, f32[128,4,4,128]{3,0,2,1:T(8,128)S(1)} %get-tuple-element.982, (s32[]{:T(128)}, s32[]{:T(128)}, bf16[4,512,4,128]{3,1,2,0:T(8,128)(2,1)}, s32[]{:T(128)}, bf16[128,4,4,128]{0,3,2,1:T(8,128)(2,1)}, ...), branch_computations={%region_14.14_spmd, %region_15.15_spmd} | conditional | flops 1353515648 | bytes 27950104 | solution.py:243
  163.2 2.3 fusion.52
  165.5 1.8 fusion.49
  167.3 1.9 fusion.56
  169.1 0.8 fusion.53
  170.0 2.3 fusion.55
  172.3 1.1 constant_dynamic-update-slice_fusion.2
  175.4 1.0 constant_dynamic-update-slice_fusion.2
  178.5 1.1 constant_dynamic-update-slice_fusion.2
  181.6 1.0 constant_dynamic-update-slice_fusion.2
  182.7 6.3 %copy.46 = bf16[4,512,1024]{2,1,0:T(8,128)(2,1)} copy(bf16[4,512,1024]{1,2,0:T(8,128)(2,1)} %get-tuple-element.443) | data formatting | bytes 8388608 | tf_op jit(solution)/shard_map/convert_element_type | solution.py:255
  189.0 134.0 %reduce-scatter.2.cloned.1.call-done = bf16[256,1024]{1,0:T(8,128)(2,1)} async-done(((bf16[2048,1024]{1,0:T(8,128)(2,1)}), bf16[256,1024]{1,0:T(8,128)(2,1)}) %reduce-scatter.2.cloned.1.call-update) | async-done | bytes 524304 | tf_op jit(solution)/shard_map/reduce_scatter | solution.py:254
  323.0 1.1 convert_element_type.67
  324.1 0.7 dynamic-slice_convert_fusion
  324.9 1.5 collective-permute-start.3
  326.4 0.7 copy.45
  327.1 1.4 broadcast_in_dim_reshape.3
  329.0 2.4 collective-permute-done.3
  331.5 0.8 slice_bitcast_fusion
  (91 shorter events, 11.5 us)
Async XLA Ops:
  7.2 105.1 %copy-start = (bf16[1,8,512,128]{3,2,1,0:T(8,128)(2,1)S(1)}, bf16[1,8,512,128]{3,2,1,0:T(8,128)(2,1)}, u32[]{:S(2)}) copy-start(bf16[1,8,512,128]{3,2,1,0:T(8,128)(2,1)} %param.22) | copy-start | bytes 3145732
  7.2 34.3 %all-gather.11.cloned.1.call-start = ((), (), s32[]{:S(2)}) async-start(), calls=%async_computation.4 | async-start | bytes 2359296 | tf_op jit(solution)/shard_map/all_gather | solution.py:115
  7.9 63.8 %all-gather.13.cloned.1.call-start = ((), (), s32[]{:S(2)}) async-start(), calls=%async_computation.5 | async-start | bytes 2359296 | tf_op jit(solution)/shard_map/all_gather | solution.py:116
  8.7 109.2 %all-gather.9.cloned.1.call-start = ((), (), s32[]{:S(2)}) async-start(), calls=%async_computation.2 | async-start | bytes 2359296 | tf_op jit(solution)/shard_map/all_gather | solution.py:159
  8.7 6.7 %collective-permute-start.1 = (bf16[128,512]{1,0:T(8,128)(2,1)}, bf16[128,512]{1,0:T(8,128)(2,1)S(1)}, u32[]{:S(2)}, u32[]{:S(2)}) collective-permute-start(bf16[128,512]{1,0:T(8,128)(2,1)} %bitcast.179), channel_id=1, source_target_pairs={{0,8},{8,0},{16,24},{24,16},{1,9},{9,1},{17,25},{25,17},{2,10},{10... | collective-permute-start | bytes 393224 | tf_op jit(solution)/shard_map/ppermute | solution.py:21
  17.2 115.8 %all-gather.7.cloned.1.call-start = ((), (), s32[]{:S(2)}) async-start(), calls=%async_computation.1 | async-start | bytes 2359296 | tf_op jit(solution)/shard_map/all_gather | solution.py:158
  17.3 5.2 %collective-permute-start = (bf16[128,512]{1,0:T(8,128)(2,1)}, bf16[128,512]{1,0:T(8,128)(2,1)S(1)}, u32[]{:S(2)}, u32[]{:S(2)}) collective-permute-start(bf16[128,512]{1,0:T(8,128)(2,1)} %bitcast.181), channel_id=1, source_target_pairs={{0,8},{8,0},{16,24},{24,16},{1,9},{9,1},{17,25},{25,17},{2,10},{10... | collective-permute-start | bytes 393224 | tf_op jit(solution)/shard_map/ppermute | solution.py:21
  24.3 298.7 %reduce-scatter.2.cloned.1.call-start = ((), (), s32[]{:S(2)}) async-start(), calls=%async_computation.3 | async-start | bytes 4718592 | tf_op jit(solution)/shard_map/reduce_scatter | solution.py:254
  109.3 6.2 %copy-start.5 = (bf16[1,128,2048]{2,1,0:T(8,128)(2,1)S(1)}, bf16[1,128,2048]{2,1,0:T(8,128)(2,1)}, u32[]{:S(2)}) copy-start(bf16[1,128,2048]{2,1,0:T(8,128)(2,1)} %param.23) | copy-start | bytes 1572868
  113.6 43.5 %collective-permute-start.2 = (bf16[128,8,128]{0,2,1:T(8,128)(2,1)}, bf16[128,8,128]{0,2,1:T(8,128)(2,1)S(1)}, u32[]{:S(2)}, u32[]{:S(2)}) collective-permute-start(bf16[128,8,128]{0,2,1:T(8,128)(2,1)} %get-tuple-element.659), channel_id=1, source_target_pairs={{0,8},{8,0},{16,24},{24,16},{1,9},{9,1},{17,25},{25,17},{2,10},{10... | collective-permute-start | bytes 786440 | tf_op jit(solution)/shard_map/ppermute | solution.py:21
  142.3 1.8 copy-start.3
  146.8 1.0 copy-start.4
  153.7 7.3 %copy-start.2 = (bf16[4,512,4,128]{3,1,2,0:T(8,128)(2,1)}, bf16[4,512,4,128]{3,1,2,0:T(8,128)(2,1)S(1)}, u32[]{:S(2)}) copy-start(bf16[4,512,4,128]{3,1,2,0:T(8,128)(2,1)S(1)} %get-tuple-element.1018) | copy-start | bytes 6291460
  157.1 0.7 copy-start.6
  324.9 6.6 %collective-permute-start.3 = (bf16[128,1024]{1,0:T(8,128)(2,1)}, bf16[128,1024]{1,0:T(8,128)(2,1)S(1)}, u32[]{:S(2)}, u32[]{:S(2)}) collective-permute-start(bf16[128,1024]{1,0:T(8,128)(2,1)} %dynamic-slice_convert_fusion), channel_id=1, source_target_pairs={{0,8},{8,0},{16,24},{24,16},{1,9},{9,1},{17,25},{25,17},{2,10},{10... | collective-permute-start | bytes 786440 | tf_op jit(solution)/shard_map/ppermute | solution.py:21
  326.3 6.0 %copy-start.1 = (bf16[1,8,512,128]{3,2,1,0:T(8,128)(2,1)S(1)}, bf16[1,8,512,128]{3,2,1,0:T(8,128)(2,1)}, u32[]{:S(2)}) copy-start(bf16[1,8,512,128]{3,2,1,0:T(8,128)(2,1)} %param.22) | copy-start | bytes 3145732
Sparse Core Ops, SparseCore 0:
  9.6 31.8 all-gather.10
  43.1 28.5 all-gather.12
  73.9 28.5 all-gather.8
  104.5 28.5 all-gather.6
  189.1 133.8 reduce-scatter.1
where the time goes:
time: 341 us; the launch traced here: 339 us
  waiting for transfers between devices  193 us (57%)
  local copies, waits for them, and re-layouts  64.7 us (19%)
  matrix products  26 us (8%)
  other arithmetic  17.2 us (5%)
  loops' own time  16.6 us (5%)
  between operations  14 us (4%)
  starting transfers between devices  7.77 us (2%)
    reduce_scatter x1, waiting for transfers between devices, body(): lax.psum_scatter(terms_of_keys.astype(jnp.bfloat16), 'seq', scatter_dimen...  134 us
    all_gather x1, waiting for transfers between devices, body(): lax.all_gather(teacher_value_array[0], 'seq', axis=0, tiled=True)  25.9 us
    unnamed x18, local copies, waits for them, and re-layouts  15.9 us
    dot_general x2, matrix products, absorb(): jnp.einsum('gjqk,kgd->qgjd', weights.astype(jnp.bfloat16), value_block, p...  11.4 us
    all_gather x1, waiting for transfers between devices, body(): lax.all_gather(block_keys, 'seq', axis=0, tiled=True)  10.9 us
    all_gather x1, waiting for transfers between devices, body(): lax.all_gather(teacher_keys[0], 'seq', axis=0, tiled=True)  10.8 us
    another operation x2, loops' own time, online_pass(): lax.scan(online_step, carried, (jnp.arange(count_of_blocks, dtype=jnp.int...  10.8 us
    ppermute x4, waiting for transfers between devices, partner(): return lax.ppermute(value, axis, pairs)  9.56 us
  transfers between devices with their start and end apart: 9, of which 7 were waited for; matrix products, arithmetic and copies ran while one was open for 23% of the time, Pallas kernels for 0%

commit v1 on v0

v1 whole, which is shorter than its diff:
```python
import functools
import math

import jax
import jax.numpy as jnp
from jax import lax
from jax.experimental import pallas as pl
from jax.experimental.pallas import tpu as pltpu
from jax.sharding import PartitionSpec as P

HEAD = 128
TEACHER_Q_HEADS = 64
TEACHER_KV_HEADS = 8
STUDENT_Q_HEADS = 16
STUDENT_KV_HEADS = 4
GROUP_T = TEACHER_Q_HEADS // TEACHER_KV_HEADS
GROUP_S = STUDENT_Q_HEADS // STUDENT_KV_HEADS
PER_TARGET = TEACHER_Q_HEADS // STUDENT_Q_HEADS

floor_score = -1e30
inverse_root = 1.0 / math.sqrt(HEAD)
exp2_scale = inverse_root * math.log2(math.e)
vmem_limit = 60 * 1024 * 1024


def dot(left, right):
    return lax.dot_general(
        left, right, (((1,), (0,)), ((), ())), preferred_element_type=jnp.float32
    )


def shift(value, chips, least=0):
    size = lax.axis_size("seq")
    pairs = [(i, i + 2 * chips) for i in range(2 * least, size - 2 * chips)]
    return lax.ppermute(value, "seq", pairs)


def back(value, chips):
    size = lax.axis_size("seq")
    pairs = [(i, i - 2 * chips) for i in range(2 * chips, size)]
    return lax.ppermute(value, "seq", pairs)


def swap(value, axis):
    pairs = [(i, i ^ 1) for i in range(lax.axis_size(axis))]
    return lax.ppermute(value, axis, pairs)


def spread(own):
    chips = lax.axis_size("seq") // 2
    mine = [own]
    for step in range(1, chips):
        if step <= 2:
            mine.append(shift(own, step))
        else:
            mine.append(shift(mine[-1], 1, step - 1))
    return [(block, swap(block, "seq")) for block in mine]


def fold_max(tile):
    return jnp.max(tile.reshape(-1, 8, tile.shape[1]), axis=0)


def fold_sum(tile):
    return jnp.sum(tile.reshape(-1, 8, tile.shape[1]), axis=0)


def teacher_kernel(chips, rows, info, q_ref, *refs):
    key_refs = refs[: 2 * chips]
    value_refs = refs[2 * chips : 4 * chips]
    proj_ref, out_ref = refs[4 * chips : 4 * chips + 2]
    keys, values_t, query_t, scores, total, context = refs[4 * chips + 2 :]
    chip, core = info[0], info[1]
    wide = 2 * rows
    for b in range(chips):
        for half in range(2):
            part = pl.ds(half * rows, rows)
            keys[b, part, :] = key_refs[2 * b + half][...]
            values_t[b, :, part] = value_refs[2 * b + half][...].T
    for h in range(GROUP_T):
        query_t[h] = q_ref[:, h * HEAD : (h + 1) * HEAD].T

    key_id = lax.broadcasted_iota(jnp.int32, (wide, rows), 0)
    row_id = lax.broadcasted_iota(jnp.int32, (wide, rows), 1)
    ahead = jnp.where(key_id < rows, key_id, key_id + (1 - 2 * core) * rows - rows)
    allowed = ahead <= row_id

    def score(h, slot, b, peak, diagonal):
        tile = dot(keys[b], query_t[h])
        if diagonal:
            tile = jnp.where(allowed, tile, floor_score)
        scores[slot, b] = tile
        return jnp.maximum(peak, fold_max(tile))

    def absorb(slot, b, shifted, row_sum, first):
        weights = jnp.exp2(scores[slot, b] * exp2_scale - shifted)
        added = dot(values_t[b], weights.astype(jnp.bfloat16))
        total[...] = added if first else total[...] + added
        return row_sum + fold_sum(weights)

    def reduced(peak):
        return jnp.max(peak, axis=0, keepdims=True) * exp2_scale

    def finish(h, row_sum):
        denominator = jnp.sum(row_sum, axis=0, keepdims=True)
        start = pl.multiple_of(h * HEAD, HEAD)
        context[pl.ds(start, HEAD), :] = (total[...] / denominator).astype(jnp.bfloat16)

    low = jnp.full((8, rows), floor_score, jnp.float32)
    none = jnp.zeros((8, rows), jnp.float32)

    peak = score(0, 0, 0, low, True)
    peak = lax.fori_loop(1, chip + 1, lambda b, p: score(0, 0, b, p, False), peak)

    def head(h, peak):
        slot = lax.rem(h, 2)
        shifted = reduced(peak)
        new_peak = score(h, slot, 0, low, True)
        row_sum = absorb(1 - slot, 0, shifted, none, True)

        def block(b, carried):
            new_peak, row_sum = carried
            new_peak = score(h, slot, b, new_peak, False)
            row_sum = absorb(1 - slot, b, shifted, row_sum, False)
            return new_peak, row_sum

        new_peak, row_sum = lax.fori_loop(1, chip + 1, block, (new_peak, row_sum))
        finish(h - 1, row_sum)
        return new_peak

    peak = lax.fori_loop(1, GROUP_T, head, peak)
    shifted = reduced(peak)
    slot = (GROUP_T - 1) % 2
    row_sum = absorb(slot, 0, shifted, none, True)
    row_sum = lax.fori_loop(
        1, chip + 1, lambda b, r: absorb(slot, b, shifted, r, False), row_sum
    )
    finish(GROUP_T - 1, row_sum)
    deep = PER_TARGET * HEAD
    for t in range(GROUP_T // PER_TARGET):
        made = dot(proj_ref[t].T, context[t * deep : (t + 1) * deep, :])
        out_ref[t * HEAD : (t + 1) * HEAD, :] = made.astype(jnp.bfloat16)


def teacher(info, queries, blocks, projection, first_head, heads):
    chips = len(blocks)
    rows = queries.shape[0]
    flat = [part for pair in blocks for part in pair]
    targets = GROUP_T // PER_TARGET
    in_specs = [pl.BlockSpec((rows, GROUP_T * HEAD), lambda g, i: (0, first_head + g))]
    in_specs += [pl.BlockSpec((rows, HEAD), lambda g, i: (0, g))] * len(flat)
    in_specs += [pl.BlockSpec((rows, HEAD), lambda g, i: (0, heads + g))] * len(flat)
    in_specs += [
        pl.BlockSpec(
            (targets, PER_TARGET * HEAD, HEAD), lambda g, i: (first_head + g, 0, 0)
        )
    ]
    wide = 2 * rows
    work = heads * GROUP_T * rows * chips * wide
    return pl.pallas_call(
        functools.partial(teacher_kernel, chips, rows),
        out_shape=jax.ShapeDtypeStruct((heads * targets * HEAD, rows), jnp.bfloat16),
        grid_spec=pltpu.PrefetchScalarGridSpec(
            num_scalar_prefetch=1,
            grid=(heads,),
            in_specs=in_specs,
            out_specs=pl.BlockSpec((targets * HEAD, rows), lambda g, i: (g, 0)),
            scratch_shapes=[
                pltpu.VMEM((chips, wide, HEAD), jnp.bfloat16),
                pltpu.VMEM((chips, HEAD, wide), jnp.bfloat16),
                pltpu.VMEM((GROUP_T, HEAD, rows), jnp.bfloat16),
                pltpu.VMEM((2, chips, wide, rows), jnp.float32),
                pltpu.VMEM((HEAD, rows), jnp.float32),
                pltpu.VMEM((GROUP_T * HEAD, rows), jnp.bfloat16),
            ],
        ),
        compiler_params=pltpu.CompilerParams(
            dimension_semantics=("arbitrary",), vmem_limit_bytes=vmem_limit
        ),
        cost_estimate=pl.CostEstimate(
            flops=4 * HEAD * work, bytes_accessed=4 * wide * HEAD * chips, transcendentals=work
        ),
        name="teacher",
    )(info, queries, *flat, *flat, projection)


def student_kernel(chips, rows, info, own_q_ref, far_q_ref, target_ref, *refs):
    key_refs = refs[: 2 * chips]
    value_refs = refs[2 * chips : 4 * chips]
    near_ref, away_ref, loss_ref, kept_ref, sent_ref = refs[4 * chips : 4 * chips + 5]
    (
        keys,
        keys_t,
        values,
        values_t,
        query,
        query_t,
        scores,
        total,
        key_sum,
        value_sum,
        query_sum,
        loss_sum,
    ) = refs[4 * chips + 5 :]
    chip, core, bit = info[0], info[1], info[2]
    wide = 2 * rows
    half_rows = rows // 2
    for b in range(chips):
        for half in range(2):
            part = pl.ds(half * rows, rows)
            key_block = key_refs[2 * b + half][...]
            value_block = value_refs[2 * b + half][...]
            keys[b, part, :] = key_block
            keys_t[b, :, part] = key_block.T
            values[b, part, :] = value_block
            values_t[b, :, part] = value_block.T
    mine = pl.ds(pl.multiple_of(bit * half_rows, half_rows), half_rows)
    other = pl.ds(pl.multiple_of((1 - bit) * half_rows, half_rows), half_rows)
    for h in range(GROUP_S):
        query[h, mine, :] = own_q_ref[:, h * HEAD : (h + 1) * HEAD]
        query[h, other, :] = far_q_ref[:, h * HEAD : (h + 1) * HEAD]
    for h in range(GROUP_S):
        query_t[h] = query[h].T

    key_id = lax.broadcasted_iota(jnp.int32, (wide, rows), 0)
    row_id = lax.broadcasted_iota(jnp.int32, (wide, rows), 1)
    within = lax.rem(key_id, rows)
    place = jnp.where(within < half_rows, within + bit * half_rows, within - bit * half_rows)
    ahead = jnp.where(key_id < rows, place, place + (1 - 2 * core) * rows)
    allowed = ahead <= row_id

    low = jnp.full((8, rows), floor_score, jnp.float32)
    none = jnp.zeros((8, rows), jnp.float32)
    loss_sum[...] = jnp.zeros_like(loss_sum)

    def head(h, first):
        def score(b, peak, diagonal):
            tile = dot(keys[b], query_t[h])
            if diagonal:
                tile = jnp.where(allowed, tile, floor_score)
            scores[b] = tile
            return jnp.maximum(peak, fold_max(tile))

        peak = score(0, low, True)
        peak = lax.fori_loop(1, chip + 1, lambda b, p: score(b, p, False), peak)
        shifted = jnp.max(peak, axis=0, keepdims=True) * exp2_scale

        def absorb(b, row_sum, first):
            weights = jnp.exp2(scores[b] * exp2_scale - shifted)
            scores[b] = weights
            added = dot(values_t[b], weights.astype(jnp.bfloat16))
            total[...] = added if first else total[...] + added
            return row_sum + fold_sum(weights)

        row_sum = absorb(0, none, True)
        row_sum = lax.fori_loop(1, chip + 1, lambda b, r: absorb(b, r, False), row_sum)
        inverse = 1.0 / jnp.sum(row_sum, axis=0, keepdims=True)
        made = total[...] * inverse
        start = pl.multiple_of(h * HEAD, HEAD)
        mismatch = made - target_ref[pl.ds(start, HEAD), :].astype(jnp.float32)
        loss_sum[...] += fold_sum(jnp.square(mismatch))
        delta = jnp.sum(mismatch * made, axis=0, keepdims=True)
        grad_t = mismatch.astype(jnp.bfloat16)
        grad = mismatch.T.astype(jnp.bfloat16)

        def gradient(b, start):
            prob = scores[b] * inverse
            grad_prob = dot(values[b], grad_t)
            grad_score = (prob * (grad_prob - delta)).astype(jnp.bfloat16)
            added = dot(keys_t[b], grad_score)
            total[...] = added if start else total[...] + added
            key_added = dot(grad_score, query[h])
            value_added = dot(prob.astype(jnp.bfloat16), grad)
            if first:
                key_sum[b] = key_added
                value_sum[b] = value_added
            else:
                key_sum[b] += key_added
                value_sum[b] += value_added

        gradient(0, True)
        lax.fori_loop(1, chip + 1, lambda b, c: (gradient(b, False), c)[1], 0)
        query_sum[h] = (total[...] * inverse_root).T

    head(0, True)
    lax.fori_loop(1, GROUP_S, lambda h, c: (head(h, False), c)[1], 0)
    for h in range(GROUP_S):
        near_ref[:, h * HEAD : (h + 1) * HEAD] = query_sum[h, mine, :]
        away_ref[:, h * HEAD : (h + 1) * HEAD] = query_sum[h, other, :].astype(jnp.bfloat16)
    loss_ref[...] = loss_sum[...]
    for b in range(chips):

        @pl.when(b <= chip)
        def _():
            kept_ref[b, :, :HEAD] = key_sum[b, :rows, :] * inverse_root
            kept_ref[b, :, HEAD:] = value_sum[b, :rows, :]
            sent_ref[b, :, :HEAD] = (key_sum[b, rows:, :] * inverse_root).astype(jnp.bfloat16)
            sent_ref[b, :, HEAD:] = value_sum[b, rows:, :].astype(jnp.bfloat16)


def student(info, own_queries, far_queries, target, blocks, pair, heads):
    chips = len(blocks)
    rows = blocks[0][0].shape[0]
    half_rows = rows // 2
    wide = 2 * rows
    flat = [part for both in blocks for part in both]
    width = GROUP_S * HEAD
    full = lambda i, info: (0, 0)
    in_specs = [
        pl.BlockSpec((half_rows, width), lambda i, info: (0, info[2] * heads + pair)),
        pl.BlockSpec((half_rows, width), lambda i, info: (0, pair)),
        pl.BlockSpec((width, rows), full),
    ]
    in_specs += [pl.BlockSpec((rows, HEAD), lambda i, info: (0, pair))] * len(flat)
    in_specs += [pl.BlockSpec((rows, HEAD), lambda i, info: (0, heads + pair))] * len(flat)
    work = GROUP_S * rows * chips * wide
    return pl.pallas_call(
        functools.partial(student_kernel, chips, rows),
        out_shape=(
            jax.ShapeDtypeStruct((half_rows, width), jnp.float32),
            jax.ShapeDtypeStruct((half_rows, width), jnp.bfloat16),
            jax.ShapeDtypeStruct((8, rows), jnp.float32),
            jax.ShapeDtypeStruct((chips, rows, 2 * HEAD), jnp.float32),
            jax.ShapeDtypeStruct((chips, rows, 2 * HEAD), jnp.bfloat16),
        ),
        grid_spec=pltpu.PrefetchScalarGridSpec(
            num_scalar_prefetch=1,
            grid=(1,),
            in_specs=in_specs,
            out_specs=(
                pl.BlockSpec((half_rows, width), full),
                pl.BlockSpec((half_rows, width), full),
                pl.BlockSpec((8, rows), full),
                pl.BlockSpec((chips, rows, 2 * HEAD), lambda i, info: (0, 0, 0)),
                pl.BlockSpec((chips, rows, 2 * HEAD), lambda i, info: (0, 0, 0)),
            ),
            scratch_shapes=[
                pltpu.VMEM((chips, wide, HEAD), jnp.bfloat16),
                pltpu.VMEM((chips, HEAD, wide), jnp.bfloat16),
                pltpu.VMEM((chips, wide, HEAD), jnp.bfloat16),
                pltpu.VMEM((chips, HEAD, wide), jnp.bfloat16),
                pltpu.VMEM((GROUP_S, rows, HEAD), jnp.bfloat16),
                pltpu.VMEM((GROUP_S, HEAD, rows), jnp.bfloat16),
                pltpu.VMEM((chips, wide, rows), jnp.float32),
                pltpu.VMEM((HEAD, rows), jnp.float32),
                pltpu.VMEM((chips, wide, HEAD), jnp.float32),
                pltpu.VMEM((chips, wide, HEAD), jnp.float32),
                pltpu.VMEM((GROUP_S, rows, HEAD), jnp.float32),
                pltpu.VMEM((8, rows), jnp.float32),
            ],
        ),
        compiler_params=pltpu.CompilerParams(
            dimension_semantics=("arbitrary",), vmem_limit_bytes=vmem_limit
        ),
        cost_estimate=pl.CostEstimate(
            flops=12 * HEAD * work, bytes_accessed=8 * wide * HEAD * chips, transcendentals=work
        ),
        name="student",
    )(info, own_queries, far_queries, target, *flat, *flat)


def body(
    teacher_query_array,
    teacher_keys,
    teacher_value_array,
    projection,
    student_query_array,
    student_keys,
    student_value_array,
):
    bit = lax.axis_index("section") % 2
    seq = lax.axis_index("seq")
    chips = lax.axis_size("seq") // 2
    info = jnp.stack([seq // 2, seq % 2, bit]).astype(jnp.int32)
    teacher_heads = TEACHER_KV_HEADS // 2
    student_heads = STUDENT_KV_HEADS // 2
    per_pair = teacher_heads // student_heads
    rows = teacher_keys.shape[1]
    half_rows = rows // 2

    def columns(array, which, width):
        return lax.dynamic_slice_in_dim(array, which * width, width, 1)

    kv_width = student_heads * HEAD
    q_width = STUDENT_Q_HEADS // 2 * HEAD
    own_q = student_query_array[0]

    def pair_rows(which):
        return jnp.concatenate(
            [
                columns(student_keys[0], which, kv_width),
                columns(student_value_array[0], which, kv_width),
            ],
            1,
        )

    student_rows = jnp.concatenate([pair_rows(bit), swap(pair_rows(1 - bit), "section")], 0)
    far_q = swap(columns(own_q, 1 - bit, q_width), "section")

    def teacher_rows(pair):
        part = slice(pair * per_pair * HEAD, (pair + 1) * per_pair * HEAD)
        return jnp.concatenate([teacher_keys[0][:, part], teacher_value_array[0][:, part]], 1)

    teacher_blocks = [spread(teacher_rows(0))]
    student_blocks = spread(student_rows)
    for pair in range(1, student_heads):
        teacher_blocks.append(spread(teacher_rows(pair)))

    query_own, query_far, key_own, key_far, loss = [], [], [], [], 0.0
    for pair in range(student_heads):
        target = teacher(
            info,
            teacher_query_array[0],
            teacher_blocks[pair],
            projection[0],
            pair * per_pair,
            per_pair,
        )
        near, away, squares, kept, sent = student(
            info, own_q, far_q, target, student_blocks, pair, student_heads
        )
        query_own.append(near)
        query_far.append(swap(away, "section").astype(jnp.float32))
        loss = loss + jnp.sum(squares, axis=0)
        terms = kept + swap(sent, "seq").astype(jnp.float32)
        summed = terms[0]
        for step in range(1, chips):
            summed = summed + back(terms[step].astype(jnp.bfloat16), step).astype(jnp.float32)
        far = swap(summed[half_rows:].astype(jnp.bfloat16), "section").astype(jnp.float32)
        key_own.append(summed[:half_rows])
        key_far.append(far)

    def arrange(own, far):
        return jnp.where(
            bit == 0,
            jnp.concatenate(own + far, 1),
            jnp.concatenate(far + own, 1),
        )

    grad_q = arrange(query_own, query_far)
    grad_k = arrange([x[:, :HEAD] for x in key_own], [x[:, :HEAD] for x in key_far])
    grad_v = arrange([x[:, HEAD:] for x in key_own], [x[:, HEAD:] for x in key_far])
    halves = loss.reshape(2, half_rows)
    mine = jnp.where(bit == 0, halves[0], halves[1])
    theirs = jnp.where(bit == 0, halves[1], halves[0])
    token_loss = (mine + swap(theirs, "section")) / (STUDENT_Q_HEADS * HEAD)
    return grad_q[None], grad_k[None], grad_v[None], token_loss[None]


def solution(mesh):
    in_specs = (
        P("section", "seq", None),
        P("section", "seq", None),
        P("section", "seq", None),
        P("section", None, None, None),
        P("section", "seq", None),
        P("section", "seq", None),
        P("section", "seq", None),
    )
    out_specs = (
        P("section", "seq", None),
        P("section", "seq", None),
        P("section", "seq", None),
        P("section", "seq"),
    )
    return jax.shard_map(body, mesh=mesh, in_specs=in_specs, out_specs=out_specs, check_vma=False)
```

time: 341 us -> 219 us (0.64)
  waiting for transfers between devices: 193 us -> 99.2 us
  local copies, waits for them, and re-layouts: 64.7 us -> 3.34 us
  starting transfers between devices: 7.77 us -> 64.2 us
  Pallas kernels: 0 us -> 43.1 us
  matrix products: 26 us -> 0 us
  loops' own time: 16.6 us -> 0 us
  between operations: 14 us -> 1.3 us
  other arithmetic: 17.2 us -> 6.86 us
    reduce_scatter x1 -> x0, waiting for transfers between devices: 134 us -> none  [body(): lax.psum_scatter(terms_of_keys.astype(jnp.bfloat16), 'seq', scatter_dimen...]
    ppermute x4 -> x36, waiting for transfers between devices: 9.56 us -> 99.2 us  [the longest x6 84.9 us: back(): return lax.ppermute(value, 'seq', pairs)]
    ppermute x4 -> x36, starting transfers between devices: 7.58 us -> 64.2 us  [the longest x9 44.3 us: shift(): return lax.ppermute(value, 'seq', pairs)]
    all_gather x4 -> x0, waiting for transfers between devices: 47.6 us -> none  [the longest x1 25.9 us: body(): lax.all_gather(teacher_value_array[0], 'seq', axis=0, tiled=True)]
    pallas_call x0 -> x4, Pallas kernels: none -> 43.1 us  [the longest x2 26 us: teacher(): pl.pallas_call(functools.partial(teacher_kernel, chips, rows), out_shape=...]
    dot_general x10 -> x0, matrix products: 26 us -> none  [the longest x2 11.4 us: absorb(): jnp.einsum('gjqk,kgd->qgjd', weights.astype(jnp.bfloat16), value_block, p...]
    another operation x15 -> x0, loops' own time: 16.6 us -> none  [the longest x2 10.8 us: online_pass(): lax.scan(online_step, carried, (jnp.arange(count_of_blocks, dtype=jnp.int...]
    unnamed x18 -> x50, local copies, waits for them, and re-layouts: 15.9 us -> 1.06 us
  transfers between devices with their start and end apart: 9 -> 36, of which waited for: 7 -> 10; matrix products, arithmetic and copies ran while one was open for 23% -> 2% of each run, Pallas kernels for 0% -> 12%
where the time goes in v1:
time: 219 us; the launch traced here: 218 us
  waiting for transfers between devices  99.2 us (45%)
  starting transfers between devices  64.2 us (29%)
  Pallas kernels  43.1 us (20%)
  other arithmetic  6.86 us (3%)
  local copies, waits for them, and re-layouts  3.34 us (2%)
    ppermute x6, waiting for transfers between devices, back(): return lax.ppermute(value, 'seq', pairs)  84.9 us
    ppermute x9, starting transfers between devices, shift(): return lax.ppermute(value, 'seq', pairs)  44.3 us
    pallas_call x2, Pallas kernels, teacher(): pl.pallas_call(functools.partial(teacher_kernel, chips, rows), out_shape=...  26 us
    pallas_call x2, Pallas kernels, student(): pl.pallas_call(functools.partial(student_kernel, chips, rows), out_shape=...  17.1 us
    ppermute x21, starting transfers between devices, swap(): return lax.ppermute(value, axis, pairs)  12 us
    ppermute x21, waiting for transfers between devices, swap(): return lax.ppermute(value, axis, pairs)  9.86 us
    ppermute x6, starting transfers between devices, back(): return lax.ppermute(value, 'seq', pairs)  7.87 us
  transfers between devices with their start and end apart: 36, of which 10 were waited for; matrix products, arithmetic and copies ran while one was open for 2% of the time, Pallas kernels for 12%

profile of v1, /device:TPU:0, one launch (start us, length us, event | category | flops | bytes accessed | tf_op | source)
XLA Modules:
  0.0 218.0 jit_solution(915571937269474486)
XLA Ops:
  0.6 1.2 fusion.11
  1.9 6.0 %collective-permute-start.19 = (bf16[256,512]{1,0:T(8,128)(2,1)S(1)}, bf16[256,512]{1,0:T(8,128)(2,1)S(1)}, u32[]{:S(2)}, u32[]{:S(2)}) collective-permute-start(bf16[256,512]{1,0:T(8,128)(2,1)S(1)} %pad_maximum_fusion.2.refs_0_.refs_8_), channel_id=1, source_target_pairs={{0,4},{1,5},{2,6},{3,7},{8,12},{9,13},{10,14},{11,15},{16,20},{17,... | collective-permute-start | bytes 786440 | tf_op jit(solution)/shard_map/ppermute | solution.py:35
  7.9 3.5 %collective-permute-start.17 = (bf16[256,512]{1,0:T(8,128)(2,1)S(1)}, bf16[256,512]{1,0:T(8,128)(2,1)S(1)}, u32[]{:S(2)}, u32[]{:S(2)}) collective-permute-start(bf16[256,512]{1,0:T(8,128)(2,1)S(1)} %pad_maximum_fusion.2.refs_0_.refs_8_), channel_id=1, source_target_pairs={{0,2},{1,3},{2,4},{3,5},{4,6},{5,7},{8,10},{9,11},{10,12},{11,13},... | collective-permute-start | bytes 786440 | tf_op jit(solution)/shard_map/ppermute | solution.py:35
  11.4 1.0 dynamic-slice_bitcast_fusion.3
  12.4 1.6 collective-permute-start.8
  14.0 1.3 collective-permute-start.4
  15.3 2.1 collective-permute-done.8
  17.4 1.9 collective-permute-start.2
  19.3 0.1 collective-permute-start.1
  19.4 0.8 collective-permute-done.17.refs_2_.refs_10_
  20.2 1.4 collective-permute-start.21
  21.6 16.1 %collective-permute-start.12 = (bf16[256,512]{1,0:T(8,128)(2,1)S(1)}, bf16[256,512]{1,0:T(8,128)(2,1)S(1)}, u32[]{:S(2)}, u32[]{:S(2)}) collective-permute-start(bf16[256,512]{1,0:T(8,128)(2,1)S(1)} %pad_maximum_fusion.1.refs_0_.refs_8_), channel_id=1, source_target_pairs={{0,4},{1,5},{2,6},{3,7},{8,12},{9,13},{10,14},{11,15},{16,20},{17,... | collective-permute-start | bytes 786440 | tf_op jit(solution)/shard_map/ppermute | solution.py:35
  37.8 0.1 collective-permute-start.20
  37.9 0.5 collective-permute-start.18
  38.3 0.7 collective-permute-start.6
  39.0 0.2 collective-permute-start.22
  39.2 0.6 pad_add_fusion.info
  39.8 3.6 %collective-permute-done.12.refs_4_.refs_12_ = bf16[256,512]{1,0:T(8,128)(2,1)S(1)} collective-permute-done((bf16[256,512]{1,0:T(8,128)(2,1)S(1)}, bf16[256,512]{1,0:T(8,128)(2,1)S(1)}, u32[]{:S(2)}, u32[]{:S(2)}) %collective-permute-start.12) | collective-permute-done | bytes 262176 | tf_op jit(solution)/shard_map/ppermute | solution.py:35
  43.4 12.8 %collective-permute-start.10 = (bf16[256,512]{1,0:T(8,128)(2,1)S(1)}, bf16[256,512]{1,0:T(8,128)(2,1)S(1)}, u32[]{:S(2)}, u32[]{:S(2)}) collective-permute-start(bf16[256,512]{1,0:T(8,128)(2,1)S(1)} %pad_maximum_fusion.1.refs_0_.refs_8_), channel_id=1, source_target_pairs={{0,2},{1,3},{2,4},{3,5},{4,6},{5,7},{8,10},{9,11},{10,12},{11,13},... | collective-permute-start | bytes 786440 | tf_op jit(solution)/shard_map/ppermute | solution.py:35
  56.2 0.1 collective-permute-start.5
  56.3 0.5 collective-permute-start.3
  56.8 0.7 collective-permute-start.14
  57.5 0.2 collective-permute-start.7
  57.7 13.0 %teacher.3.target_ref = bf16[512,256]{1,0:T(8,128)(2,1)} custom-call(s32[3]{0:T(128)} %pad_add_fusion.info, bf16[256,4096]{1,0:T(8,128)(2,1)} %bitcast.78, bf16[256,512]{1,0:T(8,128)(2,1)} %copy-done.3, bf16[256,512]{1,0:T(8,128)(2,1)} %copy-done.14, bf16[256,512]{1,0:T(8,128)(2,1)} %copy-done.9, bf16[256,512]{1,0:T(8,128)(2,1)} %collective-permute-done.18.refs_3_.refs_11_, ...), custom_call_target="tpu_custom_call" | custom-call | flops 4294967296 | bytes 1048576 | tf_op jit(solution)/shard_map/teacher/pallas_call | solution.py:160
  70.8 1.6 collective-permute-start
  72.3 0.2 collective-permute-start.9
  72.5 0.4 collective-permute-start.13
  72.9 0.1 collective-permute-start.11
  73.1 0.4 collective-permute-start.15
  73.4 13.0 %teacher.2.target_ref = bf16[512,256]{1,0:T(8,128)(2,1)} custom-call(s32[3]{0:T(128)} %pad_add_fusion.info, bf16[256,4096]{1,0:T(8,128)(2,1)} %bitcast.79, bf16[256,512]{1,0:T(8,128)(2,1)} %copy-done.5, bf16[256,512]{1,0:T(8,128)(2,1)} %copy-done.13, bf16[256,512]{1,0:T(8,128)(2,1)} %copy-done.12, bf16[256,512]{1,0:T(8,128)(2,1)} %collective-permute-done.3.refs_3_.refs_11_, ...), custom_call_target="tpu_custom_call" | custom-call | flops 4294967296 | bytes 1048576 | tf_op jit(solution)/shard_map/teacher/pallas_call | solution.py:160
  86.6 0.6 copy-done.18
  87.2 0.1 copy-done.20
  87.3 0.1 copy-done.21
  87.4 0.1 copy-done.23
  87.5 8.4 %student.2 = (f32[128,512]{1,0:T(8,128)}, bf16[128,512]{1,0:T(8,128)(2,1)}, f32[8,256]{1,0:T(8,128)}, f32[4,256,256]{2,1,0:T(8,128)}, bf16[4,256,256]{2,1,0:T(8,128)(2,1)}) custom-call(s32[3]{0:T(128)} %pad_add_fusion.info, bf16[128,2048]{1,0:T(8,128)(2,1)} %bitcast.76, bf16[128,1024]{1,0:T(8,128)(2,1)} %copy-done.18, bf16[512,256]{1,0:T(8,128)(2,1)} %teacher.2.target_ref, ...), custom_call_target="tpu_custom_call" | custom-call | flops 3221225472 | bytes 2097152 | tf_op jit(solution)/shard_map/student/pallas_call | solution.py:317
  95.9 0.7 reduce_sum.18
  96.6 8.7 %student.3 = (f32[128,512]{1,0:T(8,128)}, bf16[128,512]{1,0:T(8,128)(2,1)}, f32[8,256]{1,0:T(8,128)}, f32[4,256,256]{2,1,0:T(8,128)}, bf16[4,256,256]{2,1,0:T(8,128)(2,1)}) custom-call(s32[3]{0:T(128)} %pad_add_fusion.info, bf16[128,2048]{1,0:T(8,128)(2,1)} %bitcast.77, bf16[128,1024]{1,0:T(8,128)(2,1)} %copy-done.18, bf16[512,256]{1,0:T(8,128)(2,1)} %teacher.3.target_ref, ...), custom_call_target="tpu_custom_call" | custom-call | flops 3221225472 | bytes 2097152 | tf_op jit(solution)/shard_map/student/pallas_call | solution.py:317
  105.4 0.8 reduce_sum.19
  106.2 0.6 collective-permute-start.35
  106.8 1.5 collective-permute-start.23
  108.3 0.5 collective-permute-start.24
  108.8 0.5 collective-permute-start.29
  109.3 0.5 collective-permute-done.35
  109.8 0.5 fusion.8
  110.3 2.8 %collective-permute-done.23 = bf16[128,512]{1,0:T(8,128)(2,1)S(1)} collective-permute-done((bf16[128,512]{1,0:T(8,128)(2,1)S(1)}, bf16[128,512]{1,0:T(8,128)(2,1)S(1)}, u32[]{:S(2)}, u32[]{:S(2)}) %collective-permute-start.23) | collective-permute-done | bytes 131104 | tf_op jit(solution)/shard_map/ppermute | solution.py:46
  113.2 1.7 collective-permute-done.24
  114.9 2.2 maximum_select_fusion
  117.1 0.2 fusion.9
  117.3 1.4 collective-permute-start.26
  118.7 1.3 collective-permute-start.28
  120.0 1.3 collective-permute-start.27
  121.3 0.2 fusion.10
  121.6 1.3 collective-permute-start.30
  122.9 1.3 collective-permute-start.32
  124.2 22.0 %collective-permute-done.26 = bf16[256,256]{1,0:T(8,128)(2,1)S(1)} collective-permute-done((bf16[256,256]{1,0:T(8,128)(2,1)S(1)}, bf16[256,256]{1,0:T(8,128)(2,1)S(1)}, u32[]{:S(2)}, u32[]{:S(2)}) %collective-permute-start.26) | collective-permute-done | bytes 131104 | tf_op jit(solution)/shard_map/ppermute | solution.py:41
  146.2 1.3 collective-permute-start.31
  147.5 56.5 %collective-permute-done.28 = bf16[256,256]{1,0:T(8,128)(2,1)S(1)} collective-permute-done((bf16[256,256]{1,0:T(8,128)(2,1)S(1)}, bf16[256,256]{1,0:T(8,128)(2,1)S(1)}, u32[]{:S(2)}, u32[]{:S(2)}) %collective-permute-start.28) | collective-permute-done | bytes 131104 | tf_op jit(solution)/shard_map/ppermute | solution.py:41
  203.9 0.1 fusion.5
  204.0 1.6 collective-permute-start.33
  205.6 6.5 %collective-permute-done.32 = bf16[256,256]{1,0:T(8,128)(2,1)S(1)} collective-permute-done((bf16[256,256]{1,0:T(8,128)(2,1)S(1)}, bf16[256,256]{1,0:T(8,128)(2,1)S(1)}, u32[]{:S(2)}, u32[]{:S(2)}) %collective-permute-start.32) | collective-permute-done | bytes 131104 | tf_op jit(solution)/shard_map/ppermute | solution.py:41
  212.2 1.6 collective-permute-start.34
  213.8 2.7 %collective-permute-done.34 = bf16[128,256]{1,0:T(8,128)(2,1)S(1)} collective-permute-done((bf16[128,256]{1,0:T(8,128)(2,1)S(1)}, bf16[128,256]{1,0:T(8,128)(2,1)S(1)}, u32[]{:S(2)}, u32[]{:S(2)}) %collective-permute-start.34) | collective-permute-done | bytes 65568 | tf_op jit(solution)/shard_map/ppermute | solution.py:46
  216.5 0.7 maximum_select_fusion.2
  217.3 0.7 maximum_select_fusion.1
  (94 shorter events, 0.6 us)
Async XLA Ops:
  0.6 39.2 %copy-start.6 = (bf16[1,128,2048]{2,1,0:T(8,128)(2,1)S(1)}, bf16[1,128,2048]{2,1,0:T(8,128)(2,1)}, u32[]{:S(2)}) copy-start(bf16[1,128,2048]{2,1,0:T(8,128)(2,1)} %param.11) | copy-start | bytes 1572868
  1.9 55.8 %copy-start.3 = (bf16[256,512]{1,0:T(8,128)(2,1)}, bf16[256,512]{1,0:T(8,128)(2,1)S(1)}, u32[]{:S(2)}) copy-start(bf16[256,512]{1,0:T(8,128)(2,1)S(1)} %pad_maximum_fusion.2.refs_0_.refs_8_) | copy-start | bytes 786436
  1.9 17.5 %collective-permute-start.19 = (bf16[256,512]{1,0:T(8,128)(2,1)S(1)}, bf16[256,512]{1,0:T(8,128)(2,1)S(1)}, u32[]{:S(2)}, u32[]{:S(2)}) collective-permute-start(bf16[256,512]{1,0:T(8,128)(2,1)S(1)} %pad_maximum_fusion.2.refs_0_.refs_8_), channel_id=1, source_target_pairs={{0,4},{1,5},{2,6},{3,7},{8,12},{9,13},{10,14},{11,15},{16,20},{17,... | collective-permute-start | bytes 786440 | tf_op jit(solution)/shard_map/ppermute | solution.py:35
  7.9 12.3 %collective-permute-start.17 = (bf16[256,512]{1,0:T(8,128)(2,1)S(1)}, bf16[256,512]{1,0:T(8,128)(2,1)S(1)}, u32[]{:S(2)}, u32[]{:S(2)}) collective-permute-start(bf16[256,512]{1,0:T(8,128)(2,1)S(1)} %pad_maximum_fusion.2.refs_0_.refs_8_), channel_id=1, source_target_pairs={{0,2},{1,3},{2,4},{3,5},{4,6},{5,7},{8,10},{9,11},{10,12},{11,13},... | collective-permute-start | bytes 786440 | tf_op jit(solution)/shard_map/ppermute | solution.py:35
  12.4 5.0 %collective-permute-start.8 = (bf16[128,512]{1,0:T(8,128)(2,1)S(1)}, bf16[128,512]{1,0:T(8,128)(2,1)S(1)}, u32[]{:S(2)}, u32[]{:S(2)}) collective-permute-start(bf16[128,512]{1,0:T(8,128)(2,1)S(1)} %pad_maximum_fusion.3), channel_id=1, source_target_pairs={{0,8},{8,0},{16,24},{24,16},{1,9},{9,1},{17,25},{25,17},{2,10},{10... | collective-permute-start | bytes 393224 | tf_op jit(solution)/shard_map/ppermute | solution.py:46
  13.9 7.6 %collective-permute-start.16 = (bf16[256,512]{1,0:T(8,128)(2,1)S(1)}, bf16[256,512]{1,0:T(8,128)(2,1)S(1)}, u32[]{:S(2)}, u32[]{:S(2)}) collective-permute-start(bf16[256,512]{1,0:T(8,128)(2,1)S(1)} %pad_maximum_fusion.2.refs_0_.refs_8_), channel_id=1, source_target_pairs={{0,1},{1,0},{2,3},{3,2},{4,5},{5,4},{6,7},{7,6},{8,9},{9,8},{10,11... | collective-permute-start | bytes 786440 | tf_op jit(solution)/shard_map/ppermute | solution.py:46
  14.0 56.7 %copy-start.5 = (bf16[256,512]{1,0:T(8,128)(2,1)}, bf16[256,512]{1,0:T(8,128)(2,1)S(1)}, u32[]{:S(2)}) copy-start(bf16[256,512]{1,0:T(8,128)(2,1)S(1)} %pad_maximum_fusion.refs_0_.refs_8_) | copy-start | bytes 786436
  14.0 23.8 %collective-permute-start.4 = (bf16[256,512]{1,0:T(8,128)(2,1)S(1)}, bf16[256,512]{1,0:T(8,128)(2,1)S(1)}, u32[]{:S(2)}, u32[]{:S(2)}) collective-permute-start(bf16[256,512]{1,0:T(8,128)(2,1)S(1)} %pad_maximum_fusion.refs_0_.refs_8_), channel_id=1, source_target_pairs={{0,4},{1,5},{2,6},{3,7},{8,12},{9,13},{10,14},{11,15},{16,20},{17,... | collective-permute-start | bytes 786440 | tf_op jit(solution)/shard_map/ppermute | solution.py:35
  17.4 20.4 %collective-permute-start.2 = (bf16[256,512]{1,0:T(8,128)(2,1)S(1)}, bf16[256,512]{1,0:T(8,128)(2,1)S(1)}, u32[]{:S(2)}, u32[]{:S(2)}) collective-permute-start(bf16[256,512]{1,0:T(8,128)(2,1)S(1)} %pad_maximum_fusion.refs_0_.refs_8_), channel_id=1, source_target_pairs={{0,2},{1,3},{2,4},{3,5},{4,6},{5,7},{8,10},{9,11},{10,12},{11,13},... | collective-permute-start | bytes 786440 | tf_op jit(solution)/shard_map/ppermute | solution.py:35
  19.3 38.3 %copy-start.8 = (bf16[256,512]{1,0:T(8,128)(2,1)}, bf16[256,512]{1,0:T(8,128)(2,1)S(1)}, u32[]{:S(2)}) copy-start(bf16[256,512]{1,0:T(8,128)(2,1)S(1)} %collective-permute-done.19.refs_4_.refs_12_) | copy-start | bytes 786436
  19.3 19.0 %collective-permute-start.1 = (bf16[256,512]{1,0:T(8,128)(2,1)S(1)}, bf16[256,512]{1,0:T(8,128)(2,1)S(1)}, u32[]{:S(2)}, u32[]{:S(2)}) collective-permute-start(bf16[256,512]{1,0:T(8,128)(2,1)S(1)} %pad_maximum_fusion.refs_0_.refs_8_), channel_id=1, source_target_pairs={{0,1},{1,0},{2,3},{3,2},{4,5},{5,4},{6,7},{7,6},{8,9},{9,8},{10,11... | collective-permute-start | bytes 786440 | tf_op jit(solution)/shard_map/ppermute | solution.py:46
  20.2 37.5 %copy-start.9 = (bf16[256,512]{1,0:T(8,128)(2,1)}, bf16[256,512]{1,0:T(8,128)(2,1)S(1)}, u32[]{:S(2)}) copy-start(bf16[256,512]{1,0:T(8,128)(2,1)S(1)} %collective-permute-done.17.refs_2_.refs_10_) | copy-start | bytes 786436
  20.2 18.8 %collective-permute-start.21 = (bf16[256,512]{1,0:T(8,128)(2,1)S(1)}, bf16[256,512]{1,0:T(8,128)(2,1)}, u32[]{:S(2)}, u32[]{:S(2)}) collective-permute-start(bf16[256,512]{1,0:T(8,128)(2,1)S(1)} %collective-permute-done.19.refs_4_.refs_12_), channel_id=1, source_target_pairs={{4,6},{5,7},{12,14},{13,15},{20,22},{21,23},{28,30},{29,31}} | collective-permute-start | bytes 786440 | tf_op jit(solution)/shard_map/ppermute | solution.py:35
  21.6 50.8 %copy-start.4 = (bf16[256,512]{1,0:T(8,128)(2,1)}, bf16[256,512]{1,0:T(8,128)(2,1)S(1)}, u32[]{:S(2)}) copy-start(bf16[256,512]{1,0:T(8,128)(2,1)S(1)} %pad_maximum_fusion.1.refs_0_.refs_8_) | copy-start | bytes 786436
  21.6 36.1 %copy-start.14 = (bf16[256,512]{1,0:T(8,128)(2,1)}, bf16[256,512]{1,0:T(8,128)(2,1)S(1)}, u32[]{:S(2)}) copy-start(bf16[256,512]{1,0:T(8,128)(2,1)S(1)} %collective-permute-done.16.refs_1_.refs_9_) | copy-start | bytes 786436
  21.6 21.8 %collective-permute-start.12 = (bf16[256,512]{1,0:T(8,128)(2,1)S(1)}, bf16[256,512]{1,0:T(8,128)(2,1)S(1)}, u32[]{:S(2)}, u32[]{:S(2)}) collective-permute-start(bf16[256,512]{1,0:T(8,128)(2,1)S(1)} %pad_maximum_fusion.1.refs_0_.refs_8_), channel_id=1, source_target_pairs={{0,4},{1,5},{2,6},{3,7},{8,12},{9,13},{10,14},{11,15},{16,20},{17,... | collective-permute-start | bytes 786440 | tf_op jit(solution)/shard_map/ppermute | solution.py:35
  37.8 33.0 %copy-start.11 = (bf16[256,512]{1,0:T(8,128)(2,1)}, bf16[256,512]{1,0:T(8,128)(2,1)S(1)}, u32[]{:S(2)}) copy-start(bf16[256,512]{1,0:T(8,128)(2,1)S(1)} %collective-permute-done.4.refs_4_.refs_12_) | copy-start | bytes 786436
  37.8 18.5 %collective-permute-start.20 = (bf16[256,512]{1,0:T(8,128)(2,1)S(1)}, bf16[256,512]{1,0:T(8,128)(2,1)}, u32[]{:S(2)}, u32[]{:S(2)}) collective-permute-start(bf16[256,512]{1,0:T(8,128)(2,1)S(1)} %collective-permute-done.19.refs_4_.refs_12_), channel_id=1, source_target_pairs={{0,1},{1,0},{2,3},{3,2},{4,5},{5,4},{6,7},{7,6},{8,9},{9,8},{10,11... | collective-permute-start | bytes 786440 | tf_op jit(solution)/shard_map/ppermute | solution.py:46
  37.9 32.9 %copy-start.12 = (bf16[256,512]{1,0:T(8,128)(2,1)}, bf16[256,512]{1,0:T(8,128)(2,1)S(1)}, u32[]{:S(2)}) copy-start(bf16[256,512]{1,0:T(8,128)(2,1)S(1)} %collective-permute-done.2.refs_2_.refs_10_) | copy-start | bytes 786436
  37.9 18.5 %collective-permute-start.18 = (bf16[256,512]{1,0:T(8,128)(2,1)S(1)}, bf16[256,512]{1,0:T(8,128)(2,1)}, u32[]{:S(2)}, u32[]{:S(2)}) collective-permute-start(bf16[256,512]{1,0:T(8,128)(2,1)S(1)} %collective-permute-done.17.refs_2_.refs_10_), channel_id=1, source_target_pairs={{0,1},{1,0},{2,3},{3,2},{4,5},{5,4},{6,7},{7,6},{8,9},{9,8},{10,11... | collective-permute-start | bytes 786440 | tf_op jit(solution)/shard_map/ppermute | solution.py:46
  38.3 32.4 %copy-start.13 = (bf16[256,512]{1,0:T(8,128)(2,1)}, bf16[256,512]{1,0:T(8,128)(2,1)S(1)}, u32[]{:S(2)}) copy-start(bf16[256,512]{1,0:T(8,128)(2,1)S(1)} %collective-permute-done.1.refs_1_.refs_9_) | copy-start | bytes 786436
  38.3 18.5 %collective-permute-start.6 = (bf16[256,512]{1,0:T(8,128)(2,1)S(1)}, bf16[256,512]{1,0:T(8,128)(2,1)S(1)}, u32[]{:S(2)}, u32[]{:S(2)}) collective-permute-start(bf16[256,512]{1,0:T(8,128)(2,1)S(1)} %collective-permute-done.4.refs_4_.refs_12_), channel_id=1, source_target_pairs={{4,6},{5,7},{12,14},{13,15},{20,22},{21,23},{28,30},{29,31}} | collective-permute-start | bytes 786440 | tf_op jit(solution)/shard_map/ppermute | solution.py:35
  39.0 18.5 %collective-permute-start.22 = (bf16[256,512]{1,0:T(8,128)(2,1)}, bf16[256,512]{1,0:T(8,128)(2,1)}, u32[]{:S(2)}, u32[]{:S(2)}) collective-permute-start(bf16[256,512]{1,0:T(8,128)(2,1)} %collective-permute-done.21.refs_6_.refs_14_), channel_id=1, source_target_pairs={{0,1},{1,0},{2,3},{3,2},{4,5},{5,4},{6,7},{7,6},{8,9},{9,8},{10,11... | collective-permute-start | bytes 786440 | tf_op jit(solution)/shard_map/ppermute | solution.py:46
  43.4 29.1 %copy-start.10 = (bf16[256,512]{1,0:T(8,128)(2,1)}, bf16[256,512]{1,0:T(8,128)(2,1)S(1)}, u32[]{:S(2)}) copy-start(bf16[256,512]{1,0:T(8,128)(2,1)S(1)} %collective-permute-done.12.refs_4_.refs_12_) | copy-start | bytes 786436
  43.4 27.3 %collective-permute-start.10 = (bf16[256,512]{1,0:T(8,128)(2,1)S(1)}, bf16[256,512]{1,0:T(8,128)(2,1)S(1)}, u32[]{:S(2)}, u32[]{:S(2)}) collective-permute-start(bf16[256,512]{1,0:T(8,128)(2,1)S(1)} %pad_maximum_fusion.1.refs_0_.refs_8_), channel_id=1, source_target_pairs={{0,2},{1,3},{2,4},{3,5},{4,6},{5,7},{8,10},{9,11},{10,12},{11,13},... | collective-permute-start | bytes 786440 | tf_op jit(solution)/shard_map/ppermute | solution.py:35
  56.2 16.1 %collective-permute-start.5 = (bf16[256,512]{1,0:T(8,128)(2,1)S(1)}, bf16[256,512]{1,0:T(8,128)(2,1)S(1)}, u32[]{:S(2)}, u32[]{:S(2)}) collective-permute-start(bf16[256,512]{1,0:T(8,128)(2,1)S(1)} %collective-permute-done.4.refs_4_.refs_12_), channel_id=1, source_target_pairs={{0,1},{1,0},{2,3},{3,2},{4,5},{5,4},{6,7},{7,6},{8,9},{9,8},{10,11... | collective-permute-start | bytes 786440 | tf_op jit(solution)/shard_map/ppermute | solution.py:46
  56.3 16.2 %collective-permute-start.3 = (bf16[256,512]{1,0:T(8,128)(2,1)S(1)}, bf16[256,512]{1,0:T(8,128)(2,1)}, u32[]{:S(2)}, u32[]{:S(2)}) collective-permute-start(bf16[256,512]{1,0:T(8,128)(2,1)S(1)} %collective-permute-done.2.refs_2_.refs_10_), channel_id=1, source_target_pairs={{0,1},{1,0},{2,3},{3,2},{4,5},{5,4},{6,7},{7,6},{8,9},{9,8},{10,11... | collective-permute-start | bytes 786440 | tf_op jit(solution)/shard_map/ppermute | solution.py:46
  56.8 13.9 %copy-start.15 = (bf16[256,512]{1,0:T(8,128)(2,1)}, bf16[256,512]{1,0:T(8,128)(2,1)S(1)}, u32[]{:S(2)}) copy-start(bf16[256,512]{1,0:T(8,128)(2,1)S(1)} %collective-permute-done.6.refs_6_.refs_14_) | copy-start | bytes 786436
  56.8 16.1 %collective-permute-start.14 = (bf16[256,512]{1,0:T(8,128)(2,1)S(1)}, bf16[256,512]{1,0:T(8,128)(2,1)S(1)}, u32[]{:S(2)}, u32[]{:S(2)}) collective-permute-start(bf16[256,512]{1,0:T(8,128)(2,1)S(1)} %collective-permute-done.12.refs_4_.refs_12_), channel_id=1, source_target_pairs={{4,6},{5,7},{12,14},{13,15},{20,22},{21,23},{28,30},{29,31}} | collective-permute-start | bytes 786440 | tf_op jit(solution)/shard_map/ppermute | solution.py:35
  57.5 15.6 %collective-permute-start.7 = (bf16[256,512]{1,0:T(8,128)(2,1)S(1)}, bf16[256,512]{1,0:T(8,128)(2,1)}, u32[]{:S(2)}, u32[]{:S(2)}) collective-permute-start(bf16[256,512]{1,0:T(8,128)(2,1)S(1)} %collective-permute-done.6.refs_6_.refs_14_), channel_id=1, source_target_pairs={{0,1},{1,0},{2,3},{3,2},{4,5},{5,4},{6,7},{7,6},{8,9},{9,8},{10,11... | collective-permute-start | bytes 786440 | tf_op jit(solution)/shard_map/ppermute | solution.py:46
  70.8 15.7 %copy-start.16 = (bf16[256,512]{1,0:T(8,128)(2,1)}, bf16[256,512]{1,0:T(8,128)(2,1)S(1)}, u32[]{:S(2)}) copy-start(bf16[256,512]{1,0:T(8,128)(2,1)S(1)} %collective-permute-done.10.refs_2_.refs_10_) | copy-start | bytes 786436
  70.8 15.7 %collective-permute-start = (bf16[128,1024]{1,0:T(8,128)(2,1)S(1)}, bf16[128,1024]{1,0:T(8,128)(2,1)S(1)}, u32[]{:S(2)}, u32[]{:S(2)}) collective-permute-start(bf16[128,1024]{1,0:T(8,128)(2,1)S(1)} %dynamic-slice_bitcast_fusion), channel_id=1, source_target_pairs={{0,8},{8,0},{16,24},{24,16},{1,9},{9,1},{17,25},{25,17},{2,10},{10... | collective-permute-start | bytes 786440 | tf_op jit(solution)/shard_map/ppermute | solution.py:46
  72.3 1.1 copy-start.19
  72.3 14.2 %collective-permute-start.9 = (bf16[256,512]{1,0:T(8,128)(2,1)S(1)}, bf16[256,512]{1,0:T(8,128)(2,1)S(1)}, u32[]{:S(2)}, u32[]{:S(2)}) collective-permute-start(bf16[256,512]{1,0:T(8,128)(2,1)S(1)} %pad_maximum_fusion.1.refs_0_.refs_8_), channel_id=1, source_target_pairs={{0,1},{1,0},{2,3},{3,2},{4,5},{5,4},{6,7},{7,6},{8,9},{9,8},{10,11... | collective-permute-start | bytes 786440 | tf_op jit(solution)/shard_map/ppermute | solution.py:46
  72.5 14.0 %collective-permute-start.13 = (bf16[256,512]{1,0:T(8,128)(2,1)S(1)}, bf16[256,512]{1,0:T(8,128)(2,1)S(1)}, u32[]{:S(2)}, u32[]{:S(2)}) collective-permute-start(bf16[256,512]{1,0:T(8,128)(2,1)S(1)} %collective-permute-done.12.refs_4_.refs_12_), channel_id=1, source_target_pairs={{0,1},{1,0},{2,3},{3,2},{4,5},{5,4},{6,7},{7,6},{8,9},{9,8},{10,11... | collective-permute-start | bytes 786440 | tf_op jit(solution)/shard_map/ppermute | solution.py:46
  72.9 13.5 %copy-start.17 = (bf16[256,512]{1,0:T(8,128)(2,1)}, bf16[256,512]{1,0:T(8,128)(2,1)S(1)}, u32[]{:S(2)}) copy-start(bf16[256,512]{1,0:T(8,128)(2,1)S(1)} %collective-permute-done.14.refs_6_.refs_14_) | copy-start | bytes 786436
  72.9 13.6 %collective-permute-start.11 = (bf16[256,512]{1,0:T(8,128)(2,1)S(1)}, bf16[256,512]{1,0:T(8,128)(2,1)S(1)}, u32[]{:S(2)}, u32[]{:S(2)}) collective-permute-start(bf16[256,512]{1,0:T(8,128)(2,1)S(1)} %collective-permute-done.10.refs_2_.refs_10_), channel_id=1, source_target_pairs={{0,1},{1,0},{2,3},{3,2},{4,5},{5,4},{6,7},{7,6},{8,9},{9,8},{10,11... | collective-permute-start | bytes 786440 | tf_op jit(solution)/shard_map/ppermute | solution.py:46
  73.1 13.5 %collective-permute-start.15 = (bf16[256,512]{1,0:T(8,128)(2,1)S(1)}, bf16[256,512]{1,0:T(8,128)(2,1)S(1)}, u32[]{:S(2)}, u32[]{:S(2)}) collective-permute-start(bf16[256,512]{1,0:T(8,128)(2,1)S(1)} %collective-permute-done.14.refs_6_.refs_14_), channel_id=1, source_target_pairs={{0,1},{1,0},{2,3},{3,2},{4,5},{5,4},{6,7},{7,6},{8,9},{9,8},{10,11... | collective-permute-start | bytes 786440 | tf_op jit(solution)/shard_map/ppermute | solution.py:46
  86.5 0.7 copy-start.18
  86.5 0.8 copy-start.20
  86.5 0.9 copy-start.21
  86.6 0.9 copy-start.22
  86.6 1.0 copy-start.23
  96.6 10.1 %copy-start.24 = (bf16[128,512]{1,0:T(8,128)(2,1)S(1)}, bf16[128,512]{1,0:T(8,128)(2,1)}, u32[]{:S(2)}) copy-start(bf16[128,512]{1,0:T(8,128)(2,1)} %get-tuple-element.16) | copy-start | bytes 393220
  96.6 12.2 %copy-start.7 = (bf16[4,256,256]{2,1,0:T(8,128)(2,1)S(1)}, bf16[4,256,256]{2,1,0:T(8,128)(2,1)}, u32[]{:S(2)}) copy-start(bf16[4,256,256]{2,1,0:T(8,128)(2,1)} %get-tuple-element.19) | copy-start | bytes 1572868
  96.6 18.3 %copy-start.2 = (f32[128,512]{1,0:T(8,128)S(1)}, f32[128,512]{1,0:T(8,128)}, u32[]{:S(2)}) copy-start(f32[128,512]{1,0:T(8,128)} %get-tuple-element.14) | copy-start | bytes 786436
  105.4 11.7 %copy-start.1 = (f32[4,256,256]{2,1,0:T(8,128)S(1)}, f32[4,256,256]{2,1,0:T(8,128)}, u32[]{:S(2)}) copy-start(f32[4,256,256]{2,1,0:T(8,128)} %get-tuple-element.18) | copy-start | bytes 3145732
  106.2 3.6 %collective-permute-start.35 = (f32[128]{0:T(128)S(1)}, f32[128]{0:T(128)S(1)}, u32[]{:S(2)}, u32[]{:S(2)}) collective-permute-start(f32[128]{0:T(128)S(1)} %broadcast_select_fusion), channel_id=1, source_target_pairs={{0,8},{8,0},{16,24},{24,16},{1,9},{9,1},{17,25},{25,17},{2,10},{10... | collective-permute-start | bytes 1544 | tf_op jit(solution)/shard_map/ppermute | solution.py:46
  106.8 6.4 %collective-permute-start.23 = (bf16[128,512]{1,0:T(8,128)(2,1)S(1)}, bf16[128,512]{1,0:T(8,128)(2,1)S(1)}, u32[]{:S(2)}, u32[]{:S(2)}) collective-permute-start(bf16[128,512]{1,0:T(8,128)(2,1)S(1)} %copy-done.24), channel_id=1, source_target_pairs={{0,8},{8,0},{16,24},{24,16},{1,9},{9,1},{17,25},{25,17},{2,10},{10... | collective-permute-start | bytes 393224 | tf_op jit(solution)/shard_map/ppermute | solution.py:46
  108.3 6.6 %collective-permute-start.24 = (bf16[128,512]{1,0:T(8,128)(2,1)}, bf16[128,512]{1,0:T(8,128)(2,1)S(1)}, u32[]{:S(2)}, u32[]{:S(2)}) collective-permute-start(bf16[128,512]{1,0:T(8,128)(2,1)} %get-tuple-element.17), channel_id=1, source_target_pairs={{0,8},{8,0},{16,24},{24,16},{1,9},{9,1},{17,25},{25,17},{2,10},{10... | collective-permute-start | bytes 393224 | tf_op jit(solution)/shard_map/ppermute | solution.py:46
  108.8 8.3 %collective-permute-start.25 = (bf16[4,256,256]{2,1,0:T(8,128)(2,1)S(1)}, bf16[4,256,256]{2,1,0:T(8,128)(2,1)S(1)}, u32[]{:S(2)}, u32[]{:S(2)}) collective-permute-start(bf16[4,256,256]{2,1,0:T(8,128)(2,1)S(1)} %copy-done.7), channel_id=1, source_target_pairs={{0,1},{1,0},{2,3},{3,2},{4,5},{5,4},{6,7},{7,6},{8,9},{9,8},{10,11... | collective-permute-start | bytes 1572872 | tf_op jit(solution)/shard_map/ppermute | solution.py:46
  108.8 12.5 %collective-permute-start.29 = (bf16[4,256,256]{2,1,0:T(8,128)(2,1)}, bf16[4,256,256]{2,1,0:T(8,128)(2,1)S(1)}, u32[]{:S(2)}, u32[]{:S(2)}) collective-permute-start(bf16[4,256,256]{2,1,0:T(8,128)(2,1)} %get-tuple-element.21), channel_id=1, source_target_pairs={{0,1},{1,0},{2,3},{3,2},{4,5},{5,4},{6,7},{7,6},{8,9},{9,8},{10,11... | collective-permute-start | bytes 1572872 | tf_op jit(solution)/shard_map/ppermute | solution.py:46
  117.1 4.3 %copy-start = (f32[4,256,256]{2,1,0:T(8,128)S(1)}, f32[4,256,256]{2,1,0:T(8,128)}, u32[]{:S(2)}) copy-start(f32[4,256,256]{2,1,0:T(8,128)} %get-tuple-element.20) | copy-start | bytes 3145732
  117.3 28.9 %collective-permute-start.26 = (bf16[256,256]{1,0:T(8,128)(2,1)S(1)}, bf16[256,256]{1,0:T(8,128)(2,1)S(1)}, u32[]{:S(2)}, u32[]{:S(2)}) collective-permute-start(bf16[256,256]{1,0:T(8,128)(2,1)S(1)} %get-tuple-element.28), channel_id=1, source_target_pairs={{2,0},{3,1},{4,2},{5,3},{6,4},{7,5},{10,8},{11,9},{12,10},{13,11},... | collective-permute-start | bytes 393224 | tf_op jit(solution)/shard_map/ppermute | solution.py:41
  118.7 85.2 %collective-permute-start.28 = (bf16[256,256]{1,0:T(8,128)(2,1)S(1)}, bf16[256,256]{1,0:T(8,128)(2,1)S(1)}, u32[]{:S(2)}, u32[]{:S(2)}) collective-permute-start(bf16[256,256]{1,0:T(8,128)(2,1)S(1)} %get-tuple-element.29), channel_id=1, source_target_pairs={{6,0},{7,1},{14,8},{15,9},{22,16},{23,17},{30,24},{31,25}} | collective-permute-start | bytes 393224 | tf_op jit(solution)/shard_map/ppermute | solution.py:41
  120.0 83.9 %collective-permute-start.27 = (bf16[256,256]{1,0:T(8,128)(2,1)S(1)}, bf16[256,256]{1,0:T(8,128)(2,1)S(1)}, u32[]{:S(2)}, u32[]{:S(2)}) collective-permute-start(bf16[256,256]{1,0:T(8,128)(2,1)S(1)} %get-tuple-element.30), channel_id=1, source_target_pairs={{4,0},{5,1},{6,2},{7,3},{12,8},{13,9},{14,10},{15,11},{20,16},{21,... | collective-permute-start | bytes 393224 | tf_op jit(solution)/shard_map/ppermute | solution.py:41
  121.6 84.0 %collective-permute-start.30 = (bf16[256,256]{1,0:T(8,128)(2,1)S(1)}, bf16[256,256]{1,0:T(8,128)(2,1)S(1)}, u32[]{:S(2)}, u32[]{:S(2)}) collective-permute-start(bf16[256,256]{1,0:T(8,128)(2,1)S(1)} %get-tuple-element.31), channel_id=1, source_target_pairs={{2,0},{3,1},{4,2},{5,3},{6,4},{7,5},{10,8},{11,9},{12,10},{13,11},... | collective-permute-start | bytes 393224 | tf_op jit(solution)/shard_map/ppermute | solution.py:41
  122.9 89.2 %collective-permute-start.32 = (bf16[256,256]{1,0:T(8,128)(2,1)S(1)}, bf16[256,256]{1,0:T(8,128)(2,1)S(1)}, u32[]{:S(2)}, u32[]{:S(2)}) collective-permute-start(bf16[256,256]{1,0:T(8,128)(2,1)S(1)} %get-tuple-element.32), channel_id=1, source_target_pairs={{6,0},{7,1},{14,8},{15,9},{22,16},{23,17},{30,24},{31,25}} | collective-permute-start | bytes 393224 | tf_op jit(solution)/shard_map/ppermute | solution.py:41
  146.2 65.9 %collective-permute-start.31 = (bf16[256,256]{1,0:T(8,128)(2,1)S(1)}, bf16[256,256]{1,0:T(8,128)(2,1)S(1)}, u32[]{:S(2)}, u32[]{:S(2)}) collective-permute-start(bf16[256,256]{1,0:T(8,128)(2,1)S(1)} %get-tuple-element.33), channel_id=1, source_target_pairs={{4,0},{5,1},{6,2},{7,3},{12,8},{13,9},{14,10},{15,11},{20,16},{21,... | collective-permute-start | bytes 393224 | tf_op jit(solution)/shard_map/ppermute | solution.py:41
  204.0 9.8 %collective-permute-start.33 = (bf16[128,256]{1,0:T(8,128)(2,1)S(1)}, bf16[128,256]{1,0:T(8,128)(2,1)S(1)}, u32[]{:S(2)}, u32[]{:S(2)}) collective-permute-start(bf16[128,256]{1,0:T(8,128)(2,1)S(1)} %slice.171), channel_id=1, source_target_pairs={{0,8},{8,0},{16,24},{24,16},{1,9},{9,1},{17,25},{25,17},{2,10},{10... | collective-permute-start | bytes 196616 | tf_op jit(solution)/shard_map/ppermute | solution.py:46
  212.2 4.3 %collective-permute-start.34 = (bf16[128,256]{1,0:T(8,128)(2,1)S(1)}, bf16[128,256]{1,0:T(8,128)(2,1)S(1)}, u32[]{:S(2)}, u32[]{:S(2)}) collective-permute-start(bf16[128,256]{1,0:T(8,128)(2,1)S(1)} %slice.170), channel_id=1, source_target_pairs={{0,8},{8,0},{16,24},{24,16},{1,9},{9,1},{17,25},{25,17},{2,10},{10... | collective-permute-start | bytes 196616 | tf_op jit(solution)/shard_map/ppermute | solution.py:46

commit v2 on v1

v2 whole, which is shorter than its diff:
```python
import functools
import math

import jax
import jax.numpy as jnp
from jax import lax
from jax.experimental import pallas as pl
from jax.experimental.pallas import tpu as pltpu
from jax.sharding import PartitionSpec as P


HEAD = 128
TEACHER_Q_HEADS = 64
TEACHER_KV_HEADS = 8
STUDENT_Q_HEADS = 16
STUDENT_KV_HEADS = 4
GROUP_T = TEACHER_Q_HEADS // TEACHER_KV_HEADS
GROUP_S = STUDENT_Q_HEADS // STUDENT_KV_HEADS
PER_TARGET = TEACHER_Q_HEADS // STUDENT_Q_HEADS

floor_score = -1e30
inverse_root = 1.0 / math.sqrt(HEAD)
exp2_scale = inverse_root * math.log2(math.e)
vmem_limit = 60 * 1024 * 1024
chunk = 64
pace = 10000
piece = 512


def dot(left, right):
    return lax.dot_general(
        left, right, (((1,), (0,)), ((), ())), preferred_element_type=jnp.float32
    )


def shift(value, chips, least=0):
    size = lax.axis_size("seq")
    pairs = [(i, i + 2 * chips) for i in range(2 * least, size - 2 * chips)]
    return lax.ppermute(value, "seq", pairs)


def back(value, chips):
    size = lax.axis_size("seq")
    pairs = [(i, i - 2 * chips) for i in range(2 * chips, size)]
    return lax.ppermute(value, "seq", pairs)


def swap(value, axis):
    pairs = [(i, i ^ 1) for i in range(lax.axis_size(axis))]
    return lax.ppermute(value, axis, pairs)


def spread(own, relay):
    chips = lax.axis_size("seq") // 2
    mine = [own]
    for step in range(1, chips):
        if step <= 2 or not relay:
            mine.append(shift(own, step))
        else:
            mine.append(shift(mine[-1], 1, step - 1))
    return mine


def both_cores(mine):
    blocks = []
    for block in mine:
        blocks.append((block, swap(block, "seq")))
    return blocks


def variants(chips):
    return [*range(2, chips, 2), chips]


def fold_max(tile):
    return jnp.max(tile.reshape(-1, 8, tile.shape[1]), axis=0)


def fold_sum(tile):
    return jnp.sum(tile.reshape(-1, 8, tile.shape[1]), axis=0)


def paced(history, bound):
    if len(history) <= pace:
        return bound
    return jnp.maximum(bound, floor_score - history[-pace])


def weigh(scores, weights, start, size, peak, history, keep):
    row_sum = history[-1]
    for u in range(start, start + size, chunk):
        part = pl.ds(u, chunk)
        gap = scores[part, :].reshape(-1, 8, peak.shape[1]) - paced(history, peak)
        weight = jnp.exp2(gap * exp2_scale).reshape(chunk, peak.shape[1])
        if keep:
            scores[part, :] = weight
        weights[part, :] = weight.astype(jnp.bfloat16)
        row_sum = row_sum + fold_sum(weight)
        history.append(row_sum)


def spread_max(peak):
    return jnp.broadcast_to(jnp.max(peak, axis=0, keepdims=True), peak.shape)


def teacher_kernel(chips, rows, heads, info, q_ref, *refs):
    key_refs = refs[: 2 * chips]
    value_refs = refs[2 * chips : 4 * chips]
    proj_ref, out_ref, keys, values_t, query_t, *refs = refs[4 * chips :]
    scores, weights, (peaks, context) = refs[:2], refs[2:4], refs[4:]
    chip, core = info[0], info[1]
    wide = 2 * rows
    pairs = GROUP_T // 2
    for b in range(2 * chips):
        part = pl.ds(b * rows, rows)

        @pl.when(b < 2 * (chip + 2))
        def _():
            for g in range(heads):
                columns = slice(g * HEAD, (g + 1) * HEAD)
                keys[g, part, :] = key_refs[b][:, columns]
                values_t[g, :, part] = value_refs[b][:, columns].T

    for h in range(heads * GROUP_T):
        half = pl.ds(h % 2 * rows, rows)
        query_t[h // 2, :, half] = q_ref[:, h * HEAD : (h + 1) * HEAD].T

    key_id = lax.broadcasted_iota(jnp.int32, (wide, wide), 0)
    row_id = lax.broadcasted_iota(jnp.int32, (wide, wide), 1)
    row_id = jnp.where(row_id < rows, row_id, row_id - rows)
    ahead = jnp.where(key_id < rows, key_id, key_id + (1 - 2 * core) * rows - rows)
    allowed = ahead <= row_id

    def score(b, pair, slot, peak):
        part = pl.ds(b * wide, wide)
        tile = dot(keys[pair // pairs, part, :], query_t[pair])
        if b == 0:
            tile = jnp.where(allowed, tile, floor_score)
        scores[slot][part, :] = tile
        return jnp.maximum(peak, held(b, fold_max(tile), floor_score))

    def held(b, value, otherwise):
        return value if b == 0 else jnp.where(b <= chip, value, otherwise)

    low = jnp.full((8, wide), floor_score, jnp.float32)

    for least, count in zip([0, *variants(chips)], variants(chips)):

        @pl.when(jnp.logical_and(chip >= least, chip < count))
        def _():
            peak = low
            for b in range(count):
                peak = score(b, 0, 0, peak)
            peaks[...] = peak

            def step(pair, slot):
                later = jnp.minimum(pair + 1, heads * pairs - 1)
                top = spread_max(peaks[...])
                history = [jnp.zeros((8, wide), jnp.float32)]
                peak = low
                for b in range(count):
                    bound = held(b, top, -floor_score)
                    weigh(scores[slot], weights[slot], b * wide, wide, bound, history, False)
                    peak = score(b, later, 1 - slot, peak)
                end = count * wide
                mixed = dot(values_t[pair // pairs, :, :end], weights[slot][:end, :])
                mixed = mixed / jnp.sum(history[-1], axis=0, keepdims=True)
                for half in range(2):
                    start = pl.multiple_of((2 * pair + half) * HEAD, HEAD)
                    made = mixed[:, half * rows : (half + 1) * rows]
                    context[pl.ds(start, HEAD), :] = made.astype(jnp.bfloat16)
                peaks[...] = peak

            def two(i, carried):
                step(2 * i, 0)
                step(2 * i + 1, 1)
                return carried

            lax.fori_loop(0, heads * pairs // 2, two, 0)

    deep = PER_TARGET * HEAD
    for t in range(heads * GROUP_T // PER_TARGET):
        made = dot(proj_ref[t].T, context[t * deep : (t + 1) * deep, :])
        out_ref[t * HEAD : (t + 1) * HEAD, :] = made.astype(jnp.bfloat16)


def teacher(info, queries, blocks, projection, first_head, heads):
    chips = len(blocks)
    rows = queries.shape[0]
    flat = [part for pair in blocks for part in pair]
    targets = heads * GROUP_T // PER_TARGET
    turn = first_head // heads
    in_specs = [pl.BlockSpec((rows, heads * GROUP_T * HEAD), lambda i, info: (0, turn))]
    in_specs += [pl.BlockSpec((rows, heads * HEAD), lambda i, info: (0, 0))] * len(flat)
    in_specs += [pl.BlockSpec((rows, heads * HEAD), lambda i, info: (0, 1))] * len(flat)
    in_specs += [
        pl.BlockSpec((targets, PER_TARGET * HEAD, HEAD), lambda i, info: (turn, 0, 0))
    ]
    wide = 2 * rows
    work = heads * GROUP_T * rows * chips * wide
    return pl.pallas_call(
        functools.partial(teacher_kernel, chips, rows, heads),
        out_shape=jax.ShapeDtypeStruct((targets * HEAD, rows), jnp.bfloat16),
        grid_spec=pltpu.PrefetchScalarGridSpec(
            num_scalar_prefetch=1,
            grid=(1,),
            in_specs=in_specs,
            out_specs=pl.BlockSpec((targets * HEAD, rows), lambda i, info: (0, 0)),
            scratch_shapes=[
                pltpu.VMEM((heads, chips * wide, HEAD), jnp.bfloat16),
                pltpu.VMEM((heads, HEAD, chips * wide), jnp.bfloat16),
                pltpu.VMEM((heads * GROUP_T // 2, HEAD, wide), jnp.bfloat16),
                *[pltpu.VMEM((chips * wide, wide), jnp.float32)] * 2,
                *[pltpu.VMEM((chips * wide, wide), jnp.bfloat16)] * 2,
                pltpu.VMEM((8, wide), jnp.float32),
                pltpu.VMEM((heads * GROUP_T * HEAD, rows), jnp.bfloat16),
            ],
        ),
        compiler_params=pltpu.CompilerParams(
            dimension_semantics=("arbitrary",), vmem_limit_bytes=vmem_limit
        ),
        cost_estimate=pl.CostEstimate(
            flops=4 * HEAD * work, bytes_accessed=4 * wide * HEAD * chips, transcendentals=work
        ),
        name="teacher",
    )(info, queries, *flat, *flat, projection)


def student_kernel(chips, rows, info, own_q_ref, far_q_ref, target_ref, *refs):
    key_refs = refs[: 2 * chips]
    value_refs = refs[2 * chips : 4 * chips]
    near_ref, away_ref, loss_ref, kept_ref, sent_ref = refs[4 * chips : 4 * chips + 5]
    keys, keys_t, values, values_t, query, query_t, scores, weights = refs[
        4 * chips + 5 : 4 * chips + 13
    ]
    grad_scores, key_sum, value_sum, query_sum, loss_sum = refs[4 * chips + 13 :]
    chip, core, bit = info[0], info[1], info[2]
    wide = 2 * rows
    half_rows = rows // 2
    for b in range(2 * chips):
        part = pl.ds(b * rows, rows)

        @pl.when(b < 2 * (chip + 2))
        def _():
            key_block = key_refs[b][...]
            value_block = value_refs[b][...]
            keys[part, :] = key_block
            keys_t[:, part] = key_block.T
            values[part, :] = value_block
            values_t[:, part] = value_block.T
            key_sum[part, :] = jnp.zeros((rows, HEAD), jnp.float32)
            value_sum[part, :] = jnp.zeros((rows, HEAD), jnp.float32)

    mine = pl.multiple_of(bit * half_rows, half_rows)
    other = pl.multiple_of((1 - bit) * half_rows, half_rows)
    for h in range(GROUP_S):
        columns = slice(h * HEAD, (h + 1) * HEAD)
        base = h % 2 * rows
        query[h // 2, pl.ds(base + mine, half_rows), :] = own_q_ref[:, columns]
        query[h // 2, pl.ds(base + other, half_rows), :] = far_q_ref[:, columns]
    for p in range(GROUP_S // 2):
        query_t[p] = query[p].T

    key_id = lax.broadcasted_iota(jnp.int32, (wide, wide), 0)
    row_id = lax.broadcasted_iota(jnp.int32, (wide, wide), 1)
    row_id = jnp.where(row_id < rows, row_id, row_id - rows)
    within = jnp.where(key_id < rows, key_id, key_id - rows)
    place = jnp.where(within < half_rows, within + bit * half_rows, within - bit * half_rows)
    ahead = jnp.where(key_id < rows, place, place + (1 - 2 * core) * rows)
    allowed = ahead <= row_id
    loss_sum[...] = jnp.zeros_like(loss_sum)

    def held(b, value, otherwise):
        return value if b == 0 else jnp.where(b <= chip, value, otherwise)

    for least, count in zip([0, *variants(chips)], variants(chips)):

        @pl.when(jnp.logical_and(chip >= least, chip < count))
        def _():
            def step(pair, carried):
                end = count * wide
                peak = jnp.full((8, wide), floor_score, jnp.float32)
                for b in range(count):
                    part = pl.ds(b * wide, wide)
                    tile = dot(keys[part, :], query_t[pair])
                    if b == 0:
                        tile = jnp.where(allowed, tile, floor_score)
                    scores[part, :] = tile
                    peak = jnp.maximum(peak, held(b, fold_max(tile), floor_score))
                history = [jnp.zeros((8, wide), jnp.float32)]
                top = spread_max(peak)
                for b in range(count):
                    bound = held(b, top, -floor_score)
                    weigh(scores, weights, b * wide, wide, bound, history, True)
                inverse = 1.0 / jnp.sum(history[-1], axis=0, keepdims=True)
                made = dot(values_t[:, :end], weights[:end, :]) * inverse
                start = pl.multiple_of(pair * 2 * HEAD, 2 * HEAD)
                target = target_ref[pl.ds(start, 2 * HEAD), :].astype(jnp.float32)
                mismatch = made - jnp.concatenate([target[:HEAD], target[HEAD:]], 1)
                squares = fold_sum(jnp.square(mismatch))
                loss_sum[...] += squares[:, :rows] + squares[:, rows:]
                delta = jnp.sum(mismatch * made, axis=0, keepdims=True)
                grad_t = mismatch.astype(jnp.bfloat16)
                grad = mismatch.T.astype(jnp.bfloat16)
                for u in range(0, end, piece):
                    part = pl.ds(u, piece)
                    prob = scores[part, :] * inverse
                    grad_prob = dot(values[part, :], grad_t)
                    grad_score = (prob * (grad_prob - delta)).astype(jnp.bfloat16)
                    grad_scores[part, :] = grad_score
                    key_sum[part, :] += dot(grad_score, query[pair])
                    value_sum[part, :] += dot(prob.astype(jnp.bfloat16), grad)
                summed = dot(keys_t[:, :end], grad_scores[:end, :]) * inverse_root
                query_sum[2 * pair] = summed[:, :rows].T
                query_sum[2 * pair + 1] = summed[:, rows:].T
                return carried

            lax.fori_loop(0, GROUP_S // 2, step, 0)

    for h in range(GROUP_S):
        near_ref[:, h * HEAD : (h + 1) * HEAD] = query_sum[h, pl.ds(mine, half_rows), :]
        away_ref[:, h * HEAD : (h + 1) * HEAD] = query_sum[h, pl.ds(other, half_rows), :].astype(
            jnp.bfloat16
        )
    loss_ref[...] = jnp.sum(loss_sum[...], axis=0, keepdims=True)
    for b in range(chips):

        @pl.when(b <= chip)
        def _():
            own = pl.ds(b * wide, rows)
            far = pl.ds(b * wide + rows, rows)
            kept_ref[b, :, :HEAD] = key_sum[own, :] * inverse_root
            kept_ref[b, :, HEAD:] = value_sum[own, :]
            sent_ref[b, :, :HEAD] = (key_sum[far, :] * inverse_root).astype(jnp.bfloat16)
            sent_ref[b, :, HEAD:] = value_sum[far, :].astype(jnp.bfloat16)


def student(info, own_queries, far_queries, target, blocks, pair, heads):
    chips = len(blocks)
    rows = blocks[0][0].shape[0]
    half_rows = rows // 2
    wide = 2 * rows
    flat = [part for both in blocks for part in both]
    width = GROUP_S * HEAD
    full = lambda i, info: (0, 0)
    in_specs = [
        pl.BlockSpec((half_rows, width), lambda i, info: (0, info[2] * heads + pair)),
        pl.BlockSpec((half_rows, width), lambda i, info: (0, pair)),
        pl.BlockSpec((width, rows), full),
    ]
    in_specs += [pl.BlockSpec((rows, HEAD), lambda i, info: (0, 0))] * len(flat)
    in_specs += [pl.BlockSpec((rows, HEAD), lambda i, info: (0, 1))] * len(flat)
    work = GROUP_S * rows * chips * wide
    return pl.pallas_call(
        functools.partial(student_kernel, chips, rows),
        out_shape=(
            jax.ShapeDtypeStruct((half_rows, width), jnp.float32),
            jax.ShapeDtypeStruct((half_rows, width), jnp.bfloat16),
            jax.ShapeDtypeStruct((1, rows), jnp.float32),
            jax.ShapeDtypeStruct((chips, rows, 2 * HEAD), jnp.float32),
            jax.ShapeDtypeStruct((chips, rows, 2 * HEAD), jnp.bfloat16),
        ),
        grid_spec=pltpu.PrefetchScalarGridSpec(
            num_scalar_prefetch=1,
            grid=(1,),
            in_specs=in_specs,
            out_specs=(
                pl.BlockSpec((half_rows, width), full),
                pl.BlockSpec((half_rows, width), full),
                pl.BlockSpec((1, rows), full),
                pl.BlockSpec((chips, rows, 2 * HEAD), lambda i, info: (0, 0, 0)),
                pl.BlockSpec((chips, rows, 2 * HEAD), lambda i, info: (0, 0, 0)),
            ),
            scratch_shapes=[
                pltpu.VMEM((chips * wide, HEAD), jnp.bfloat16),
                pltpu.VMEM((HEAD, chips * wide), jnp.bfloat16),
                pltpu.VMEM((chips * wide, HEAD), jnp.bfloat16),
                pltpu.VMEM((HEAD, chips * wide), jnp.bfloat16),
                pltpu.VMEM((GROUP_S // 2, wide, HEAD), jnp.bfloat16),
                pltpu.VMEM((GROUP_S // 2, HEAD, wide), jnp.bfloat16),
                pltpu.VMEM((chips * wide, wide), jnp.float32),
                *[pltpu.VMEM((chips * wide, wide), jnp.bfloat16)] * 2,
                *[pltpu.VMEM((chips * wide, HEAD), jnp.float32)] * 2,
                pltpu.VMEM((GROUP_S, rows, HEAD), jnp.float32),
                pltpu.VMEM((8, rows), jnp.float32),
            ],
        ),
        compiler_params=pltpu.CompilerParams(
            dimension_semantics=("arbitrary",), vmem_limit_bytes=vmem_limit
        ),
        cost_estimate=pl.CostEstimate(
            flops=12 * HEAD * work, bytes_accessed=8 * wide * HEAD * chips, transcendentals=work
        ),
        name="student",
    )(info, own_queries, far_queries, target, *flat, *flat)


def program(
    teacher_query_array,
    teacher_keys,
    teacher_value_array,
    projection,
    student_query_array,
    student_keys,
    student_value_array,
):
    bit = lax.axis_index("section") % 2
    seq = lax.axis_index("seq")
    chips = lax.axis_size("seq") // 2
    info = jnp.stack([seq // 2, seq % 2, bit]).astype(jnp.int32)
    teacher_heads = TEACHER_KV_HEADS // 2
    student_heads = STUDENT_KV_HEADS // 2
    per_pair = teacher_heads // student_heads
    rows = teacher_keys.shape[1]
    half_rows = rows // 2

    def columns(array, which, width):
        return lax.dynamic_slice_in_dim(array, which * width, width, 1)

    kv_width = student_heads * HEAD
    q_width = STUDENT_Q_HEADS // 2 * HEAD
    own_q = student_query_array[0]

    def teacher_rows(pair):
        part = slice(pair * per_pair * HEAD, (pair + 1) * per_pair * HEAD)
        return jnp.concatenate([teacher_keys[0][:, part], teacher_value_array[0][:, part]], 1)

    def pair_rows(which):
        return jnp.concatenate(
            [
                columns(student_keys[0], which, kv_width),
                columns(student_value_array[0], which, kv_width),
            ],
            1,
        )

    teacher_mine = [spread(teacher_rows(0), False)]
    far_rows = swap(pair_rows(1 - bit), "section")
    student_rows = jnp.concatenate([pair_rows(bit), far_rows], 0)
    student_mine = []
    for pair in range(student_heads):
        if pair:
            teacher_mine.append(spread(teacher_rows(pair), False))
        key_part = student_rows[:, pair * HEAD : (pair + 1) * HEAD]
        value_part = student_rows[:, kv_width + pair * HEAD : kv_width + (pair + 1) * HEAD]
        student_mine.append(spread(jnp.concatenate([key_part, value_part], 1), False))
    far_q = swap(columns(own_q, 1 - bit, q_width), "section")

    query_own, query_far, key_own, key_far, loss = [], [], [], [], 0.0
    for pair in range(student_heads):
        blocks = both_cores(teacher_mine[pair])
        target = teacher(
            info, teacher_query_array[0], blocks, projection[0], pair * per_pair, per_pair
        )
        blocks = both_cores(student_mine[pair])
        near, away, squares, kept, sent = student(
            info, own_q, far_q, target, blocks, pair, student_heads
        )
        query_own.append(near)
        query_far.append(swap(away, "section"))
        loss = loss + squares[0]
        terms = kept + swap(sent, "seq").astype(jnp.float32)
        summed = terms[0]
        for step in range(1, chips):
            got = back(terms[step].astype(jnp.bfloat16), step)
            summed = summed + got.astype(jnp.float32)
        far = swap(summed[half_rows:].astype(jnp.bfloat16), "section")
        key_own.append(summed[:half_rows])
        key_far.append(far.astype(jnp.float32))
    query_far = [part.astype(jnp.float32) for part in query_far]

    def arrange(own, far):
        return jnp.where(
            bit == 0,
            jnp.concatenate(own + far, 1),
            jnp.concatenate(far + own, 1),
        )

    grad_q = arrange(query_own, query_far)
    grad_k = arrange([x[:, :HEAD] for x in key_own], [x[:, :HEAD] for x in key_far])
    grad_v = arrange([x[:, HEAD:] for x in key_own], [x[:, HEAD:] for x in key_far])
    halves = loss.reshape(2, half_rows)
    mine = jnp.where(bit == 0, halves[0], halves[1])
    theirs = jnp.where(bit == 0, halves[1], halves[0])
    got = swap(theirs, "section")
    token_loss = (mine + got) / (STUDENT_Q_HEADS * HEAD)
    return grad_q[None], grad_k[None], grad_v[None], token_loss[None]


def solution(mesh):
    in_specs = (
        P("section", "seq", None),
        P("section", "seq", None),
        P("section", "seq", None),
        P("section", None, None, None),
        P("section", "seq", None),
        P("section", "seq", None),
        P("section", "seq", None),
    )
    out_specs = (
        P("section", "seq", None),
        P("section", "seq", None),
        P("section", "seq", None),
        P("section", "seq"),
    )
    return jax.shard_map(
        program, mesh=mesh, in_specs=in_specs, out_specs=out_specs, check_vma=False
    )
```

time: 219 us -> 184 us (0.84)
  waiting for transfers between devices: 99.2 us -> 43.7 us
  starting transfers between devices: 64.2 us -> 87 us
  Pallas kernels: 43.1 us -> 40.3 us
    ppermute x6, waiting for transfers between devices: 84.9 us -> 27.5 us  [back(): return lax.ppermute(value, 'seq', pairs)]
    ppermute x9 -> x12, starting transfers between devices: 44.3 us -> 65.5 us  [shift(): return lax.ppermute(value, 'seq', pairs)]
    pallas_call x2, Pallas kernels: 26 us -> 21.8 us  [teacher(): pl.pallas_call(functools.partial(teacher_kernel, chips, rows, heads), out...]
    ppermute x9 -> x12, waiting for transfers between devices: 4.35 us -> 7.58 us  [shift(): return lax.ppermute(value, 'seq', pairs)]
    ppermute x21 -> x25, starting transfers between devices: 12 us -> 13.6 us  [swap(): return lax.ppermute(value, axis, pairs)]
    ppermute x21 -> x25, waiting for transfers between devices: 9.86 us -> 8.57 us  [swap(): return lax.ppermute(value, axis, pairs)]
  transfers between devices with their start and end apart: 36 -> 43, of which waited for: 10 -> 10; matrix products, arithmetic and copies ran while one was open for 2% -> 3% of each run, Pallas kernels for 12% -> 17%
where the time goes in v2:
time: 184 us; the launch traced here: 183 us
  starting transfers between devices  87 us (47%)
  waiting for transfers between devices  43.7 us (24%)
  Pallas kernels  40.3 us (22%)
  other arithmetic  6.15 us (3%)
  local copies, waits for them, and re-layouts  4.7 us (3%)
    ppermute x12, starting transfers between devices, shift(): return lax.ppermute(value, 'seq', pairs)  65.5 us
    ppermute x6, waiting for transfers between devices, back(): return lax.ppermute(value, 'seq', pairs)  27.5 us
    pallas_call x2, Pallas kernels, teacher(): pl.pallas_call(functools.partial(teacher_kernel, chips, rows, heads), out...  21.8 us
    pallas_call x2, Pallas kernels, student(): pl.pallas_call(functools.partial(student_kernel, chips, rows), out_shape=...  18.5 us
    ppermute x25, starting transfers between devices, swap(): return lax.ppermute(value, axis, pairs)  13.6 us
    ppermute x25, waiting for transfers between devices, swap(): return lax.ppermute(value, axis, pairs)  8.57 us
    ppermute x6, starting transfers between devices, back(): return lax.ppermute(value, 'seq', pairs)  7.87 us
    ppermute x12, waiting for transfers between devices, shift(): return lax.ppermute(value, 'seq', pairs)  7.58 us
  transfers between devices with their start and end apart: 43, of which 10 were waited for; matrix products, arithmetic and copies ran while one was open for 3% of the time, Pallas kernels for 17%

profile of v2, /device:TPU:0, one launch (start us, length us, event | category | flops | bytes accessed | tf_op | source)
XLA Modules:
  0.0 183.3 jit_solution(3449031249874773592)
XLA Ops:
  0.7 1.0 dynamic-slice_bitcast_fusion.3
  1.7 3.0 %collective-permute-start.8 = (bf16[128,512]{1,0:T(8,128)(2,1)S(1)}, bf16[128,512]{1,0:T(8,128)(2,1)S(1)}, u32[]{:S(2)}, u32[]{:S(2)}) collective-permute-start(bf16[128,512]{1,0:T(8,128)(2,1)S(1)} %pad_maximum_fusion.3), channel_id=1, source_target_pairs={{0,8},{8,0},{16,24},{24,16},{1,9},{9,1},{17,25},{25,17},{2,10},{10... | collective-permute-start | bytes 393224 | tf_op jit(solution)/shard_map/ppermute | solution.py:50
  4.7 1.1 fusion.14
  5.9 3.5 %collective-permute-start.2 = (bf16[256,512]{1,0:T(8,128)(2,1)S(1)}, bf16[256,512]{1,0:T(8,128)(2,1)S(1)}, u32[]{:S(2)}, u32[]{:S(2)}) collective-permute-start(bf16[256,512]{1,0:T(8,128)(2,1)S(1)} %pad_maximum_fusion.refs_0_.refs_8_), channel_id=1, source_target_pairs={{0,2},{1,3},{2,4},{3,5},{4,6},{5,7},{8,10},{9,11},{10,12},{11,13},... | collective-permute-start | bytes 786440 | tf_op jit(solution)/shard_map/ppermute | solution.py:39
  9.4 4.5 %collective-permute-start.4 = (bf16[256,512]{1,0:T(8,128)(2,1)S(1)}, bf16[256,512]{1,0:T(8,128)(2,1)S(1)}, u32[]{:S(2)}, u32[]{:S(2)}) collective-permute-start(bf16[256,512]{1,0:T(8,128)(2,1)S(1)} %pad_maximum_fusion.refs_0_.refs_8_), channel_id=1, source_target_pairs={{0,4},{1,5},{2,6},{3,7},{8,12},{9,13},{10,14},{11,15},{16,20},{17,... | collective-permute-start | bytes 786440 | tf_op jit(solution)/shard_map/ppermute | solution.py:39
  13.9 1.3 collective-permute-start.6
  15.5 1.3 collective-permute-start.10
  16.8 0.6 collective-permute-start
  17.4 4.3 %collective-permute-done.4.refs_4_.refs_12_ = bf16[256,512]{1,0:T(8,128)(2,1)S(1)} collective-permute-done((bf16[256,512]{1,0:T(8,128)(2,1)S(1)}, bf16[256,512]{1,0:T(8,128)(2,1)S(1)}, u32[]{:S(2)}, u32[]{:S(2)}) %collective-permute-start.4) | collective-permute-done | bytes 262176 | tf_op jit(solution)/shard_map/ppermute | solution.py:39
  21.7 14.7 %collective-permute-start.17 = (bf16[256,512]{1,0:T(8,128)(2,1)S(1)}, bf16[256,512]{1,0:T(8,128)(2,1)S(1)}, u32[]{:S(2)}, u32[]{:S(2)}) collective-permute-start(bf16[256,512]{1,0:T(8,128)(2,1)S(1)} %pad_maximum_fusion.2.refs_0_.refs_8_), channel_id=1, source_target_pairs={{0,2},{1,3},{2,4},{3,5},{4,6},{5,7},{8,10},{9,11},{10,12},{11,13},... | collective-permute-start | bytes 786440 | tf_op jit(solution)/shard_map/ppermute | solution.py:39
  36.4 5.3 %collective-permute-start.12 = (bf16[256,256]{1,0:T(8,128)(2,1)S(1)}, bf16[256,256]{1,0:T(8,128)(2,1)S(1)}, u32[]{:S(2)}, u32[]{:S(2)}) collective-permute-start(bf16[256,256]{1,0:T(8,128)(2,1)S(1)} %pad_maximum_fusion.4.refs_0_.refs_8_), channel_id=1, source_target_pairs={{0,4},{1,5},{2,6},{3,7},{8,12},{9,13},{10,14},{11,15},{16,20},{17,... | collective-permute-start | bytes 393224 | tf_op jit(solution)/shard_map/ppermute | solution.py:39
  41.7 1.3 collective-permute-start.14
  43.1 1.4 collective-permute-done.12.refs_4_.refs_12_
  44.5 5.3 %collective-permute-start.19 = (bf16[256,512]{1,0:T(8,128)(2,1)S(1)}, bf16[256,512]{1,0:T(8,128)(2,1)S(1)}, u32[]{:S(2)}, u32[]{:S(2)}) collective-permute-start(bf16[256,512]{1,0:T(8,128)(2,1)S(1)} %pad_maximum_fusion.2.refs_0_.refs_8_), channel_id=1, source_target_pairs={{0,4},{1,5},{2,6},{3,7},{8,12},{9,13},{10,14},{11,15},{16,20},{17,... | collective-permute-start | bytes 786440 | tf_op jit(solution)/shard_map/ppermute | solution.py:39
  49.9 12.0 %collective-permute-start.21 = (bf16[256,512]{1,0:T(8,128)(2,1)S(1)}, bf16[256,512]{1,0:T(8,128)(2,1)S(1)}, u32[]{:S(2)}, u32[]{:S(2)}) collective-permute-start(bf16[256,512]{1,0:T(8,128)(2,1)S(1)} %pad_maximum_fusion.2.refs_0_.refs_8_), channel_id=1, source_target_pairs={{0,6},{1,7},{8,14},{9,15},{16,22},{17,23},{24,30},{25,31}} | collective-permute-start | bytes 786440 | tf_op jit(solution)/shard_map/ppermute | solution.py:39
  62.0 0.5 collective-permute-start.5
  62.5 0.1 collective-permute-start.7
  62.7 0.7 pad_add_fusion.info
  63.4 0.5 collective-permute-start.16
  63.9 1.9 %collective-permute-done.21.refs_6_.refs_14_ = bf16[256,512]{1,0:T(8,128)(2,1)S(1)} collective-permute-done((bf16[256,512]{1,0:T(8,128)(2,1)S(1)}, bf16[256,512]{1,0:T(8,128)(2,1)S(1)}, u32[]{:S(2)}, u32[]{:S(2)}) %collective-permute-start.21) | collective-permute-done | bytes 262176 | tf_op jit(solution)/shard_map/ppermute | solution.py:39
  65.8 4.6 %collective-permute-start.24 = (bf16[256,256]{1,0:T(8,128)(2,1)S(1)}, bf16[256,256]{1,0:T(8,128)(2,1)}, u32[]{:S(2)}, u32[]{:S(2)}) collective-permute-start(bf16[256,256]{1,0:T(8,128)(2,1)S(1)} %pad_maximum_fusion.5.refs_0_.refs_8_), channel_id=1, source_target_pairs={{0,2},{1,3},{2,4},{3,5},{4,6},{5,7},{8,10},{9,11},{10,12},{11,13},... | collective-permute-start | bytes 393224 | tf_op jit(solution)/shard_map/ppermute | solution.py:39
  70.4 0.2 collective-permute-start.18
  70.6 0.3 collective-permute-start.20
  70.9 0.2 collective-permute-start.22
  71.2 0.2 copy-done.19
  71.3 10.9 %teacher.2.target_ref = bf16[512,256]{1,0:T(8,128)(2,1)} custom-call(s32[3]{0:T(128)} %pad_add_fusion.info, bf16[256,4096]{1,0:T(8,128)(2,1)} %bitcast.88, bf16[256,512]{1,0:T(8,128)(2,1)} %copy-done.3, bf16[256,512]{1,0:T(8,128)(2,1)} %copy-done.14, bf16[256,512]{1,0:T(8,128)(2,1)} %copy-done.11, bf16[256,512]{1,0:T(8,128)(2,1)} %copy-done.18, ...), custom_call_target="tpu_custom_call" | custom-call | flops 4294967296 | bytes 1048576 | tf_op jit(solution)/shard_map/teacher/pallas_call | solution.py:201
  82.3 10.5 %collective-permute-start.26 = (bf16[256,256]{1,0:T(8,128)(2,1)S(1)}, bf16[256,256]{1,0:T(8,128)(2,1)S(1)}, u32[]{:S(2)}, u32[]{:S(2)}) collective-permute-start(bf16[256,256]{1,0:T(8,128)(2,1)S(1)} %pad_maximum_fusion.5.refs_0_.refs_8_), channel_id=1, source_target_pairs={{0,4},{1,5},{2,6},{3,7},{8,12},{9,13},{10,14},{11,15},{16,20},{17,... | collective-permute-start | bytes 393224 | tf_op jit(solution)/shard_map/ppermute | solution.py:39
  92.8 1.3 collective-permute-start.28
  94.2 0.5 collective-permute-start.13
  94.8 10.9 %teacher.3.target_ref = bf16[512,256]{1,0:T(8,128)(2,1)} custom-call(s32[3]{0:T(128)} %pad_add_fusion.info, bf16[256,4096]{1,0:T(8,128)(2,1)} %bitcast.89, bf16[256,512]{1,0:T(8,128)(2,1)} %copy-done.4, bf16[256,512]{1,0:T(8,128)(2,1)} %copy-done.20, bf16[256,512]{1,0:T(8,128)(2,1)} %copy-done.15, bf16[256,512]{1,0:T(8,128)(2,1)} %collective-permute-done.18.refs_3_.refs_11_, ...), custom_call_target="tpu_custom_call" | custom-call | flops 4294967296 | bytes 1048576 | tf_op jit(solution)/shard_map/teacher/pallas_call | solution.py:201
  105.7 0.5 collective-permute-start.23
  106.3 0.4 collective-permute-start.27
  106.8 0.1 copy-done.30
  106.9 0.4 copy-done.32
  107.5 9.1 %student.2 = (f32[128,512]{1,0:T(8,128)}, bf16[128,512]{1,0:T(8,128)(2,1)}, f32[1,256]{1,0:T(1,128)}, f32[4,256,256]{2,1,0:T(8,128)}, bf16[4,256,256]{2,1,0:T(8,128)(2,1)}) custom-call(s32[3]{0:T(128)} %pad_add_fusion.info, bf16[128,2048]{1,0:T(8,128)(2,1)} %bitcast.86, bf16[128,1024]{1,0:T(8,128)(2,1)} %copy-done.10, bf16[512,256]{1,0:T(8,128)(2,1)} %teacher.2.target_ref, ...), custom_call_target="tpu_custom_call" | custom-call | flops 3221225472 | bytes 2097152 | tf_op jit(solution)/shard_map/student/pallas_call | solution.py:354
  116.7 0.6 copy-done.31
  117.4 0.7 copy-done.36
  118.1 9.4 %student.3 = (f32[128,512]{1,0:T(8,128)}, bf16[128,512]{1,0:T(8,128)(2,1)}, f32[1,256]{1,0:T(1,128)}, f32[4,256,256]{2,1,0:T(8,128)}, bf16[4,256,256]{2,1,0:T(8,128)(2,1)}) custom-call(s32[3]{0:T(128)} %pad_add_fusion.info, bf16[128,2048]{1,0:T(8,128)(2,1)} %bitcast.87, bf16[128,1024]{1,0:T(8,128)(2,1)} %copy-done.10, bf16[512,256]{1,0:T(8,128)(2,1)} %teacher.3.target_ref, ...), custom_call_target="tpu_custom_call" | custom-call | flops 3221225472 | bytes 2097152 | tf_op jit(solution)/shard_map/student/pallas_call | solution.py:354
  127.5 0.8 add.63
  128.2 0.5 collective-permute-start.42
  128.8 0.1 collective-permute-start.32
  128.9 0.4 collective-permute-start.36
  129.3 1.5 collective-permute-start.30
  130.8 0.5 collective-permute-start.31
  131.3 0.5 collective-permute-done.42
  131.8 0.5 fusion.10
  132.3 3.3 %collective-permute-done.30 = bf16[128,512]{1,0:T(8,128)(2,1)S(1)} collective-permute-done((bf16[128,512]{1,0:T(8,128)(2,1)S(1)}, bf16[128,512]{1,0:T(8,128)(2,1)S(1)}, u32[]{:S(2)}, u32[]{:S(2)}) %collective-permute-start.30) | collective-permute-done | bytes 131104 | tf_op jit(solution)/shard_map/ppermute | solution.py:50
  135.7 2.0 %collective-permute-done.31 = bf16[128,512]{1,0:T(8,128)(2,1)S(1)} collective-permute-done((bf16[128,512]{1,0:T(8,128)(2,1)}, bf16[128,512]{1,0:T(8,128)(2,1)S(1)}, u32[]{:S(2)}, u32[]{:S(2)}) %collective-permute-start.31) | collective-permute-done | bytes 131104 | tf_op jit(solution)/shard_map/ppermute | solution.py:50
  137.7 2.2 %maximum_select_fusion = f32[1,128,2048]{2,1,0:T(8,128)} fusion(f32[1,128,512]{2,1,0:T(8,128)S(1)} %bitcast_convert_fusion, f32[1,128,512]{2,1,0:T(8,128)S(1)} %bitcast_convert_fusion.1, f32[1,128,512]{2,1,0:T(8,128)} %bitcast.83, f32[1,128,512]{2,1,0:T(8,128)S(1)} %bitcast.82, pred[]{:T(512)S(6)} %eq.5), kind=kLoop, calls=%fused_computation | loop fusion | flops 1835008 | bytes 2097153 | tf_op jit(solution)/shard_map/jit(_where)/select_n | solution.py:473
  139.8 0.2 fusion.11
  140.0 1.4 collective-permute-start.33
  141.5 1.3 collective-permute-start.34
  142.8 1.3 collective-permute-start.35
  144.1 0.2 fusion.12
  144.3 1.3 collective-permute-start.37
  145.6 1.3 collective-permute-start.38
  147.0 1.3 collective-permute-start.39
  148.3 25.0 %collective-permute-done.34 = bf16[256,256]{1,0:T(8,128)(2,1)S(1)} collective-permute-done((bf16[256,256]{1,0:T(8,128)(2,1)S(1)}, bf16[256,256]{1,0:T(8,128)(2,1)S(1)}, u32[]{:S(2)}, u32[]{:S(2)}) %collective-permute-start.34) | collective-permute-done | bytes 131104 | tf_op jit(solution)/shard_map/ppermute | solution.py:45
  173.4 1.6 collective-permute-start.40
  175.0 2.4 %collective-permute-done.38 = bf16[256,256]{1,0:T(8,128)(2,1)S(1)} collective-permute-done((bf16[256,256]{1,0:T(8,128)(2,1)S(1)}, bf16[256,256]{1,0:T(8,128)(2,1)S(1)}, u32[]{:S(2)}, u32[]{:S(2)}) %collective-permute-start.38) | collective-permute-done | bytes 131104 | tf_op jit(solution)/shard_map/ppermute | solution.py:45
  177.5 1.6 collective-permute-start.41
  179.1 2.7 %collective-permute-done.41 = bf16[128,256]{1,0:T(8,128)(2,1)S(1)} collective-permute-done((bf16[128,256]{1,0:T(8,128)(2,1)S(1)}, bf16[128,256]{1,0:T(8,128)(2,1)S(1)}, u32[]{:S(2)}, u32[]{:S(2)}) %collective-permute-start.41) | collective-permute-done | bytes 65568 | tf_op jit(solution)/shard_map/ppermute | solution.py:50
  181.9 0.7 maximum_select_fusion.2
  182.6 0.7 maximum_select_fusion.1
  (133 shorter events, 1.6 us)
Async XLA Ops:
  0.6 14.7 %copy-start.5 = (bf16[1,128,2048]{2,1,0:T(8,128)(2,1)S(1)}, bf16[1,128,2048]{2,1,0:T(8,128)(2,1)}, u32[]{:S(2)}) copy-start(bf16[1,128,2048]{2,1,0:T(8,128)(2,1)} %param.11) | copy-start | bytes 1572868
  1.7 13.7 %collective-permute-start.8 = (bf16[128,512]{1,0:T(8,128)(2,1)S(1)}, bf16[128,512]{1,0:T(8,128)(2,1)S(1)}, u32[]{:S(2)}, u32[]{:S(2)}) collective-permute-start(bf16[128,512]{1,0:T(8,128)(2,1)S(1)} %pad_maximum_fusion.3), channel_id=1, source_target_pairs={{0,8},{8,0},{16,24},{24,16},{1,9},{9,1},{17,25},{25,17},{2,10},{10... | collective-permute-start | bytes 393224 | tf_op jit(solution)/shard_map/ppermute | solution.py:50
  5.9 65.2 %copy-start.3 = (bf16[256,512]{1,0:T(8,128)(2,1)}, bf16[256,512]{1,0:T(8,128)(2,1)S(1)}, u32[]{:S(2)}) copy-start(bf16[256,512]{1,0:T(8,128)(2,1)S(1)} %pad_maximum_fusion.refs_0_.refs_8_) | copy-start | bytes 786436
  5.9 10.9 %collective-permute-start.2 = (bf16[256,512]{1,0:T(8,128)(2,1)S(1)}, bf16[256,512]{1,0:T(8,128)(2,1)S(1)}, u32[]{:S(2)}, u32[]{:S(2)}) collective-permute-start(bf16[256,512]{1,0:T(8,128)(2,1)S(1)} %pad_maximum_fusion.refs_0_.refs_8_), channel_id=1, source_target_pairs={{0,2},{1,3},{2,4},{3,5},{4,6},{5,7},{8,10},{9,11},{10,12},{11,13},... | collective-permute-start | bytes 786440 | tf_op jit(solution)/shard_map/ppermute | solution.py:39
  9.4 12.3 %collective-permute-start.4 = (bf16[256,512]{1,0:T(8,128)(2,1)S(1)}, bf16[256,512]{1,0:T(8,128)(2,1)S(1)}, u32[]{:S(2)}, u32[]{:S(2)}) collective-permute-start(bf16[256,512]{1,0:T(8,128)(2,1)S(1)} %pad_maximum_fusion.refs_0_.refs_8_), channel_id=1, source_target_pairs={{0,4},{1,5},{2,6},{3,7},{8,12},{9,13},{10,14},{11,15},{16,20},{17,... | collective-permute-start | bytes 786440 | tf_op jit(solution)/shard_map/ppermute | solution.py:39
  13.9 22.5 %collective-permute-start.6 = (bf16[256,512]{1,0:T(8,128)(2,1)S(1)}, bf16[256,512]{1,0:T(8,128)(2,1)S(1)}, u32[]{:S(2)}, u32[]{:S(2)}) collective-permute-start(bf16[256,512]{1,0:T(8,128)(2,1)S(1)} %pad_maximum_fusion.refs_0_.refs_8_), channel_id=1, source_target_pairs={{0,6},{1,7},{8,14},{9,15},{16,22},{17,23},{24,30},{25,31}} | collective-permute-start | bytes 786440 | tf_op jit(solution)/shard_map/ppermute | solution.py:39
  15.2 26.5 %collective-permute-start.1 = (bf16[256,512]{1,0:T(8,128)(2,1)S(1)}, bf16[256,512]{1,0:T(8,128)(2,1)S(1)}, u32[]{:S(2)}, u32[]{:S(2)}) collective-permute-start(bf16[256,512]{1,0:T(8,128)(2,1)S(1)} %pad_maximum_fusion.refs_0_.refs_8_), channel_id=1, source_target_pairs={{0,1},{1,0},{2,3},{3,2},{4,5},{5,4},{6,7},{7,6},{8,9},{9,8},{10,11... | collective-permute-start | bytes 786440 | tf_op jit(solution)/shard_map/ppermute | solution.py:50
  15.5 66.7 %copy-start.6 = (bf16[256,256]{1,0:T(8,128)(2,1)}, bf16[256,256]{1,0:T(8,128)(2,1)S(1)}, u32[]{:S(2)}) copy-start(bf16[256,256]{1,0:T(8,128)(2,1)S(1)} %pad_maximum_fusion.4.refs_0_.refs_8_) | copy-start | bytes 393220
  15.5 27.6 %collective-permute-start.10 = (bf16[256,256]{1,0:T(8,128)(2,1)S(1)}, bf16[256,256]{1,0:T(8,128)(2,1)S(1)}, u32[]{:S(2)}, u32[]{:S(2)}) collective-permute-start(bf16[256,256]{1,0:T(8,128)(2,1)S(1)} %pad_maximum_fusion.4.refs_0_.refs_8_), channel_id=1, source_target_pairs={{0,2},{1,3},{2,4},{3,5},{4,6},{5,7},{8,10},{9,11},{10,12},{11,13},... | collective-permute-start | bytes 393224 | tf_op jit(solution)/shard_map/ppermute | solution.py:39
  16.8 65.4 %copy-start.4 = (bf16[256,512]{1,0:T(8,128)(2,1)}, bf16[256,512]{1,0:T(8,128)(2,1)S(1)}, u32[]{:S(2)}) copy-start(bf16[256,512]{1,0:T(8,128)(2,1)S(1)} %pad_maximum_fusion.2.refs_0_.refs_8_) | copy-start | bytes 786436
  16.8 54.3 %copy-start.11 = (bf16[256,512]{1,0:T(8,128)(2,1)}, bf16[256,512]{1,0:T(8,128)(2,1)S(1)}, u32[]{:S(2)}) copy-start(bf16[256,512]{1,0:T(8,128)(2,1)S(1)} %collective-permute-done.2.refs_2_.refs_10_) | copy-start | bytes 786436
  16.8 45.1 %collective-permute-start = (bf16[128,1024]{1,0:T(8,128)(2,1)S(1)}, bf16[128,1024]{1,0:T(8,128)(2,1)S(1)}, u32[]{:S(2)}, u32[]{:S(2)}) collective-permute-start(bf16[128,1024]{1,0:T(8,128)(2,1)S(1)} %dynamic-slice_bitcast_fusion), channel_id=1, source_target_pairs={{0,8},{8,0},{16,24},{24,16},{1,9},{9,1},{17,25},{25,17},{2,10},{10... | collective-permute-start | bytes 786440 | tf_op jit(solution)/shard_map/ppermute | solution.py:50
  21.7 49.4 %copy-start.12 = (bf16[256,512]{1,0:T(8,128)(2,1)}, bf16[256,512]{1,0:T(8,128)(2,1)S(1)}, u32[]{:S(2)}) copy-start(bf16[256,512]{1,0:T(8,128)(2,1)S(1)} %collective-permute-done.4.refs_4_.refs_12_) | copy-start | bytes 786436
  21.7 40.8 %collective-permute-start.17 = (bf16[256,512]{1,0:T(8,128)(2,1)S(1)}, bf16[256,512]{1,0:T(8,128)(2,1)S(1)}, u32[]{:S(2)}, u32[]{:S(2)}) collective-permute-start(bf16[256,512]{1,0:T(8,128)(2,1)S(1)} %pad_maximum_fusion.2.refs_0_.refs_8_), channel_id=1, source_target_pairs={{0,2},{1,3},{2,4},{3,5},{4,6},{5,7},{8,10},{9,11},{10,12},{11,13},... | collective-permute-start | bytes 786440 | tf_op jit(solution)/shard_map/ppermute | solution.py:39
  36.4 34.7 %copy-start.13 = (bf16[256,512]{1,0:T(8,128)(2,1)}, bf16[256,512]{1,0:T(8,128)(2,1)S(1)}, u32[]{:S(2)}) copy-start(bf16[256,512]{1,0:T(8,128)(2,1)S(1)} %collective-permute-done.6.refs_6_.refs_14_) | copy-start | bytes 786436
  36.4 8.1 %collective-permute-start.12 = (bf16[256,256]{1,0:T(8,128)(2,1)S(1)}, bf16[256,256]{1,0:T(8,128)(2,1)S(1)}, u32[]{:S(2)}, u32[]{:S(2)}) collective-permute-start(bf16[256,256]{1,0:T(8,128)(2,1)S(1)} %pad_maximum_fusion.4.refs_0_.refs_8_), channel_id=1, source_target_pairs={{0,4},{1,5},{2,6},{3,7},{8,12},{9,13},{10,14},{11,15},{16,20},{17,... | collective-permute-start | bytes 393224 | tf_op jit(solution)/shard_map/ppermute | solution.py:39
  41.7 29.4 %copy-start.14 = (bf16[256,512]{1,0:T(8,128)(2,1)}, bf16[256,512]{1,0:T(8,128)(2,1)S(1)}, u32[]{:S(2)}) copy-start(bf16[256,512]{1,0:T(8,128)(2,1)S(1)} %collective-permute-done.1.refs_1_.refs_9_) | copy-start | bytes 786436
  41.7 8.1 %collective-permute-start.14 = (bf16[256,256]{1,0:T(8,128)(2,1)S(1)}, bf16[256,256]{1,0:T(8,128)(2,1)S(1)}, u32[]{:S(2)}, u32[]{:S(2)}) collective-permute-start(bf16[256,256]{1,0:T(8,128)(2,1)S(1)} %pad_maximum_fusion.4.refs_0_.refs_8_), channel_id=1, source_target_pairs={{0,6},{1,7},{8,14},{9,15},{16,22},{17,23},{24,30},{25,31}} | collective-permute-start | bytes 393224 | tf_op jit(solution)/shard_map/ppermute | solution.py:39
  43.1 51.0 %copy-start.21 = (bf16[256,256]{1,0:T(8,128)(2,1)}, bf16[256,256]{1,0:T(8,128)(2,1)S(1)}, u32[]{:S(2)}) copy-start(bf16[256,256]{1,0:T(8,128)(2,1)S(1)} %collective-permute-done.10.refs_2_.refs_10_) | copy-start | bytes 393220
  43.1 18.8 %collective-permute-start.9 = (bf16[256,256]{1,0:T(8,128)(2,1)S(1)}, bf16[256,256]{1,0:T(8,128)(2,1)S(1)}, u32[]{:S(2)}, u32[]{:S(2)}) collective-permute-start(bf16[256,256]{1,0:T(8,128)(2,1)S(1)} %pad_maximum_fusion.4.refs_0_.refs_8_), channel_id=1, source_target_pairs={{0,1},{1,0},{2,3},{3,2},{4,5},{5,4},{6,7},{7,6},{8,9},{9,8},{10,11... | collective-permute-start | bytes 393224 | tf_op jit(solution)/shard_map/ppermute | solution.py:50
  44.5 18.0 %copy-start.22 = (bf16[256,256]{1,0:T(8,128)(2,1)}, bf16[256,256]{1,0:T(8,128)(2,1)S(1)}, u32[]{:S(2)}) copy-start(bf16[256,256]{1,0:T(8,128)(2,1)S(1)} %collective-permute-done.12.refs_4_.refs_12_) | copy-start | bytes 393220
  44.5 18.8 %collective-permute-start.19 = (bf16[256,512]{1,0:T(8,128)(2,1)S(1)}, bf16[256,512]{1,0:T(8,128)(2,1)S(1)}, u32[]{:S(2)}, u32[]{:S(2)}) collective-permute-start(bf16[256,512]{1,0:T(8,128)(2,1)S(1)} %pad_maximum_fusion.2.refs_0_.refs_8_), channel_id=1, source_target_pairs={{0,4},{1,5},{2,6},{3,7},{8,12},{9,13},{10,14},{11,15},{16,20},{17,... | collective-permute-start | bytes 786440 | tf_op jit(solution)/shard_map/ppermute | solution.py:39
  49.9 12.6 %copy-start.24 = (bf16[256,256]{1,0:T(8,128)(2,1)}, bf16[256,256]{1,0:T(8,128)(2,1)S(1)}, u32[]{:S(2)}) copy-start(bf16[256,256]{1,0:T(8,128)(2,1)S(1)} %collective-permute-done.14.refs_6_.refs_14_) | copy-start | bytes 393220
  49.9 15.9 %collective-permute-start.21 = (bf16[256,512]{1,0:T(8,128)(2,1)S(1)}, bf16[256,512]{1,0:T(8,128)(2,1)S(1)}, u32[]{:S(2)}, u32[]{:S(2)}) collective-permute-start(bf16[256,512]{1,0:T(8,128)(2,1)S(1)} %pad_maximum_fusion.2.refs_0_.refs_8_), channel_id=1, source_target_pairs={{0,6},{1,7},{8,14},{9,15},{16,22},{17,23},{24,30},{25,31}} | collective-permute-start | bytes 786440 | tf_op jit(solution)/shard_map/ppermute | solution.py:39
  61.9 8.5 %collective-permute-start.3 = (bf16[256,512]{1,0:T(8,128)(2,1)S(1)}, bf16[256,512]{1,0:T(8,128)(2,1)S(1)}, u32[]{:S(2)}, u32[]{:S(2)}) collective-permute-start(bf16[256,512]{1,0:T(8,128)(2,1)S(1)} %collective-permute-done.2.refs_2_.refs_10_), channel_id=1, source_target_pairs={{0,1},{1,0},{2,3},{3,2},{4,5},{5,4},{6,7},{7,6},{8,9},{9,8},{10,11... | collective-permute-start | bytes 786440 | tf_op jit(solution)/shard_map/ppermute | solution.py:50
  62.0 20.2 %copy-start.10 = (bf16[128,1024]{1,0:T(8,128)(2,1)}, bf16[128,1024]{1,0:T(8,128)(2,1)S(1)}, u32[]{:S(2)}) copy-start(bf16[128,1024]{1,0:T(8,128)(2,1)S(1)} %collective-permute-done.far_q_ref) | copy-start | bytes 786436
  62.0 8.6 %collective-permute-start.5 = (bf16[256,512]{1,0:T(8,128)(2,1)S(1)}, bf16[256,512]{1,0:T(8,128)(2,1)S(1)}, u32[]{:S(2)}, u32[]{:S(2)}) collective-permute-start(bf16[256,512]{1,0:T(8,128)(2,1)S(1)} %collective-permute-done.4.refs_4_.refs_12_), channel_id=1, source_target_pairs={{0,1},{1,0},{2,3},{3,2},{4,5},{5,4},{6,7},{7,6},{8,9},{9,8},{10,11... | collective-permute-start | bytes 786440 | tf_op jit(solution)/shard_map/ppermute | solution.py:50
  62.5 19.7 %copy-start.15 = (bf16[256,512]{1,0:T(8,128)(2,1)}, bf16[256,512]{1,0:T(8,128)(2,1)S(1)}, u32[]{:S(2)}) copy-start(bf16[256,512]{1,0:T(8,128)(2,1)S(1)} %collective-permute-done.17.refs_2_.refs_10_) | copy-start | bytes 786436
  62.5 8.4 %collective-permute-start.7 = (bf16[256,512]{1,0:T(8,128)(2,1)S(1)}, bf16[256,512]{1,0:T(8,128)(2,1)}, u32[]{:S(2)}, u32[]{:S(2)}) collective-permute-start(bf16[256,512]{1,0:T(8,128)(2,1)S(1)} %collective-permute-done.6.refs_6_.refs_14_), channel_id=1, source_target_pairs={{0,1},{1,0},{2,3},{3,2},{4,5},{5,4},{6,7},{7,6},{8,9},{9,8},{10,11... | collective-permute-start | bytes 786440 | tf_op jit(solution)/shard_map/ppermute | solution.py:50
  63.4 42.3 %copy-start.7 = (bf16[256,256]{1,0:T(8,128)(2,1)}, bf16[256,256]{1,0:T(8,128)(2,1)S(1)}, u32[]{:S(2)}) copy-start(bf16[256,256]{1,0:T(8,128)(2,1)S(1)} %pad_maximum_fusion.5.refs_0_.refs_8_) | copy-start | bytes 393220
  63.4 18.9 %copy-start.16 = (bf16[256,512]{1,0:T(8,128)(2,1)}, bf16[256,512]{1,0:T(8,128)(2,1)S(1)}, u32[]{:S(2)}) copy-start(bf16[256,512]{1,0:T(8,128)(2,1)S(1)} %collective-permute-done.19.refs_4_.refs_12_) | copy-start | bytes 786436
  63.4 29.3 %collective-permute-start.16 = (bf16[256,512]{1,0:T(8,128)(2,1)S(1)}, bf16[256,512]{1,0:T(8,128)(2,1)S(1)}, u32[]{:S(2)}, u32[]{:S(2)}) collective-permute-start(bf16[256,512]{1,0:T(8,128)(2,1)S(1)} %pad_maximum_fusion.2.refs_0_.refs_8_), channel_id=1, source_target_pairs={{0,1},{1,0},{2,3},{3,2},{4,5},{5,4},{6,7},{7,6},{8,9},{9,8},{10,11... | collective-permute-start | bytes 786440 | tf_op jit(solution)/shard_map/ppermute | solution.py:50
  65.8 16.5 %copy-start.17 = (bf16[256,512]{1,0:T(8,128)(2,1)}, bf16[256,512]{1,0:T(8,128)(2,1)S(1)}, u32[]{:S(2)}) copy-start(bf16[256,512]{1,0:T(8,128)(2,1)S(1)} %collective-permute-done.21.refs_6_.refs_14_) | copy-start | bytes 786436
  65.8 16.5 %collective-permute-start.24 = (bf16[256,256]{1,0:T(8,128)(2,1)S(1)}, bf16[256,256]{1,0:T(8,128)(2,1)}, u32[]{:S(2)}, u32[]{:S(2)}) collective-permute-start(bf16[256,256]{1,0:T(8,128)(2,1)S(1)} %pad_maximum_fusion.5.refs_0_.refs_8_), channel_id=1, source_target_pairs={{0,2},{1,3},{2,4},{3,5},{4,6},{5,7},{8,10},{9,11},{10,12},{11,13},... | collective-permute-start | bytes 393224 | tf_op jit(solution)/shard_map/ppermute | solution.py:39
  70.4 23.7 %collective-permute-start.18 = (bf16[256,512]{1,0:T(8,128)(2,1)S(1)}, bf16[256,512]{1,0:T(8,128)(2,1)}, u32[]{:S(2)}, u32[]{:S(2)}) collective-permute-start(bf16[256,512]{1,0:T(8,128)(2,1)S(1)} %collective-permute-done.17.refs_2_.refs_10_), channel_id=1, source_target_pairs={{0,1},{1,0},{2,3},{3,2},{4,5},{5,4},{6,7},{7,6},{8,9},{9,8},{10,11... | collective-permute-start | bytes 786440 | tf_op jit(solution)/shard_map/ppermute | solution.py:50
  70.6 23.6 %collective-permute-start.20 = (bf16[256,512]{1,0:T(8,128)(2,1)S(1)}, bf16[256,512]{1,0:T(8,128)(2,1)}, u32[]{:S(2)}, u32[]{:S(2)}) collective-permute-start(bf16[256,512]{1,0:T(8,128)(2,1)S(1)} %collective-permute-done.19.refs_4_.refs_12_), channel_id=1, source_target_pairs={{0,1},{1,0},{2,3},{3,2},{4,5},{5,4},{6,7},{7,6},{8,9},{9,8},{10,11... | collective-permute-start | bytes 786440 | tf_op jit(solution)/shard_map/ppermute | solution.py:50
  70.9 23.8 %collective-permute-start.22 = (bf16[256,512]{1,0:T(8,128)(2,1)S(1)}, bf16[256,512]{1,0:T(8,128)(2,1)}, u32[]{:S(2)}, u32[]{:S(2)}) collective-permute-start(bf16[256,512]{1,0:T(8,128)(2,1)S(1)} %collective-permute-done.21.refs_6_.refs_14_), channel_id=1, source_target_pairs={{0,1},{1,0},{2,3},{3,2},{4,5},{5,4},{6,7},{7,6},{8,9},{9,8},{10,11... | collective-permute-start | bytes 786440 | tf_op jit(solution)/shard_map/ppermute | solution.py:50
  71.3 22.8 %copy-start.23 = (bf16[256,256]{1,0:T(8,128)(2,1)S(1)}, bf16[256,256]{1,0:T(8,128)(2,1)}, u32[]{:S(2)}) copy-start(bf16[256,256]{1,0:T(8,128)(2,1)} %copy-done.22) | copy-start | bytes 393220
  71.3 23.3 %copy-start.25 = (bf16[256,256]{1,0:T(8,128)(2,1)S(1)}, bf16[256,256]{1,0:T(8,128)(2,1)}, u32[]{:S(2)}) copy-start(bf16[256,256]{1,0:T(8,128)(2,1)} %copy-done.24) | copy-start | bytes 393220
  82.3 23.4 %collective-permute-start.26 = (bf16[256,256]{1,0:T(8,128)(2,1)S(1)}, bf16[256,256]{1,0:T(8,128)(2,1)S(1)}, u32[]{:S(2)}, u32[]{:S(2)}) collective-permute-start(bf16[256,256]{1,0:T(8,128)(2,1)S(1)} %pad_maximum_fusion.5.refs_0_.refs_8_), channel_id=1, source_target_pairs={{0,4},{1,5},{2,6},{3,7},{8,12},{9,13},{10,14},{11,15},{16,20},{17,... | collective-permute-start | bytes 393224 | tf_op jit(solution)/shard_map/ppermute | solution.py:39
  92.8 13.4 %collective-permute-start.28 = (bf16[256,256]{1,0:T(8,128)(2,1)S(1)}, bf16[256,256]{1,0:T(8,128)(2,1)S(1)}, u32[]{:S(2)}, u32[]{:S(2)}) collective-permute-start(bf16[256,256]{1,0:T(8,128)(2,1)S(1)} %pad_maximum_fusion.5.refs_0_.refs_8_), channel_id=1, source_target_pairs={{0,6},{1,7},{8,14},{9,15},{16,22},{17,23},{24,30},{25,31}} | collective-permute-start | bytes 393224 | tf_op jit(solution)/shard_map/ppermute | solution.py:39
  94.1 12.2 %collective-permute-start.11 = (bf16[256,256]{1,0:T(8,128)(2,1)S(1)}, bf16[256,256]{1,0:T(8,128)(2,1)S(1)}, u32[]{:S(2)}, u32[]{:S(2)}) collective-permute-start(bf16[256,256]{1,0:T(8,128)(2,1)S(1)} %collective-permute-done.10.refs_2_.refs_10_), channel_id=1, source_target_pairs={{0,1},{1,0},{2,3},{3,2},{4,5},{5,4},{6,7},{7,6},{8,9},{9,8},{10,11... | collective-permute-start | bytes 393224 | tf_op jit(solution)/shard_map/ppermute | solution.py:50
  94.2 12.5 %collective-permute-start.13 = (bf16[256,256]{1,0:T(8,128)(2,1)S(1)}, bf16[256,256]{1,0:T(8,128)(2,1)S(1)}, u32[]{:S(2)}, u32[]{:S(2)}) collective-permute-start(bf16[256,256]{1,0:T(8,128)(2,1)S(1)} %copy-done.23), channel_id=1, source_target_pairs={{0,1},{1,0},{2,3},{3,2},{4,5},{5,4},{6,7},{7,6},{8,9},{9,8},{10,11... | collective-permute-start | bytes 393224 | tf_op jit(solution)/shard_map/ppermute | solution.py:50
  94.7 12.1 %collective-permute-start.15 = (bf16[256,256]{1,0:T(8,128)(2,1)S(1)}, bf16[256,256]{1,0:T(8,128)(2,1)S(1)}, u32[]{:S(2)}, u32[]{:S(2)}) collective-permute-start(bf16[256,256]{1,0:T(8,128)(2,1)S(1)} %copy-done.25), channel_id=1, source_target_pairs={{0,1},{1,0},{2,3},{3,2},{4,5},{5,4},{6,7},{7,6},{8,9},{9,8},{10,11... | collective-permute-start | bytes 393224 | tf_op jit(solution)/shard_map/ppermute | solution.py:50
  105.7 10.9 %collective-permute-start.23 = (bf16[256,256]{1,0:T(8,128)(2,1)S(1)}, bf16[256,256]{1,0:T(8,128)(2,1)S(1)}, u32[]{:S(2)}, u32[]{:S(2)}) collective-permute-start(bf16[256,256]{1,0:T(8,128)(2,1)S(1)} %pad_maximum_fusion.5.refs_0_.refs_8_), channel_id=1, source_target_pairs={{0,1},{1,0},{2,3},{3,2},{4,5},{5,4},{6,7},{7,6},{8,9},{9,8},{10,11... | collective-permute-start | bytes 393224 | tf_op jit(solution)/shard_map/ppermute | solution.py:50
  106.2 10.5 %collective-permute-start.25 = (bf16[256,256]{1,0:T(8,128)(2,1)}, bf16[256,256]{1,0:T(8,128)(2,1)S(1)}, u32[]{:S(2)}, u32[]{:S(2)}) collective-permute-start(bf16[256,256]{1,0:T(8,128)(2,1)} %collective-permute-done.24.refs_2_.refs_10_), channel_id=1, source_target_pairs={{0,1},{1,0},{2,3},{3,2},{4,5},{5,4},{6,7},{7,6},{8,9},{9,8},{10,11... | collective-permute-start | bytes 393224 | tf_op jit(solution)/shard_map/ppermute | solution.py:50
  106.3 10.4 %collective-permute-start.27 = (bf16[256,256]{1,0:T(8,128)(2,1)S(1)}, bf16[256,256]{1,0:T(8,128)(2,1)S(1)}, u32[]{:S(2)}, u32[]{:S(2)}) collective-permute-start(bf16[256,256]{1,0:T(8,128)(2,1)S(1)} %collective-permute-done.26.refs_4_.refs_12_), channel_id=1, source_target_pairs={{0,1},{1,0},{2,3},{3,2},{4,5},{5,4},{6,7},{7,6},{8,9},{9,8},{10,11... | collective-permute-start | bytes 393224 | tf_op jit(solution)/shard_map/ppermute | solution.py:50
  106.7 10.0 %collective-permute-start.29 = (bf16[256,256]{1,0:T(8,128)(2,1)S(1)}, bf16[256,256]{1,0:T(8,128)(2,1)S(1)}, u32[]{:S(2)}, u32[]{:S(2)}) collective-permute-start(bf16[256,256]{1,0:T(8,128)(2,1)S(1)} %collective-permute-done.28.refs_6_.refs_14_), channel_id=1, source_target_pairs={{0,1},{1,0},{2,3},{3,2},{4,5},{5,4},{6,7},{7,6},{8,9},{9,8},{10,11... | collective-permute-start | bytes 393224 | tf_op jit(solution)/shard_map/ppermute | solution.py:50
  116.6 12.7 %copy-start.29 = (bf16[128,512]{1,0:T(8,128)(2,1)S(1)}, bf16[128,512]{1,0:T(8,128)(2,1)}, u32[]{:S(2)}) copy-start(bf16[128,512]{1,0:T(8,128)(2,1)} %get-tuple-element.16) | copy-start | bytes 393220
  116.6 21.0 %copy-start.2 = (f32[128,512]{1,0:T(8,128)S(1)}, f32[128,512]{1,0:T(8,128)}, u32[]{:S(2)}) copy-start(f32[128,512]{1,0:T(8,128)} %get-tuple-element.14) | copy-start | bytes 786436
  127.4 12.4 %copy-start.1 = (f32[4,256,256]{2,1,0:T(8,128)S(1)}, f32[4,256,256]{2,1,0:T(8,128)}, u32[]{:S(2)}) copy-start(f32[4,256,256]{2,1,0:T(8,128)} %get-tuple-element.18) | copy-start | bytes 3145732
  128.2 3.6 %collective-permute-start.42 = (f32[128]{0:T(128)S(1)}, f32[128]{0:T(128)S(1)}, u32[]{:S(2)}, u32[]{:S(2)}) collective-permute-start(f32[128]{0:T(128)S(1)} %fusion.9), channel_id=1, source_target_pairs={{0,8},{8,0},{16,24},{24,16},{1,9},{9,1},{17,25},{25,17},{2,10},{10... | collective-permute-start | bytes 1544 | tf_op jit(solution)/shard_map/ppermute | solution.py:50
  128.8 11.1 %collective-permute-start.32 = (bf16[4,256,256]{2,1,0:T(8,128)(2,1)S(1)}, bf16[4,256,256]{2,1,0:T(8,128)(2,1)S(1)}, u32[]{:S(2)}, u32[]{:S(2)}) collective-permute-start(bf16[4,256,256]{2,1,0:T(8,128)(2,1)S(1)} %copy-done.9), channel_id=1, source_target_pairs={{0,1},{1,0},{2,3},{3,2},{4,5},{5,4},{6,7},{7,6},{8,9},{9,8},{10,11... | collective-permute-start | bytes 1572872 | tf_op jit(solution)/shard_map/ppermute | solution.py:50
  128.9 15.2 %collective-permute-start.36 = (bf16[4,256,256]{2,1,0:T(8,128)(2,1)}, bf16[4,256,256]{2,1,0:T(8,128)(2,1)S(1)}, u32[]{:S(2)}, u32[]{:S(2)}) collective-permute-start(bf16[4,256,256]{2,1,0:T(8,128)(2,1)} %get-tuple-element.21), channel_id=1, source_target_pairs={{0,1},{1,0},{2,3},{3,2},{4,5},{5,4},{6,7},{7,6},{8,9},{9,8},{10,11... | collective-permute-start | bytes 1572872 | tf_op jit(solution)/shard_map/ppermute | solution.py:50
  129.3 6.4 %collective-permute-start.30 = (bf16[128,512]{1,0:T(8,128)(2,1)S(1)}, bf16[128,512]{1,0:T(8,128)(2,1)S(1)}, u32[]{:S(2)}, u32[]{:S(2)}) collective-permute-start(bf16[128,512]{1,0:T(8,128)(2,1)S(1)} %copy-done.29), channel_id=1, source_target_pairs={{0,8},{8,0},{16,24},{24,16},{1,9},{9,1},{17,25},{25,17},{2,10},{10... | collective-permute-start | bytes 393224 | tf_op jit(solution)/shard_map/ppermute | solution.py:50
  130.8 6.9 %collective-permute-start.31 = (bf16[128,512]{1,0:T(8,128)(2,1)}, bf16[128,512]{1,0:T(8,128)(2,1)S(1)}, u32[]{:S(2)}, u32[]{:S(2)}) collective-permute-start(bf16[128,512]{1,0:T(8,128)(2,1)} %get-tuple-element.17), channel_id=1, source_target_pairs={{0,8},{8,0},{16,24},{24,16},{1,9},{9,1},{17,25},{25,17},{2,10},{10... | collective-permute-start | bytes 393224 | tf_op jit(solution)/shard_map/ppermute | solution.py:50
  140.0 7.0 %collective-permute-start.33 = (bf16[256,256]{1,0:T(8,128)(2,1)S(1)}, bf16[256,256]{1,0:T(8,128)(2,1)S(1)}, u32[]{:S(2)}, u32[]{:S(2)}) collective-permute-start(bf16[256,256]{1,0:T(8,128)(2,1)S(1)} %get-tuple-element.28), channel_id=1, source_target_pairs={{2,0},{3,1},{4,2},{5,3},{6,4},{7,5},{10,8},{11,9},{12,10},{13,11},... | collective-permute-start | bytes 393224 | tf_op jit(solution)/shard_map/ppermute | solution.py:45
  141.5 31.8 %collective-permute-start.34 = (bf16[256,256]{1,0:T(8,128)(2,1)S(1)}, bf16[256,256]{1,0:T(8,128)(2,1)S(1)}, u32[]{:S(2)}, u32[]{:S(2)}) collective-permute-start(bf16[256,256]{1,0:T(8,128)(2,1)S(1)} %get-tuple-element.30), channel_id=1, source_target_pairs={{4,0},{5,1},{6,2},{7,3},{12,8},{13,9},{14,10},{15,11},{20,16},{21,... | collective-permute-start | bytes 393224 | tf_op jit(solution)/shard_map/ppermute | solution.py:45
  142.8 30.6 %collective-permute-start.35 = (bf16[256,256]{1,0:T(8,128)(2,1)S(1)}, bf16[256,256]{1,0:T(8,128)(2,1)S(1)}, u32[]{:S(2)}, u32[]{:S(2)}) collective-permute-start(bf16[256,256]{1,0:T(8,128)(2,1)S(1)} %get-tuple-element.29), channel_id=1, source_target_pairs={{6,0},{7,1},{14,8},{15,9},{22,16},{23,17},{30,24},{31,25}} | collective-permute-start | bytes 393224 | tf_op jit(solution)/shard_map/ppermute | solution.py:45
  144.3 30.7 %collective-permute-start.37 = (bf16[256,256]{1,0:T(8,128)(2,1)S(1)}, bf16[256,256]{1,0:T(8,128)(2,1)S(1)}, u32[]{:S(2)}, u32[]{:S(2)}) collective-permute-start(bf16[256,256]{1,0:T(8,128)(2,1)S(1)} %get-tuple-element.31), channel_id=1, source_target_pairs={{2,0},{3,1},{4,2},{5,3},{6,4},{7,5},{10,8},{11,9},{12,10},{13,11},... | collective-permute-start | bytes 393224 | tf_op jit(solution)/shard_map/ppermute | solution.py:45
  145.6 31.8 %collective-permute-start.38 = (bf16[256,256]{1,0:T(8,128)(2,1)S(1)}, bf16[256,256]{1,0:T(8,128)(2,1)S(1)}, u32[]{:S(2)}, u32[]{:S(2)}) collective-permute-start(bf16[256,256]{1,0:T(8,128)(2,1)S(1)} %get-tuple-element.33), channel_id=1, source_target_pairs={{4,0},{5,1},{6,2},{7,3},{12,8},{13,9},{14,10},{15,11},{20,16},{21,... | collective-permute-start | bytes 393224 | tf_op jit(solution)/shard_map/ppermute | solution.py:45
  147.0 30.4 %collective-permute-start.39 = (bf16[256,256]{1,0:T(8,128)(2,1)S(1)}, bf16[256,256]{1,0:T(8,128)(2,1)S(1)}, u32[]{:S(2)}, u32[]{:S(2)}) collective-permute-start(bf16[256,256]{1,0:T(8,128)(2,1)S(1)} %get-tuple-element.32), channel_id=1, source_target_pairs={{6,0},{7,1},{14,8},{15,9},{22,16},{23,17},{30,24},{31,25}} | collective-permute-start | bytes 393224 | tf_op jit(solution)/shard_map/ppermute | solution.py:45
  173.4 5.7 %collective-permute-start.40 = (bf16[128,256]{1,0:T(8,128)(2,1)S(1)}, bf16[128,256]{1,0:T(8,128)(2,1)S(1)}, u32[]{:S(2)}, u32[]{:S(2)}) collective-permute-start(bf16[128,256]{1,0:T(8,128)(2,1)S(1)} %slice.195), channel_id=1, source_target_pairs={{0,8},{8,0},{16,24},{24,16},{1,9},{9,1},{17,25},{25,17},{2,10},{10... | collective-permute-start | bytes 196616 | tf_op jit(solution)/shard_map/ppermute | solution.py:50
  177.5 4.3 %collective-permute-start.41 = (bf16[128,256]{1,0:T(8,128)(2,1)S(1)}, bf16[128,256]{1,0:T(8,128)(2,1)S(1)}, u32[]{:S(2)}, u32[]{:S(2)}) collective-permute-start(bf16[128,256]{1,0:T(8,128)(2,1)S(1)} %slice.194), channel_id=1, source_target_pairs={{0,8},{8,0},{16,24},{24,16},{1,9},{9,1},{17,25},{25,17},{2,10},{10... | collective-permute-start | bytes 196616 | tf_op jit(solution)/shard_map/ppermute | solution.py:50
  (16 other events, 57.4 us)

commit v3 on v2

--- a/solution.py
+++ b/solution.py
@@ -34,8 +34,7 @@
 
 
 def shift(value, chips, least=0):
-    size = lax.axis_size("seq")
-    pairs = [(i, i + 2 * chips) for i in range(2 * least, size - 2 * chips)]
+    pairs = [(i, i + 2 * chips) for i in range(2 * least, lax.axis_size("seq") - 2 * chips)]
     return lax.ppermute(value, "seq", pairs)
 
 
@@ -50,14 +49,10 @@
     return lax.ppermute(value, axis, pairs)
 
 
-def spread(own, relay):
-    chips = lax.axis_size("seq") // 2
+def spread(own, relay=False):
     mine = [own]
-    for step in range(1, chips):
-        if step <= 2 or not relay:
-            mine.append(shift(own, step))
-        else:
-            mine.append(shift(mine[-1], 1, step - 1))
+    for step in range(1, lax.axis_size("seq") // 2):
+        mine.append(shift(mine[-1], 1, step - 1) if relay else shift(own, step))
     return mine
 
 
@@ -69,7 +64,7 @@
 
 
 def variants(chips):
-    return [*range(2, chips, 2), chips]
+    return sorted({max(chips - 1, 1), chips})
 
 
 def fold_max(tile):
@@ -114,7 +109,7 @@
     for b in range(2 * chips):
         part = pl.ds(b * rows, rows)
 
-        @pl.when(b < 2 * (chip + 2))
+        @pl.when(b < 2 * jnp.maximum(chip + 1, chips - 1))
         def _():
             for g in range(heads):
                 columns = slice(g * HEAD, (g + 1) * HEAD)
@@ -240,7 +235,7 @@
     for b in range(2 * chips):
         part = pl.ds(b * rows, rows)
 
-        @pl.when(b < 2 * (chip + 2))
+        @pl.when(b < 2 * jnp.maximum(chip + 1, chips - 1))
         def _():
             key_block = key_refs[b][...]
             value_block = value_refs[b][...]
@@ -348,8 +343,8 @@
         pl.BlockSpec((half_rows, width), lambda i, info: (0, pair)),
         pl.BlockSpec((width, rows), full),
     ]
-    in_specs += [pl.BlockSpec((rows, HEAD), lambda i, info: (0, 0))] * len(flat)
-    in_specs += [pl.BlockSpec((rows, HEAD), lambda i, info: (0, 1))] * len(flat)
+    in_specs += [pl.BlockSpec((rows, HEAD), lambda i, info: (0, pair))] * len(flat)
+    in_specs += [pl.BlockSpec((rows, HEAD), lambda i, info: (0, heads + pair))] * len(flat)
     work = GROUP_S * rows * chips * wide
     return pl.pallas_call(
         functools.partial(student_kernel, chips, rows),
@@ -434,27 +429,26 @@
             1,
         )
 
-    teacher_mine = [spread(teacher_rows(0), False)]
     far_rows = swap(pair_rows(1 - bit), "section")
-    student_rows = jnp.concatenate([pair_rows(bit), far_rows], 0)
-    student_mine = []
+    student_all = jnp.concatenate([pair_rows(bit), far_rows], 0)
+
+    chunks = [spread(teacher_rows(pair), pair == 0) for pair in range(student_heads)]
+    student_mine = spread(student_all)
+    far_q = swap(columns(own_q, 1 - bit, q_width), "section")
+
+    targets = []
     for pair in range(student_heads):
-        if pair:
-            teacher_mine.append(spread(teacher_rows(pair), False))
-        key_part = student_rows[:, pair * HEAD : (pair + 1) * HEAD]
-        value_part = student_rows[:, kv_width + pair * HEAD : kv_width + (pair + 1) * HEAD]
-        student_mine.append(spread(jnp.concatenate([key_part, value_part], 1), False))
-    far_q = swap(columns(own_q, 1 - bit, q_width), "section")
+        blocks = both_cores(chunks[pair])
+        made = teacher(
+            info, teacher_query_array[0], blocks, projection[0], pair * per_pair, per_pair
+        )
+        targets.append(made)
+    student_blocks = both_cores(student_mine)
 
     query_own, query_far, key_own, key_far, loss = [], [], [], [], 0.0
     for pair in range(student_heads):
-        blocks = both_cores(teacher_mine[pair])
-        target = teacher(
-            info, teacher_query_array[0], blocks, projection[0], pair * per_pair, per_pair
-        )
-        blocks = both_cores(student_mine[pair])
         near, away, squares, kept, sent = student(
-            info, own_q, far_q, target, blocks, pair, student_heads
+            info, own_q, far_q, targets[pair], student_blocks, pair, student_heads
         )
         query_own.append(near)
         query_far.append(swap(away, "section"))

time: 184 us -> 173 us (0.940)
  starting transfers between devices: 87 us -> 44.4 us
  waiting for transfers between devices: 43.7 us -> 68.2 us
  Pallas kernels: 40.3 us -> 50.1 us
    ppermute x12 -> x9, starting transfers between devices: 65.5 us -> 26.8 us  [shift(): return lax.ppermute(value, 'seq', pairs)]
    ppermute x6, waiting for transfers between devices: 27.5 us -> 43 us  [back(): return lax.ppermute(value, 'seq', pairs)]
    ppermute x25 -> x21, waiting for transfers between devices: 8.57 us -> 14.8 us  [swap(): return lax.ppermute(value, axis, pairs)]
    pallas_call x2, Pallas kernels: 21.8 us -> 27.3 us  [teacher(): pl.pallas_call(functools.partial(teacher_kernel, chips, rows, heads), out...]
    pallas_call x2, Pallas kernels: 18.5 us -> 22.7 us  [student(): pl.pallas_call(functools.partial(student_kernel, chips, rows), out_shape=...]
    ppermute x25 -> x21, starting transfers between devices: 13.6 us -> 9.74 us  [swap(): return lax.ppermute(value, axis, pairs)]
    ppermute x12 -> x9, waiting for transfers between devices: 7.58 us -> 10.3 us  [shift(): return lax.ppermute(value, 'seq', pairs)]
  transfers between devices with their start and end apart: 43 -> 36, of which waited for: 10 -> 12; matrix products, arithmetic and copies ran while one was open for 3% -> 2% of each run, Pallas kernels for 17% -> 29%
where the time goes in v3:
time: 173 us
  waiting for transfers between devices  68.2 us (39%)
  Pallas kernels  50.1 us (29%)
  starting transfers between devices  44.4 us (26%)
  other arithmetic  4.94 us (3%)
  local copies, waits for them, and re-layouts  4.08 us (2%)
    ppermute x6, waiting for transfers between devices, back(): return lax.ppermute(value, 'seq', pairs)  43 us
    pallas_call x2, Pallas kernels, teacher(): pl.pallas_call(functools.partial(teacher_kernel, chips, rows, heads), out...  27.3 us
    ppermute x9, starting transfers between devices, shift(): return lax.ppermute(value, 'seq', pairs)  26.8 us
    pallas_call x2, Pallas kernels, student(): pl.pallas_call(functools.partial(student_kernel, chips, rows), out_shape=...  22.7 us
    ppermute x21, waiting for transfers between devices, swap(): return lax.ppermute(value, axis, pairs)  14.8 us
    ppermute x9, waiting for transfers between devices, shift(): return lax.ppermute(value, 'seq', pairs)  10.3 us
    ppermute x21, starting transfers between devices, swap(): return lax.ppermute(value, axis, pairs)  9.74 us
    ppermute x6, starting transfers between devices, back(): return lax.ppermute(value, 'seq', pairs)  7.88 us
  transfers between devices with their start and end apart: 36, of which 12 were waited for; matrix products, arithmetic and copies ran while one was open for 2% of the time, Pallas kernels for 29%

profile of v3, /device:TPU:0, one launch (start us, length us, event | category | flops | bytes accessed | tf_op | source)
XLA Modules:
  0.0 172.9 jit_solution(1278425908481902823)
XLA Ops:
  0.7 1.2 fusion.13
  1.9 7.0 %collective-permute-start.21 = (bf16[256,512]{1,0:T(8,128)(2,1)S(1)}, bf16[256,512]{1,0:T(8,128)(2,1)S(1)}, u32[]{:S(2)}, u32[]{:S(2)}) collective-permute-start(bf16[256,512]{1,0:T(8,128)(2,1)S(1)} %pad_maximum_fusion.2.refs_0_.refs_8_), channel_id=1, source_target_pairs={{0,6},{1,7},{8,14},{9,15},{16,22},{17,23},{24,30},{25,31}} | collective-permute-start | bytes 786440 | tf_op jit(solution)/shard_map/ppermute | solution.py:38
  8.9 1.3 collective-permute-start.19
  10.2 1.0 dynamic-slice_bitcast_fusion
  11.2 1.6 collective-permute-start
  12.8 0.6 collective-permute-start.8
  13.4 2.5 %collective-permute-start.17 = (bf16[256,512]{1,0:T(8,128)(2,1)S(1)}, bf16[256,512]{1,0:T(8,128)(2,1)S(1)}, u32[]{:S(2)}, u32[]{:S(2)}) collective-permute-start(bf16[256,512]{1,0:T(8,128)(2,1)S(1)} %pad_maximum_fusion.2.refs_0_.refs_8_), channel_id=1, source_target_pairs={{0,2},{1,3},{2,4},{3,5},{4,6},{5,7},{8,10},{9,11},{10,12},{11,13},... | collective-permute-start | bytes 786440 | tf_op jit(solution)/shard_map/ppermute | solution.py:38
  15.9 5.9 %collective-permute-done.8 = bf16[128,512]{1,0:T(8,128)(2,1)S(1)} collective-permute-done((bf16[128,512]{1,0:T(8,128)(2,1)S(1)}, bf16[128,512]{1,0:T(8,128)(2,1)S(1)}, u32[]{:S(2)}, u32[]{:S(2)}) %collective-permute-start.8) | collective-permute-done | bytes 131104 | tf_op jit(solution)/shard_map/ppermute | solution.py:49
  21.9 2.5 %collective-permute-start.2 = (bf16[256,512]{1,0:T(8,128)(2,1)S(1)}, bf16[256,512]{1,0:T(8,128)(2,1)S(1)}, u32[]{:S(2)}, u32[]{:S(2)}) collective-permute-start(bf16[256,512]{1,0:T(8,128)(2,1)S(1)} %pad_maximum_fusion.refs_0_.refs_8_), channel_id=1, source_target_pairs={{0,2},{1,3},{2,4},{3,5},{4,6},{5,7},{8,10},{9,11},{10,12},{11,13},... | collective-permute-start | bytes 786440 | tf_op jit(solution)/shard_map/ppermute | solution.py:38
  24.4 1.3 collective-permute-start.14
  25.7 1.3 collective-permute-start.12
  27.0 8.2 %collective-permute-start.10 = (bf16[256,512]{1,0:T(8,128)(2,1)S(1)}, bf16[256,512]{1,0:T(8,128)(2,1)S(1)}, u32[]{:S(2)}, u32[]{:S(2)}) collective-permute-start(bf16[256,512]{1,0:T(8,128)(2,1)S(1)} %pad_maximum_fusion.1.refs_0_.refs_8_), channel_id=1, source_target_pairs={{0,2},{1,3},{2,4},{3,5},{4,6},{5,7},{8,10},{9,11},{10,12},{11,13},... | collective-permute-start | bytes 786440 | tf_op jit(solution)/shard_map/ppermute | solution.py:38
  35.3 0.1 collective-permute-start.22
  35.4 0.5 collective-permute-start.20
  35.9 1.8 %collective-permute-done.14.refs_6_.refs_14_ = bf16[256,512]{1,0:T(8,128)(2,1)S(1)} collective-permute-done((bf16[256,512]{1,0:T(8,128)(2,1)S(1)}, bf16[256,512]{1,0:T(8,128)(2,1)S(1)}, u32[]{:S(2)}, u32[]{:S(2)}) %collective-permute-start.14) | collective-permute-done | bytes 262176 | tf_op jit(solution)/shard_map/ppermute | solution.py:38
  37.7 5.6 %collective-permute-done.12.refs_4_.refs_12_ = bf16[256,512]{1,0:T(8,128)(2,1)S(1)} collective-permute-done((bf16[256,512]{1,0:T(8,128)(2,1)S(1)}, bf16[256,512]{1,0:T(8,128)(2,1)S(1)}, u32[]{:S(2)}, u32[]{:S(2)}) %collective-permute-start.12) | collective-permute-done | bytes 262176 | tf_op jit(solution)/shard_map/ppermute | solution.py:38
  43.3 1.4 collective-permute-start.4
  44.7 0.6 pad_add_fusion.info
  45.3 2.9 %collective-permute-done.10.refs_2_.refs_10_ = bf16[256,512]{1,0:T(8,128)(2,1)S(1)} collective-permute-done((bf16[256,512]{1,0:T(8,128)(2,1)S(1)}, bf16[256,512]{1,0:T(8,128)(2,1)S(1)}, u32[]{:S(2)}, u32[]{:S(2)}) %collective-permute-start.10) | collective-permute-done | bytes 262176 | tf_op jit(solution)/shard_map/ppermute | solution.py:38
  48.2 0.5 collective-permute-start.15
  48.7 0.1 collective-permute-start.13
  48.8 0.4 collective-permute-start.11
  49.2 1.4 collective-permute-start.6
  50.6 13.6 %teacher.3.target_ref = bf16[512,256]{1,0:T(8,128)(2,1)} custom-call(s32[3]{0:T(128)} %pad_add_fusion.info, bf16[256,4096]{1,0:T(8,128)(2,1)} %bitcast.88, bf16[256,512]{1,0:T(8,128)(2,1)} %copy-done.4, bf16[256,512]{1,0:T(8,128)(2,1)} %copy-done.18, bf16[256,512]{1,0:T(8,128)(2,1)} %copy-done.17, bf16[256,512]{1,0:T(8,128)(2,1)} %collective-permute-done.18.refs_3_.refs_11_, ...), custom_call_target="tpu_custom_call" | custom-call | flops 4294967296 | bytes 1048576 | tf_op jit(solution)/shard_map/teacher/pallas_call | solution.py:196
  64.2 0.1 collective-permute-start.1
  64.4 0.5 collective-permute-start.3
  64.9 0.1 collective-permute-start.5
  65.0 0.4 collective-permute-start.7
  65.4 0.2 copy-done.21
  65.6 11.4 %student.3 = (f32[128,512]{1,0:T(8,128)}, bf16[128,512]{1,0:T(8,128)(2,1)}, f32[1,256]{1,0:T(1,128)}, f32[4,256,256]{2,1,0:T(8,128)}, bf16[4,256,256]{2,1,0:T(8,128)(2,1)}) custom-call(s32[3]{0:T(128)} %pad_add_fusion.info, bf16[128,2048]{1,0:T(8,128)(2,1)} %bitcast.86, bf16[128,1024]{1,0:T(8,128)(2,1)} %copy-done.10, bf16[512,256]{1,0:T(8,128)(2,1)} %teacher.3.target_ref, ...), custom_call_target="tpu_custom_call" | custom-call | flops 3221225472 | bytes 2097152 | tf_op jit(solution)/shard_map/student/pallas_call | solution.py:349
  77.0 1.5 collective-permute-start.24
  78.5 0.6 copy-done.22
  79.1 0.1 copy-done.23
  79.2 0.1 copy-done.24
  79.3 0.7 copy-done.25
  80.0 13.8 %teacher.2.target_ref = bf16[512,256]{1,0:T(8,128)(2,1)} custom-call(s32[3]{0:T(128)} %pad_add_fusion.info, bf16[256,4096]{1,0:T(8,128)(2,1)} %bitcast.89, bf16[256,512]{1,0:T(8,128)(2,1)} %copy-done.6, bf16[256,512]{1,0:T(8,128)(2,1)} %copy-done.22, bf16[256,512]{1,0:T(8,128)(2,1)} %copy-done.15, bf16[256,512]{1,0:T(8,128)(2,1)} %copy-done.23, ...), custom_call_target="tpu_custom_call" | custom-call | flops 4294967296 | bytes 1048576 | tf_op jit(solution)/shard_map/teacher/pallas_call | solution.py:196
  93.8 11.3 %student.2 = (f32[128,512]{1,0:T(8,128)}, bf16[128,512]{1,0:T(8,128)(2,1)}, f32[1,256]{1,0:T(1,128)}, f32[4,256,256]{2,1,0:T(8,128)}, bf16[4,256,256]{2,1,0:T(8,128)(2,1)}) custom-call(s32[3]{0:T(128)} %pad_add_fusion.info, bf16[128,2048]{1,0:T(8,128)(2,1)} %bitcast.87, bf16[128,1024]{1,0:T(8,128)(2,1)} %copy-done.10, bf16[512,256]{1,0:T(8,128)(2,1)} %teacher.2.target_ref, ...), custom_call_target="tpu_custom_call" | custom-call | flops 3221225472 | bytes 2097152 | tf_op jit(solution)/shard_map/student/pallas_call | solution.py:349
  105.2 0.7 add.63
  105.9 0.5 collective-permute-start.35
  106.4 1.5 collective-permute-start.23
  108.0 1.4 collective-permute-done.35
  109.4 0.5 fusion.10
  110.0 0.2 fusion.12
  110.2 1.4 collective-permute-start.30
  111.6 1.3 collective-permute-start.32
  112.9 1.3 collective-permute-start.31
  114.3 1.1 maximum_select_fusion
  115.4 17.1 %collective-permute-done.30 = bf16[256,256]{1,0:T(8,128)(2,1)S(1)} collective-permute-done((bf16[256,256]{1,0:T(8,128)(2,1)S(1)}, bf16[256,256]{1,0:T(8,128)(2,1)S(1)}, u32[]{:S(2)}, u32[]{:S(2)}) %collective-permute-start.30) | collective-permute-done | bytes 131104 | tf_op jit(solution)/shard_map/ppermute | solution.py:44
  132.5 15.5 %collective-permute-done.32 = bf16[256,256]{1,0:T(8,128)(2,1)S(1)} collective-permute-done((bf16[256,256]{1,0:T(8,128)(2,1)S(1)}, bf16[256,256]{1,0:T(8,128)(2,1)S(1)}, u32[]{:S(2)}, u32[]{:S(2)}) %collective-permute-start.32) | collective-permute-done | bytes 131104 | tf_op jit(solution)/shard_map/ppermute | solution.py:44
  148.0 0.1 fusion.2
  148.1 0.6 collective-permute-start.34
  148.7 3.7 %collective-permute-done.34 = bf16[128,256]{1,0:T(8,128)(2,1)S(1)} collective-permute-done((bf16[128,256]{1,0:T(8,128)(2,1)S(1)}, bf16[128,256]{1,0:T(8,128)(2,1)S(1)}, u32[]{:S(2)}, u32[]{:S(2)}) %collective-permute-start.34) | collective-permute-done | bytes 65568 | tf_op jit(solution)/shard_map/ppermute | solution.py:49
  152.4 0.2 fusion.11
  152.6 1.3 collective-permute-start.26
  153.9 1.3 collective-permute-start.28
  155.2 1.3 collective-permute-start.27
  156.5 4.0 %collective-permute-done.26 = bf16[256,256]{1,0:T(8,128)(2,1)S(1)} collective-permute-done((bf16[256,256]{1,0:T(8,128)(2,1)S(1)}, bf16[256,256]{1,0:T(8,128)(2,1)S(1)}, u32[]{:S(2)}, u32[]{:S(2)}) %collective-permute-start.26) | collective-permute-done | bytes 131104 | tf_op jit(solution)/shard_map/ppermute | solution.py:44
  160.5 2.1 %collective-permute-done.28 = bf16[256,256]{1,0:T(8,128)(2,1)S(1)} collective-permute-done((bf16[256,256]{1,0:T(8,128)(2,1)S(1)}, bf16[256,256]{1,0:T(8,128)(2,1)S(1)}, u32[]{:S(2)}, u32[]{:S(2)}) %collective-permute-start.28) | collective-permute-done | bytes 131104 | tf_op jit(solution)/shard_map/ppermute | solution.py:44
  162.6 4.4 %collective-permute-done.27 = bf16[256,256]{1,0:T(8,128)(2,1)S(1)} collective-permute-done((bf16[256,256]{1,0:T(8,128)(2,1)S(1)}, bf16[256,256]{1,0:T(8,128)(2,1)S(1)}, u32[]{:S(2)}, u32[]{:S(2)}) %collective-permute-start.27) | collective-permute-done | bytes 131104 | tf_op jit(solution)/shard_map/ppermute | solution.py:44
  167.0 0.1 fusion.5
  167.1 0.6 collective-permute-start.33
  167.7 3.7 %collective-permute-done.33 = bf16[128,256]{1,0:T(8,128)(2,1)S(1)} collective-permute-done((bf16[128,256]{1,0:T(8,128)(2,1)S(1)}, bf16[128,256]{1,0:T(8,128)(2,1)S(1)}, u32[]{:S(2)}, u32[]{:S(2)}) %collective-permute-start.33) | collective-permute-done | bytes 65568 | tf_op jit(solution)/shard_map/ppermute | solution.py:49
  171.4 0.7 maximum_select_fusion.2
  172.2 0.7 maximum_select_fusion.1
  (94 shorter events, 0.4 us)
Async XLA Ops:
  0.6 12.1 %copy-start.7 = (bf16[1,128,512]{2,1,0:T(8,128)(2,1)S(1)}, bf16[1,128,512]{2,1,0:T(8,128)(2,1)}, u32[]{:S(2)}) copy-start(bf16[1,128,512]{2,1,0:T(8,128)(2,1)} %param.13) | copy-start | bytes 393220
  0.6 12.1 %copy-start.8 = (bf16[1,128,512]{2,1,0:T(8,128)(2,1)S(1)}, bf16[1,128,512]{2,1,0:T(8,128)(2,1)}, u32[]{:S(2)}) copy-start(bf16[1,128,512]{2,1,0:T(8,128)(2,1)} %param.12) | copy-start | bytes 393220
  1.9 48.7 %copy-start.4 = (bf16[256,512]{1,0:T(8,128)(2,1)}, bf16[256,512]{1,0:T(8,128)(2,1)S(1)}, u32[]{:S(2)}) copy-start(bf16[256,512]{1,0:T(8,128)(2,1)S(1)} %pad_maximum_fusion.2.refs_0_.refs_8_) | copy-start | bytes 786436
  1.9 22.5 %collective-permute-start.21 = (bf16[256,512]{1,0:T(8,128)(2,1)S(1)}, bf16[256,512]{1,0:T(8,128)(2,1)S(1)}, u32[]{:S(2)}, u32[]{:S(2)}) collective-permute-start(bf16[256,512]{1,0:T(8,128)(2,1)S(1)} %pad_maximum_fusion.2.refs_0_.refs_8_), channel_id=1, source_target_pairs={{0,6},{1,7},{8,14},{9,15},{16,22},{17,23},{24,30},{25,31}} | collective-permute-start | bytes 786440 | tf_op jit(solution)/shard_map/ppermute | solution.py:38
  8.9 16.8 %collective-permute-start.19 = (bf16[256,512]{1,0:T(8,128)(2,1)S(1)}, bf16[256,512]{1,0:T(8,128)(2,1)S(1)}, u32[]{:S(2)}, u32[]{:S(2)}) collective-permute-start(bf16[256,512]{1,0:T(8,128)(2,1)S(1)} %pad_maximum_fusion.2.refs_0_.refs_8_), channel_id=1, source_target_pairs={{0,4},{1,5},{2,6},{3,7},{8,12},{9,13},{10,14},{11,15},{16,20},{17,... | collective-permute-start | bytes 786440 | tf_op jit(solution)/shard_map/ppermute | solution.py:38
  11.2 10.7 %collective-permute-start = (bf16[128,1024]{1,0:T(8,128)(2,1)S(1)}, bf16[128,1024]{1,0:T(8,128)(2,1)S(1)}, u32[]{:S(2)}, u32[]{:S(2)}) collective-permute-start(bf16[128,1024]{1,0:T(8,128)(2,1)S(1)} %dynamic-slice_bitcast_fusion), channel_id=1, source_target_pairs={{0,8},{8,0},{16,24},{24,16},{1,9},{9,1},{17,25},{25,17},{2,10},{10... | collective-permute-start | bytes 786440 | tf_op jit(solution)/shard_map/ppermute | solution.py:49
  12.8 9.0 %collective-permute-start.8 = (bf16[128,512]{1,0:T(8,128)(2,1)S(1)}, bf16[128,512]{1,0:T(8,128)(2,1)S(1)}, u32[]{:S(2)}, u32[]{:S(2)}) collective-permute-start(bf16[128,512]{1,0:T(8,128)(2,1)S(1)} %pad_maximum_fusion.3), channel_id=1, source_target_pairs={{0,8},{8,0},{16,24},{24,16},{1,9},{9,1},{17,25},{25,17},{2,10},{10... | collective-permute-start | bytes 393224 | tf_op jit(solution)/shard_map/ppermute | solution.py:49
  13.4 13.6 %collective-permute-start.17 = (bf16[256,512]{1,0:T(8,128)(2,1)S(1)}, bf16[256,512]{1,0:T(8,128)(2,1)S(1)}, u32[]{:S(2)}, u32[]{:S(2)}) collective-permute-start(bf16[256,512]{1,0:T(8,128)(2,1)S(1)} %pad_maximum_fusion.2.refs_0_.refs_8_), channel_id=1, source_target_pairs={{0,2},{1,3},{2,4},{3,5},{4,6},{5,7},{8,10},{9,11},{10,12},{11,13},... | collective-permute-start | bytes 786440 | tf_op jit(solution)/shard_map/ppermute | solution.py:38
  15.9 48.3 %copy-start.6 = (bf16[256,512]{1,0:T(8,128)(2,1)}, bf16[256,512]{1,0:T(8,128)(2,1)S(1)}, u32[]{:S(2)}) copy-start(bf16[256,512]{1,0:T(8,128)(2,1)S(1)} %pad_maximum_fusion.refs_0_.refs_8_) | copy-start | bytes 786436
  21.8 13.5 %collective-permute-start.16 = (bf16[256,512]{1,0:T(8,128)(2,1)S(1)}, bf16[256,512]{1,0:T(8,128)(2,1)S(1)}, u32[]{:S(2)}, u32[]{:S(2)}) collective-permute-start(bf16[256,512]{1,0:T(8,128)(2,1)S(1)} %pad_maximum_fusion.2.refs_0_.refs_8_), channel_id=1, source_target_pairs={{0,1},{1,0},{2,3},{3,2},{4,5},{5,4},{6,7},{7,6},{8,9},{9,8},{10,11... | collective-permute-start | bytes 786440 | tf_op jit(solution)/shard_map/ppermute | solution.py:49
  21.8 42.3 %copy-start.5 = (bf16[256,512]{1,0:T(8,128)(2,1)}, bf16[256,512]{1,0:T(8,128)(2,1)S(1)}, u32[]{:S(2)}) copy-start(bf16[256,512]{1,0:T(8,128)(2,1)S(1)} %pad_maximum_fusion.1.refs_0_.refs_8_) | copy-start | bytes 786436
  21.9 42.3 %copy-start.10 = (bf16[128,1024]{1,0:T(8,128)(2,1)}, bf16[128,1024]{1,0:T(8,128)(2,1)S(1)}, u32[]{:S(2)}) copy-start(bf16[128,1024]{1,0:T(8,128)(2,1)S(1)} %collective-permute-done.far_q_ref) | copy-start | bytes 786436
  21.9 13.5 %collective-permute-start.2 = (bf16[256,512]{1,0:T(8,128)(2,1)S(1)}, bf16[256,512]{1,0:T(8,128)(2,1)S(1)}, u32[]{:S(2)}, u32[]{:S(2)}) collective-permute-start(bf16[256,512]{1,0:T(8,128)(2,1)S(1)} %pad_maximum_fusion.refs_0_.refs_8_), channel_id=1, source_target_pairs={{0,2},{1,3},{2,4},{3,5},{4,6},{5,7},{8,10},{9,11},{10,12},{11,13},... | collective-permute-start | bytes 786440 | tf_op jit(solution)/shard_map/ppermute | solution.py:38
  24.4 26.2 %copy-start.11 = (bf16[256,512]{1,0:T(8,128)(2,1)}, bf16[256,512]{1,0:T(8,128)(2,1)S(1)}, u32[]{:S(2)}) copy-start(bf16[256,512]{1,0:T(8,128)(2,1)S(1)} %collective-permute-done.21.refs_6_.refs_14_) | copy-start | bytes 786436
  24.4 13.3 %collective-permute-start.14 = (bf16[256,512]{1,0:T(8,128)(2,1)S(1)}, bf16[256,512]{1,0:T(8,128)(2,1)S(1)}, u32[]{:S(2)}, u32[]{:S(2)}) collective-permute-start(bf16[256,512]{1,0:T(8,128)(2,1)S(1)} %pad_maximum_fusion.1.refs_0_.refs_8_), channel_id=1, source_target_pairs={{0,6},{1,7},{8,14},{9,15},{16,22},{17,23},{24,30},{25,31}} | collective-permute-start | bytes 786440 | tf_op jit(solution)/shard_map/ppermute | solution.py:38
  25.7 24.9 %copy-start.12 = (bf16[256,512]{1,0:T(8,128)(2,1)}, bf16[256,512]{1,0:T(8,128)(2,1)S(1)}, u32[]{:S(2)}) copy-start(bf16[256,512]{1,0:T(8,128)(2,1)S(1)} %collective-permute-done.19.refs_4_.refs_12_) | copy-start | bytes 786436
  25.7 17.6 %collective-permute-start.12 = (bf16[256,512]{1,0:T(8,128)(2,1)S(1)}, bf16[256,512]{1,0:T(8,128)(2,1)S(1)}, u32[]{:S(2)}, u32[]{:S(2)}) collective-permute-start(bf16[256,512]{1,0:T(8,128)(2,1)S(1)} %pad_maximum_fusion.1.refs_0_.refs_8_), channel_id=1, source_target_pairs={{0,4},{1,5},{2,6},{3,7},{8,12},{9,13},{10,14},{11,15},{16,20},{17,... | collective-permute-start | bytes 786440 | tf_op jit(solution)/shard_map/ppermute | solution.py:38
  27.0 23.6 %copy-start.17 = (bf16[256,512]{1,0:T(8,128)(2,1)}, bf16[256,512]{1,0:T(8,128)(2,1)S(1)}, u32[]{:S(2)}) copy-start(bf16[256,512]{1,0:T(8,128)(2,1)S(1)} %collective-permute-done.17.refs_2_.refs_10_) | copy-start | bytes 786436
  27.0 21.1 %collective-permute-start.10 = (bf16[256,512]{1,0:T(8,128)(2,1)S(1)}, bf16[256,512]{1,0:T(8,128)(2,1)S(1)}, u32[]{:S(2)}, u32[]{:S(2)}) collective-permute-start(bf16[256,512]{1,0:T(8,128)(2,1)S(1)} %pad_maximum_fusion.1.refs_0_.refs_8_), channel_id=1, source_target_pairs={{0,2},{1,3},{2,4},{3,5},{4,6},{5,7},{8,10},{9,11},{10,12},{11,13},... | collective-permute-start | bytes 786440 | tf_op jit(solution)/shard_map/ppermute | solution.py:38
  35.3 8.0 %copy-start.18 = (bf16[256,512]{1,0:T(8,128)(2,1)}, bf16[256,512]{1,0:T(8,128)(2,1)S(1)}, u32[]{:S(2)}) copy-start(bf16[256,512]{1,0:T(8,128)(2,1)S(1)} %collective-permute-done.16.refs_1_.refs_9_) | copy-start | bytes 786436
  35.3 12.9 %collective-permute-start.22 = (bf16[256,512]{1,0:T(8,128)(2,1)S(1)}, bf16[256,512]{1,0:T(8,128)(2,1)}, u32[]{:S(2)}, u32[]{:S(2)}) collective-permute-start(bf16[256,512]{1,0:T(8,128)(2,1)S(1)} %collective-permute-done.21.refs_6_.refs_14_), channel_id=1, source_target_pairs={{0,1},{1,0},{2,3},{3,2},{4,5},{5,4},{6,7},{7,6},{8,9},{9,8},{10,11... | collective-permute-start | bytes 786440 | tf_op jit(solution)/shard_map/ppermute | solution.py:49
  35.4 29.0 %copy-start.15 = (bf16[256,512]{1,0:T(8,128)(2,1)}, bf16[256,512]{1,0:T(8,128)(2,1)S(1)}, u32[]{:S(2)}) copy-start(bf16[256,512]{1,0:T(8,128)(2,1)S(1)} %collective-permute-done.2.refs_2_.refs_10_) | copy-start | bytes 786436
  35.4 13.3 %collective-permute-start.20 = (bf16[256,512]{1,0:T(8,128)(2,1)S(1)}, bf16[256,512]{1,0:T(8,128)(2,1)}, u32[]{:S(2)}, u32[]{:S(2)}) collective-permute-start(bf16[256,512]{1,0:T(8,128)(2,1)S(1)} %collective-permute-done.19.refs_4_.refs_12_), channel_id=1, source_target_pairs={{0,1},{1,0},{2,3},{3,2},{4,5},{5,4},{6,7},{7,6},{8,9},{9,8},{10,11... | collective-permute-start | bytes 786440 | tf_op jit(solution)/shard_map/ppermute | solution.py:49
  37.7 26.5 %copy-start.13 = (bf16[256,512]{1,0:T(8,128)(2,1)}, bf16[256,512]{1,0:T(8,128)(2,1)S(1)}, u32[]{:S(2)}) copy-start(bf16[256,512]{1,0:T(8,128)(2,1)S(1)} %collective-permute-done.14.refs_6_.refs_14_) | copy-start | bytes 786436
  37.7 11.1 %collective-permute-start.18 = (bf16[256,512]{1,0:T(8,128)(2,1)S(1)}, bf16[256,512]{1,0:T(8,128)(2,1)}, u32[]{:S(2)}, u32[]{:S(2)}) collective-permute-start(bf16[256,512]{1,0:T(8,128)(2,1)S(1)} %collective-permute-done.17.refs_2_.refs_10_), channel_id=1, source_target_pairs={{0,1},{1,0},{2,3},{3,2},{4,5},{5,4},{6,7},{7,6},{8,9},{9,8},{10,11... | collective-permute-start | bytes 786440 | tf_op jit(solution)/shard_map/ppermute | solution.py:49
  43.3 20.9 %copy-start.14 = (bf16[256,512]{1,0:T(8,128)(2,1)}, bf16[256,512]{1,0:T(8,128)(2,1)S(1)}, u32[]{:S(2)}) copy-start(bf16[256,512]{1,0:T(8,128)(2,1)S(1)} %collective-permute-done.12.refs_4_.refs_12_) | copy-start | bytes 786436
  43.3 5.9 %collective-permute-start.4 = (bf16[256,512]{1,0:T(8,128)(2,1)S(1)}, bf16[256,512]{1,0:T(8,128)(2,1)}, u32[]{:S(2)}, u32[]{:S(2)}) collective-permute-start(bf16[256,512]{1,0:T(8,128)(2,1)S(1)} %collective-permute-done.2.refs_2_.refs_10_), channel_id=1, source_target_pairs={{2,4},{3,5},{4,6},{5,7},{10,12},{11,13},{12,14},{13,15},{18,20},{1... | collective-permute-start | bytes 786440 | tf_op jit(solution)/shard_map/ppermute | solution.py:38
  48.2 16.0 %copy-start.16 = (bf16[256,512]{1,0:T(8,128)(2,1)}, bf16[256,512]{1,0:T(8,128)(2,1)S(1)}, u32[]{:S(2)}) copy-start(bf16[256,512]{1,0:T(8,128)(2,1)S(1)} %collective-permute-done.10.refs_2_.refs_10_) | copy-start | bytes 786436
  48.2 16.0 %collective-permute-start.9 = (bf16[256,512]{1,0:T(8,128)(2,1)S(1)}, bf16[256,512]{1,0:T(8,128)(2,1)S(1)}, u32[]{:S(2)}, u32[]{:S(2)}) collective-permute-start(bf16[256,512]{1,0:T(8,128)(2,1)S(1)} %pad_maximum_fusion.1.refs_0_.refs_8_), channel_id=1, source_target_pairs={{0,1},{1,0},{2,3},{3,2},{4,5},{5,4},{6,7},{7,6},{8,9},{9,8},{10,11... | collective-permute-start | bytes 786440 | tf_op jit(solution)/shard_map/ppermute | solution.py:49
  48.2 16.2 %collective-permute-start.15 = (bf16[256,512]{1,0:T(8,128)(2,1)S(1)}, bf16[256,512]{1,0:T(8,128)(2,1)S(1)}, u32[]{:S(2)}, u32[]{:S(2)}) collective-permute-start(bf16[256,512]{1,0:T(8,128)(2,1)S(1)} %collective-permute-done.14.refs_6_.refs_14_), channel_id=1, source_target_pairs={{0,1},{1,0},{2,3},{3,2},{4,5},{5,4},{6,7},{7,6},{8,9},{9,8},{10,11... | collective-permute-start | bytes 786440 | tf_op jit(solution)/shard_map/ppermute | solution.py:49
  48.7 16.2 %collective-permute-start.13 = (bf16[256,512]{1,0:T(8,128)(2,1)S(1)}, bf16[256,512]{1,0:T(8,128)(2,1)S(1)}, u32[]{:S(2)}, u32[]{:S(2)}) collective-permute-start(bf16[256,512]{1,0:T(8,128)(2,1)S(1)} %collective-permute-done.12.refs_4_.refs_12_), channel_id=1, source_target_pairs={{0,1},{1,0},{2,3},{3,2},{4,5},{5,4},{6,7},{7,6},{8,9},{9,8},{10,11... | collective-permute-start | bytes 786440 | tf_op jit(solution)/shard_map/ppermute | solution.py:49
  48.8 16.6 %collective-permute-start.11 = (bf16[256,512]{1,0:T(8,128)(2,1)S(1)}, bf16[256,512]{1,0:T(8,128)(2,1)}, u32[]{:S(2)}, u32[]{:S(2)}) collective-permute-start(bf16[256,512]{1,0:T(8,128)(2,1)S(1)} %collective-permute-done.10.refs_2_.refs_10_), channel_id=1, source_target_pairs={{0,1},{1,0},{2,3},{3,2},{4,5},{5,4},{6,7},{7,6},{8,9},{9,8},{10,11... | collective-permute-start | bytes 786440 | tf_op jit(solution)/shard_map/ppermute | solution.py:49
  49.2 15.7 %collective-permute-start.6 = (bf16[256,512]{1,0:T(8,128)(2,1)}, bf16[256,512]{1,0:T(8,128)(2,1)}, u32[]{:S(2)}, u32[]{:S(2)}) collective-permute-start(bf16[256,512]{1,0:T(8,128)(2,1)} %collective-permute-done.4.refs_4_.refs_12_), channel_id=1, source_target_pairs={{4,6},{5,7},{12,14},{13,15},{20,22},{21,23},{28,30},{29,31}} | collective-permute-start | bytes 786440 | tf_op jit(solution)/shard_map/ppermute | solution.py:38
  64.2 1.2 copy-start.19
  64.2 14.2 %collective-permute-start.1 = (bf16[256,512]{1,0:T(8,128)(2,1)S(1)}, bf16[256,512]{1,0:T(8,128)(2,1)S(1)}, u32[]{:S(2)}, u32[]{:S(2)}) collective-permute-start(bf16[256,512]{1,0:T(8,128)(2,1)S(1)} %pad_maximum_fusion.refs_0_.refs_8_), channel_id=1, source_target_pairs={{0,1},{1,0},{2,3},{3,2},{4,5},{5,4},{6,7},{7,6},{8,9},{9,8},{10,11... | collective-permute-start | bytes 786440 | tf_op jit(solution)/shard_map/ppermute | solution.py:49
  64.4 1.0 copy-start.20
  64.4 14.1 %collective-permute-start.3 = (bf16[256,512]{1,0:T(8,128)(2,1)S(1)}, bf16[256,512]{1,0:T(8,128)(2,1)S(1)}, u32[]{:S(2)}, u32[]{:S(2)}) collective-permute-start(bf16[256,512]{1,0:T(8,128)(2,1)S(1)} %collective-permute-done.2.refs_2_.refs_10_), channel_id=1, source_target_pairs={{0,1},{1,0},{2,3},{3,2},{4,5},{5,4},{6,7},{7,6},{8,9},{9,8},{10,11... | collective-permute-start | bytes 786440 | tf_op jit(solution)/shard_map/ppermute | solution.py:49
  64.9 0.7 copy-start.21
  64.9 13.6 %collective-permute-start.5 = (bf16[256,512]{1,0:T(8,128)(2,1)}, bf16[256,512]{1,0:T(8,128)(2,1)S(1)}, u32[]{:S(2)}, u32[]{:S(2)}) collective-permute-start(bf16[256,512]{1,0:T(8,128)(2,1)} %collective-permute-done.4.refs_4_.refs_12_), channel_id=1, source_target_pairs={{0,1},{1,0},{2,3},{3,2},{4,5},{5,4},{6,7},{7,6},{8,9},{9,8},{10,11... | collective-permute-start | bytes 786440 | tf_op jit(solution)/shard_map/ppermute | solution.py:49
  65.0 13.5 %collective-permute-start.7 = (bf16[256,512]{1,0:T(8,128)(2,1)}, bf16[256,512]{1,0:T(8,128)(2,1)S(1)}, u32[]{:S(2)}, u32[]{:S(2)}) collective-permute-start(bf16[256,512]{1,0:T(8,128)(2,1)} %collective-permute-done.6.refs_6_.refs_14_), channel_id=1, source_target_pairs={{0,1},{1,0},{2,3},{3,2},{4,5},{5,4},{6,7},{7,6},{8,9},{9,8},{10,11... | collective-permute-start | bytes 786440 | tf_op jit(solution)/shard_map/ppermute | solution.py:49
  77.0 29.4 %collective-permute-start.24 = (bf16[128,512]{1,0:T(8,128)(2,1)}, bf16[128,512]{1,0:T(8,128)(2,1)S(1)}, u32[]{:S(2)}, u32[]{:S(2)}) collective-permute-start(bf16[128,512]{1,0:T(8,128)(2,1)} %get-tuple-element.17), channel_id=1, source_target_pairs={{0,8},{8,0},{16,24},{24,16},{1,9},{9,1},{17,25},{25,17},{2,10},{10... | collective-permute-start | bytes 393224 | tf_op jit(solution)/shard_map/ppermute | solution.py:49
  78.5 0.7 copy-start.22
  78.5 31.5 %collective-permute-start.29 = (bf16[4,256,256]{2,1,0:T(8,128)(2,1)}, bf16[4,256,256]{2,1,0:T(8,128)(2,1)S(1)}, u32[]{:S(2)}, u32[]{:S(2)}) collective-permute-start(bf16[4,256,256]{2,1,0:T(8,128)(2,1)} %get-tuple-element.21), channel_id=1, source_target_pairs={{0,1},{1,0},{2,3},{3,2},{4,5},{5,4},{6,7},{7,6},{8,9},{9,8},{10,11... | collective-permute-start | bytes 1572872 | tf_op jit(solution)/shard_map/ppermute | solution.py:49
  78.5 0.8 copy-start.23
  78.5 0.8 copy-start.24
  79.3 0.7 copy-start.25
  93.8 11.4 %copy-start.9 = (f32[1,256]{1,0:T(1,128)S(1)}, f32[1,256]{1,0:T(1,128)}, u32[]{:S(2)}) copy-start(f32[1,256]{1,0:T(1,128)} %get-tuple-element.23) | copy-start | bytes 3076
  93.8 16.1 %copy-start.1 = (f32[4,256,256]{2,1,0:T(8,128)S(1)}, f32[4,256,256]{2,1,0:T(8,128)}, u32[]{:S(2)}) copy-start(f32[4,256,256]{2,1,0:T(8,128)} %get-tuple-element.20) | copy-start | bytes 3145732
  105.9 3.6 %collective-permute-start.35 = (f32[128]{0:T(128)S(1)}, f32[128]{0:T(128)S(1)}, u32[]{:S(2)}, u32[]{:S(2)}) collective-permute-start(f32[128]{0:T(128)S(1)} %fusion.9), channel_id=1, source_target_pairs={{0,8},{8,0},{16,24},{24,16},{1,9},{9,1},{17,25},{25,17},{2,10},{10... | collective-permute-start | bytes 1544 | tf_op jit(solution)/shard_map/ppermute | solution.py:49
  106.4 7.8 %collective-permute-start.23 = (bf16[128,512]{1,0:T(8,128)(2,1)}, bf16[128,512]{1,0:T(8,128)(2,1)S(1)}, u32[]{:S(2)}, u32[]{:S(2)}) collective-permute-start(bf16[128,512]{1,0:T(8,128)(2,1)} %get-tuple-element.16), channel_id=1, source_target_pairs={{0,8},{8,0},{16,24},{24,16},{1,9},{9,1},{17,25},{25,17},{2,10},{10... | collective-permute-start | bytes 393224 | tf_op jit(solution)/shard_map/ppermute | solution.py:49
  108.0 44.4 %collective-permute-start.25 = (bf16[4,256,256]{2,1,0:T(8,128)(2,1)}, bf16[4,256,256]{2,1,0:T(8,128)(2,1)S(1)}, u32[]{:S(2)}, u32[]{:S(2)}) collective-permute-start(bf16[4,256,256]{2,1,0:T(8,128)(2,1)} %get-tuple-element.19), channel_id=1, source_target_pairs={{0,1},{1,0},{2,3},{3,2},{4,5},{5,4},{6,7},{7,6},{8,9},{9,8},{10,11... | collective-permute-start | bytes 1572872 | tf_op jit(solution)/shard_map/ppermute | solution.py:49
  109.9 4.3 %copy-start.2 = (f32[128,512]{1,0:T(8,128)S(1)}, f32[128,512]{1,0:T(8,128)}, u32[]{:S(2)}) copy-start(f32[128,512]{1,0:T(8,128)} %get-tuple-element.15) | copy-start | bytes 786436
  110.0 4.3 %copy-start.3 = (f32[128,512]{1,0:T(8,128)S(1)}, f32[128,512]{1,0:T(8,128)}, u32[]{:S(2)}) copy-start(f32[128,512]{1,0:T(8,128)} %get-tuple-element.14) | copy-start | bytes 786436
  110.2 42.3 %copy-start = (f32[4,256,256]{2,1,0:T(8,128)S(1)}, f32[4,256,256]{2,1,0:T(8,128)}, u32[]{:S(2)}) copy-start(f32[4,256,256]{2,1,0:T(8,128)} %get-tuple-element.18) | copy-start | bytes 3145732
  110.2 22.3 %collective-permute-start.30 = (bf16[256,256]{1,0:T(8,128)(2,1)S(1)}, bf16[256,256]{1,0:T(8,128)(2,1)S(1)}, u32[]{:S(2)}, u32[]{:S(2)}) collective-permute-start(bf16[256,256]{1,0:T(8,128)(2,1)S(1)} %get-tuple-element.31), channel_id=1, source_target_pairs={{2,0},{3,1},{4,2},{5,3},{6,4},{7,5},{10,8},{11,9},{12,10},{13,11},... | collective-permute-start | bytes 393224 | tf_op jit(solution)/shard_map/ppermute | solution.py:44
  111.6 36.4 %collective-permute-start.32 = (bf16[256,256]{1,0:T(8,128)(2,1)S(1)}, bf16[256,256]{1,0:T(8,128)(2,1)S(1)}, u32[]{:S(2)}, u32[]{:S(2)}) collective-permute-start(bf16[256,256]{1,0:T(8,128)(2,1)S(1)} %get-tuple-element.32), channel_id=1, source_target_pairs={{6,0},{7,1},{14,8},{15,9},{22,16},{23,17},{30,24},{31,25}} | collective-permute-start | bytes 393224 | tf_op jit(solution)/shard_map/ppermute | solution.py:44
  112.9 35.1 %collective-permute-start.31 = (bf16[256,256]{1,0:T(8,128)(2,1)S(1)}, bf16[256,256]{1,0:T(8,128)(2,1)S(1)}, u32[]{:S(2)}, u32[]{:S(2)}) collective-permute-start(bf16[256,256]{1,0:T(8,128)(2,1)S(1)} %get-tuple-element.33), channel_id=1, source_target_pairs={{4,0},{5,1},{6,2},{7,3},{12,8},{13,9},{14,10},{15,11},{20,16},{21,... | collective-permute-start | bytes 393224 | tf_op jit(solution)/shard_map/ppermute | solution.py:44
  148.1 4.3 %collective-permute-start.34 = (bf16[128,256]{1,0:T(8,128)(2,1)S(1)}, bf16[128,256]{1,0:T(8,128)(2,1)S(1)}, u32[]{:S(2)}, u32[]{:S(2)}) collective-permute-start(bf16[128,256]{1,0:T(8,128)(2,1)S(1)} %slice.174), channel_id=1, source_target_pairs={{0,8},{8,0},{16,24},{24,16},{1,9},{9,1},{17,25},{25,17},{2,10},{10... | collective-permute-start | bytes 196616 | tf_op jit(solution)/shard_map/ppermute | solution.py:49
  152.6 7.9 %collective-permute-start.26 = (bf16[256,256]{1,0:T(8,128)(2,1)S(1)}, bf16[256,256]{1,0:T(8,128)(2,1)S(1)}, u32[]{:S(2)}, u32[]{:S(2)}) collective-permute-start(bf16[256,256]{1,0:T(8,128)(2,1)S(1)} %get-tuple-element.28), channel_id=1, source_target_pairs={{2,0},{3,1},{4,2},{5,3},{6,4},{7,5},{10,8},{11,9},{12,10},{13,11},... | collective-permute-start | bytes 393224 | tf_op jit(solution)/shard_map/ppermute | solution.py:44
  153.9 8.7 %collective-permute-start.28 = (bf16[256,256]{1,0:T(8,128)(2,1)S(1)}, bf16[256,256]{1,0:T(8,128)(2,1)S(1)}, u32[]{:S(2)}, u32[]{:S(2)}) collective-permute-start(bf16[256,256]{1,0:T(8,128)(2,1)S(1)} %get-tuple-element.29), channel_id=1, source_target_pairs={{6,0},{7,1},{14,8},{15,9},{22,16},{23,17},{30,24},{31,25}} | collective-permute-start | bytes 393224 | tf_op jit(solution)/shard_map/ppermute | solution.py:44
  155.2 11.8 %collective-permute-start.27 = (bf16[256,256]{1,0:T(8,128)(2,1)S(1)}, bf16[256,256]{1,0:T(8,128)(2,1)S(1)}, u32[]{:S(2)}, u32[]{:S(2)}) collective-permute-start(bf16[256,256]{1,0:T(8,128)(2,1)S(1)} %get-tuple-element.30), channel_id=1, source_target_pairs={{4,0},{5,1},{6,2},{7,3},{12,8},{13,9},{14,10},{15,11},{20,16},{21,... | collective-permute-start | bytes 393224 | tf_op jit(solution)/shard_map/ppermute | solution.py:44
  167.1 4.3 %collective-permute-start.33 = (bf16[128,256]{1,0:T(8,128)(2,1)S(1)}, bf16[128,256]{1,0:T(8,128)(2,1)S(1)}, u32[]{:S(2)}, u32[]{:S(2)}) collective-permute-start(bf16[128,256]{1,0:T(8,128)(2,1)S(1)} %slice.175), channel_id=1, source_target_pairs={{0,8},{8,0},{16,24},{24,16},{1,9},{9,1},{17,25},{25,17},{2,10},{10... | collective-permute-start | bytes 196616 | tf_op jit(solution)/shard_map/ppermute | solution.py:49

commit v4 on v3

--- a/solution.py
+++ b/solution.py
@@ -23,7 +23,6 @@
 exp2_scale = inverse_root * math.log2(math.e)
 vmem_limit = 60 * 1024 * 1024
 chunk = 64
-pace = 10000
 piece = 512
 
 
@@ -75,17 +74,17 @@
     return jnp.sum(tile.reshape(-1, 8, tile.shape[1]), axis=0)
 
 
-def paced(history, bound):
-    if len(history) <= pace:
+def paced(history, bound, pace):
+    if pace is None or len(history) <= pace:
         return bound
     return jnp.maximum(bound, floor_score - history[-pace])
 
 
-def weigh(scores, weights, start, size, peak, history, keep):
+def weigh(scores, weights, start, size, peak, history, keep, pace):
     row_sum = history[-1]
     for u in range(start, start + size, chunk):
         part = pl.ds(u, chunk)
-        gap = scores[part, :].reshape(-1, 8, peak.shape[1]) - paced(history, peak)
+        gap = scores[part, :].reshape(-1, 8, peak.shape[1]) - paced(history, peak, pace)
         weight = jnp.exp2(gap * exp2_scale).reshape(chunk, peak.shape[1])
         if keep:
             scores[part, :] = weight
@@ -155,7 +154,7 @@
                 peak = low
                 for b in range(count):
                     bound = held(b, top, -floor_score)
-                    weigh(scores[slot], weights[slot], b * wide, wide, bound, history, False)
+                    weigh(scores[slot], weights[slot], b * wide, wide, bound, history, False, None)
                     peak = score(b, later, 1 - slot, peak)
                 end = count * wide
                 mixed = dot(values_t[pair // pairs, :, :end], weights[slot][:end, :])
@@ -286,7 +285,7 @@
                 top = spread_max(peak)
                 for b in range(count):
                     bound = held(b, top, -floor_score)
-                    weigh(scores, weights, b * wide, wide, bound, history, True)
+                    weigh(scores, weights, b * wide, wide, bound, history, True, 2)
                 inverse = 1.0 / jnp.sum(history[-1], axis=0, keepdims=True)
                 made = dot(values_t[:, :end], weights[:end, :]) * inverse
                 start = pl.multiple_of(pair * 2 * HEAD, 2 * HEAD)

time: 173 us -> 172 us (level)
  transfers between devices with their start and end apart: 36 -> 36, of which waited for: 12 -> 12; matrix products, arithmetic and copies ran while one was open for 2% -> 3% of each run, Pallas kernels for 29% -> 29%
where the time goes in v4:
time: 172 us
  waiting for transfers between devices  68 us (40%)
  Pallas kernels  49 us (28%)
  starting transfers between devices  44.4 us (26%)
  other arithmetic  4.94 us (3%)
  local copies, waits for them, and re-layouts  4.08 us (2%)
    ppermute x6, waiting for transfers between devices, back(): return lax.ppermute(value, 'seq', pairs)  42.8 us
    pallas_call x2, Pallas kernels, teacher(): pl.pallas_call(functools.partial(teacher_kernel, chips, rows, heads), out...  27.3 us
    ppermute x9, starting transfers between devices, shift(): return lax.ppermute(value, 'seq', pairs)  26.8 us
    pallas_call x2, Pallas kernels, student(): pl.pallas_call(functools.partial(student_kernel, chips, rows), out_shape=...  21.7 us
    ppermute x21, waiting for transfers between devices, swap(): return lax.ppermute(value, axis, pairs)  14.8 us
    ppermute x9, waiting for transfers between devices, shift(): return lax.ppermute(value, 'seq', pairs)  10.3 us
    ppermute x21, starting transfers between devices, swap(): return lax.ppermute(value, axis, pairs)  9.74 us
    ppermute x6, starting transfers between devices, back(): return lax.ppermute(value, 'seq', pairs)  7.88 us
  transfers between devices with their start and end apart: 36, of which 12 were waited for; matrix products, arithmetic and copies ran while one was open for 3% of the time, Pallas kernels for 29%

profile of v4, /device:TPU:0, one launch (start us, length us, event | category | flops | bytes accessed | tf_op | source)
XLA Modules:
  0.0 171.6 jit_solution(2366865491434655768)
XLA Ops:
  0.7 1.2 fusion.13
  1.9 7.0 %collective-permute-start.21 = (bf16[256,512]{1,0:T(8,128)(2,1)S(1)}, bf16[256,512]{1,0:T(8,128)(2,1)S(1)}, u32[]{:S(2)}, u32[]{:S(2)}) collective-permute-start(bf16[256,512]{1,0:T(8,128)(2,1)S(1)} %pad_maximum_fusion.2.refs_0_.refs_8_), channel_id=1, source_target_pairs={{0,6},{1,7},{8,14},{9,15},{16,22},{17,23},{24,30},{25,31}} | collective-permute-start | bytes 786440 | tf_op jit(solution)/shard_map/ppermute | solution.py:37
  8.9 1.3 collective-permute-start.19
  10.2 1.0 dynamic-slice_bitcast_fusion
  11.2 1.6 collective-permute-start
  12.8 0.6 collective-permute-start.8
  13.4 2.5 %collective-permute-start.17 = (bf16[256,512]{1,0:T(8,128)(2,1)S(1)}, bf16[256,512]{1,0:T(8,128)(2,1)S(1)}, u32[]{:S(2)}, u32[]{:S(2)}) collective-permute-start(bf16[256,512]{1,0:T(8,128)(2,1)S(1)} %pad_maximum_fusion.2.refs_0_.refs_8_), channel_id=1, source_target_pairs={{0,2},{1,3},{2,4},{3,5},{4,6},{5,7},{8,10},{9,11},{10,12},{11,13},... | collective-permute-start | bytes 786440 | tf_op jit(solution)/shard_map/ppermute | solution.py:37
  15.9 5.9 %collective-permute-done.8 = bf16[128,512]{1,0:T(8,128)(2,1)S(1)} collective-permute-done((bf16[128,512]{1,0:T(8,128)(2,1)S(1)}, bf16[128,512]{1,0:T(8,128)(2,1)S(1)}, u32[]{:S(2)}, u32[]{:S(2)}) %collective-permute-start.8) | collective-permute-done | bytes 131104 | tf_op jit(solution)/shard_map/ppermute | solution.py:48
  21.9 2.5 %collective-permute-start.2 = (bf16[256,512]{1,0:T(8,128)(2,1)S(1)}, bf16[256,512]{1,0:T(8,128)(2,1)S(1)}, u32[]{:S(2)}, u32[]{:S(2)}) collective-permute-start(bf16[256,512]{1,0:T(8,128)(2,1)S(1)} %pad_maximum_fusion.refs_0_.refs_8_), channel_id=1, source_target_pairs={{0,2},{1,3},{2,4},{3,5},{4,6},{5,7},{8,10},{9,11},{10,12},{11,13},... | collective-permute-start | bytes 786440 | tf_op jit(solution)/shard_map/ppermute | solution.py:37
  24.4 1.3 collective-permute-start.14
  25.7 1.3 collective-permute-start.12
  27.0 8.2 %collective-permute-start.10 = (bf16[256,512]{1,0:T(8,128)(2,1)S(1)}, bf16[256,512]{1,0:T(8,128)(2,1)S(1)}, u32[]{:S(2)}, u32[]{:S(2)}) collective-permute-start(bf16[256,512]{1,0:T(8,128)(2,1)S(1)} %pad_maximum_fusion.1.refs_0_.refs_8_), channel_id=1, source_target_pairs={{0,2},{1,3},{2,4},{3,5},{4,6},{5,7},{8,10},{9,11},{10,12},{11,13},... | collective-permute-start | bytes 786440 | tf_op jit(solution)/shard_map/ppermute | solution.py:37
  35.3 0.1 collective-permute-start.22
  35.4 0.5 collective-permute-start.20
  35.9 1.8 %collective-permute-done.14.refs_6_.refs_14_ = bf16[256,512]{1,0:T(8,128)(2,1)S(1)} collective-permute-done((bf16[256,512]{1,0:T(8,128)(2,1)S(1)}, bf16[256,512]{1,0:T(8,128)(2,1)S(1)}, u32[]{:S(2)}, u32[]{:S(2)}) %collective-permute-start.14) | collective-permute-done | bytes 262176 | tf_op jit(solution)/shard_map/ppermute | solution.py:37
  37.7 5.6 %collective-permute-done.12.refs_4_.refs_12_ = bf16[256,512]{1,0:T(8,128)(2,1)S(1)} collective-permute-done((bf16[256,512]{1,0:T(8,128)(2,1)S(1)}, bf16[256,512]{1,0:T(8,128)(2,1)S(1)}, u32[]{:S(2)}, u32[]{:S(2)}) %collective-permute-start.12) | collective-permute-done | bytes 262176 | tf_op jit(solution)/shard_map/ppermute | solution.py:37
  43.3 1.4 collective-permute-start.4
  44.7 0.6 pad_add_fusion.info
  45.3 2.9 %collective-permute-done.10.refs_2_.refs_10_ = bf16[256,512]{1,0:T(8,128)(2,1)S(1)} collective-permute-done((bf16[256,512]{1,0:T(8,128)(2,1)S(1)}, bf16[256,512]{1,0:T(8,128)(2,1)S(1)}, u32[]{:S(2)}, u32[]{:S(2)}) %collective-permute-start.10) | collective-permute-done | bytes 262176 | tf_op jit(solution)/shard_map/ppermute | solution.py:37
  48.2 0.5 collective-permute-start.15
  48.7 0.1 collective-permute-start.13
  48.8 0.4 collective-permute-start.11
  49.2 1.4 collective-permute-start.6
  50.6 13.6 %teacher.3.target_ref = bf16[512,256]{1,0:T(8,128)(2,1)} custom-call(s32[3]{0:T(128)} %pad_add_fusion.info, bf16[256,4096]{1,0:T(8,128)(2,1)} %bitcast.88, bf16[256,512]{1,0:T(8,128)(2,1)} %copy-done.4, bf16[256,512]{1,0:T(8,128)(2,1)} %copy-done.18, bf16[256,512]{1,0:T(8,128)(2,1)} %copy-done.17, bf16[256,512]{1,0:T(8,128)(2,1)} %collective-permute-done.18.refs_3_.refs_11_, ...), custom_call_target="tpu_custom_call" | custom-call | flops 4294967296 | bytes 1048576 | tf_op jit(solution)/shard_map/teacher/pallas_call | solution.py:195
  64.2 0.1 collective-permute-start.1
  64.4 0.5 collective-permute-start.3
  64.9 0.1 collective-permute-start.5
  65.0 0.4 collective-permute-start.7
  65.4 0.2 copy-done.21
  65.6 10.9 %student.3 = (f32[128,512]{1,0:T(8,128)}, bf16[128,512]{1,0:T(8,128)(2,1)}, f32[1,256]{1,0:T(1,128)}, f32[4,256,256]{2,1,0:T(8,128)}, bf16[4,256,256]{2,1,0:T(8,128)(2,1)}) custom-call(s32[3]{0:T(128)} %pad_add_fusion.info, bf16[128,2048]{1,0:T(8,128)(2,1)} %bitcast.86, bf16[128,1024]{1,0:T(8,128)(2,1)} %copy-done.10, bf16[512,256]{1,0:T(8,128)(2,1)} %teacher.3.target_ref, ...), custom_call_target="tpu_custom_call" | custom-call | flops 3221225472 | bytes 2097152 | tf_op jit(solution)/shard_map/student/pallas_call | solution.py:348
  76.4 1.5 collective-permute-start.24
  78.0 0.6 copy-done.22
  78.6 0.1 copy-done.23
  78.7 0.1 copy-done.24
  78.8 0.7 copy-done.25
  79.5 13.8 %teacher.2.target_ref = bf16[512,256]{1,0:T(8,128)(2,1)} custom-call(s32[3]{0:T(128)} %pad_add_fusion.info, bf16[256,4096]{1,0:T(8,128)(2,1)} %bitcast.89, bf16[256,512]{1,0:T(8,128)(2,1)} %copy-done.6, bf16[256,512]{1,0:T(8,128)(2,1)} %copy-done.22, bf16[256,512]{1,0:T(8,128)(2,1)} %copy-done.15, bf16[256,512]{1,0:T(8,128)(2,1)} %copy-done.23, ...), custom_call_target="tpu_custom_call" | custom-call | flops 4294967296 | bytes 1048576 | tf_op jit(solution)/shard_map/teacher/pallas_call | solution.py:195
  93.3 10.8 %student.2 = (f32[128,512]{1,0:T(8,128)}, bf16[128,512]{1,0:T(8,128)(2,1)}, f32[1,256]{1,0:T(1,128)}, f32[4,256,256]{2,1,0:T(8,128)}, bf16[4,256,256]{2,1,0:T(8,128)(2,1)}) custom-call(s32[3]{0:T(128)} %pad_add_fusion.info, bf16[128,2048]{1,0:T(8,128)(2,1)} %bitcast.87, bf16[128,1024]{1,0:T(8,128)(2,1)} %copy-done.10, bf16[512,256]{1,0:T(8,128)(2,1)} %teacher.2.target_ref, ...), custom_call_target="tpu_custom_call" | custom-call | flops 3221225472 | bytes 2097152 | tf_op jit(solution)/shard_map/student/pallas_call | solution.py:348
  104.1 0.7 add.63
  104.8 0.5 collective-permute-start.35
  105.4 1.6 collective-permute-start.23
  106.9 1.4 collective-permute-done.35
  108.4 0.5 fusion.10
  108.9 0.2 fusion.12
  109.1 1.4 collective-permute-start.30
  110.5 1.3 collective-permute-start.32
  111.8 1.3 collective-permute-start.31
  113.2 1.1 maximum_select_fusion
  114.3 17.1 %collective-permute-done.30 = bf16[256,256]{1,0:T(8,128)(2,1)S(1)} collective-permute-done((bf16[256,256]{1,0:T(8,128)(2,1)S(1)}, bf16[256,256]{1,0:T(8,128)(2,1)S(1)}, u32[]{:S(2)}, u32[]{:S(2)}) %collective-permute-start.30) | collective-permute-done | bytes 131104 | tf_op jit(solution)/shard_map/ppermute | solution.py:43
  131.4 15.3 %collective-permute-done.32 = bf16[256,256]{1,0:T(8,128)(2,1)S(1)} collective-permute-done((bf16[256,256]{1,0:T(8,128)(2,1)S(1)}, bf16[256,256]{1,0:T(8,128)(2,1)S(1)}, u32[]{:S(2)}, u32[]{:S(2)}) %collective-permute-start.32) | collective-permute-done | bytes 131104 | tf_op jit(solution)/shard_map/ppermute | solution.py:43
  146.7 0.1 fusion.2
  146.8 0.6 collective-permute-start.34
  147.4 3.7 %collective-permute-done.34 = bf16[128,256]{1,0:T(8,128)(2,1)S(1)} collective-permute-done((bf16[128,256]{1,0:T(8,128)(2,1)S(1)}, bf16[128,256]{1,0:T(8,128)(2,1)S(1)}, u32[]{:S(2)}, u32[]{:S(2)}) %collective-permute-start.34) | collective-permute-done | bytes 65568 | tf_op jit(solution)/shard_map/ppermute | solution.py:48
  151.2 0.2 fusion.11
  151.4 1.3 collective-permute-start.26
  152.7 1.3 collective-permute-start.28
  154.0 1.3 collective-permute-start.27
  155.3 4.0 %collective-permute-done.26 = bf16[256,256]{1,0:T(8,128)(2,1)S(1)} collective-permute-done((bf16[256,256]{1,0:T(8,128)(2,1)S(1)}, bf16[256,256]{1,0:T(8,128)(2,1)S(1)}, u32[]{:S(2)}, u32[]{:S(2)}) %collective-permute-start.26) | collective-permute-done | bytes 131104 | tf_op jit(solution)/shard_map/ppermute | solution.py:43
  159.2 2.1 %collective-permute-done.28 = bf16[256,256]{1,0:T(8,128)(2,1)S(1)} collective-permute-done((bf16[256,256]{1,0:T(8,128)(2,1)S(1)}, bf16[256,256]{1,0:T(8,128)(2,1)S(1)}, u32[]{:S(2)}, u32[]{:S(2)}) %collective-permute-start.28) | collective-permute-done | bytes 131104 | tf_op jit(solution)/shard_map/ppermute | solution.py:43
  161.3 4.4 %collective-permute-done.27 = bf16[256,256]{1,0:T(8,128)(2,1)S(1)} collective-permute-done((bf16[256,256]{1,0:T(8,128)(2,1)S(1)}, bf16[256,256]{1,0:T(8,128)(2,1)S(1)}, u32[]{:S(2)}, u32[]{:S(2)}) %collective-permute-start.27) | collective-permute-done | bytes 131104 | tf_op jit(solution)/shard_map/ppermute | solution.py:43
  165.7 0.1 fusion.5
  165.8 0.6 collective-permute-start.33
  166.5 3.7 %collective-permute-done.33 = bf16[128,256]{1,0:T(8,128)(2,1)S(1)} collective-permute-done((bf16[128,256]{1,0:T(8,128)(2,1)S(1)}, bf16[128,256]{1,0:T(8,128)(2,1)S(1)}, u32[]{:S(2)}, u32[]{:S(2)}) %collective-permute-start.33) | collective-permute-done | bytes 65568 | tf_op jit(solution)/shard_map/ppermute | solution.py:48
  170.2 0.7 maximum_select_fusion.2
  170.9 0.7 maximum_select_fusion.1
  (94 shorter events, 0.4 us)
Async XLA Ops:
  0.6 12.1 %copy-start.7 = (bf16[1,128,512]{2,1,0:T(8,128)(2,1)S(1)}, bf16[1,128,512]{2,1,0:T(8,128)(2,1)}, u32[]{:S(2)}) copy-start(bf16[1,128,512]{2,1,0:T(8,128)(2,1)} %param.13) | copy-start | bytes 393220
  0.6 12.1 %copy-start.8 = (bf16[1,128,512]{2,1,0:T(8,128)(2,1)S(1)}, bf16[1,128,512]{2,1,0:T(8,128)(2,1)}, u32[]{:S(2)}) copy-start(bf16[1,128,512]{2,1,0:T(8,128)(2,1)} %param.12) | copy-start | bytes 393220
  1.9 48.7 %copy-start.4 = (bf16[256,512]{1,0:T(8,128)(2,1)}, bf16[256,512]{1,0:T(8,128)(2,1)S(1)}, u32[]{:S(2)}) copy-start(bf16[256,512]{1,0:T(8,128)(2,1)S(1)} %pad_maximum_fusion.2.refs_0_.refs_8_) | copy-start | bytes 786436
  1.9 22.5 %collective-permute-start.21 = (bf16[256,512]{1,0:T(8,128)(2,1)S(1)}, bf16[256,512]{1,0:T(8,128)(2,1)S(1)}, u32[]{:S(2)}, u32[]{:S(2)}) collective-permute-start(bf16[256,512]{1,0:T(8,128)(2,1)S(1)} %pad_maximum_fusion.2.refs_0_.refs_8_), channel_id=1, source_target_pairs={{0,6},{1,7},{8,14},{9,15},{16,22},{17,23},{24,30},{25,31}} | collective-permute-start | bytes 786440 | tf_op jit(solution)/shard_map/ppermute | solution.py:37
  8.9 16.8 %collective-permute-start.19 = (bf16[256,512]{1,0:T(8,128)(2,1)S(1)}, bf16[256,512]{1,0:T(8,128)(2,1)S(1)}, u32[]{:S(2)}, u32[]{:S(2)}) collective-permute-start(bf16[256,512]{1,0:T(8,128)(2,1)S(1)} %pad_maximum_fusion.2.refs_0_.refs_8_), channel_id=1, source_target_pairs={{0,4},{1,5},{2,6},{3,7},{8,12},{9,13},{10,14},{11,15},{16,20},{17,... | collective-permute-start | bytes 786440 | tf_op jit(solution)/shard_map/ppermute | solution.py:37
  11.2 10.7 %collective-permute-start = (bf16[128,1024]{1,0:T(8,128)(2,1)S(1)}, bf16[128,1024]{1,0:T(8,128)(2,1)S(1)}, u32[]{:S(2)}, u32[]{:S(2)}) collective-permute-start(bf16[128,1024]{1,0:T(8,128)(2,1)S(1)} %dynamic-slice_bitcast_fusion), channel_id=1, source_target_pairs={{0,8},{8,0},{16,24},{24,16},{1,9},{9,1},{17,25},{25,17},{2,10},{10... | collective-permute-start | bytes 786440 | tf_op jit(solution)/shard_map/ppermute | solution.py:48
  12.8 9.0 %collective-permute-start.8 = (bf16[128,512]{1,0:T(8,128)(2,1)S(1)}, bf16[128,512]{1,0:T(8,128)(2,1)S(1)}, u32[]{:S(2)}, u32[]{:S(2)}) collective-permute-start(bf16[128,512]{1,0:T(8,128)(2,1)S(1)} %pad_maximum_fusion.3), channel_id=1, source_target_pairs={{0,8},{8,0},{16,24},{24,16},{1,9},{9,1},{17,25},{25,17},{2,10},{10... | collective-permute-start | bytes 393224 | tf_op jit(solution)/shard_map/ppermute | solution.py:48
  13.4 13.6 %collective-permute-start.17 = (bf16[256,512]{1,0:T(8,128)(2,1)S(1)}, bf16[256,512]{1,0:T(8,128)(2,1)S(1)}, u32[]{:S(2)}, u32[]{:S(2)}) collective-permute-start(bf16[256,512]{1,0:T(8,128)(2,1)S(1)} %pad_maximum_fusion.2.refs_0_.refs_8_), channel_id=1, source_target_pairs={{0,2},{1,3},{2,4},{3,5},{4,6},{5,7},{8,10},{9,11},{10,12},{11,13},... | collective-permute-start | bytes 786440 | tf_op jit(solution)/shard_map/ppermute | solution.py:37
  15.9 48.3 %copy-start.6 = (bf16[256,512]{1,0:T(8,128)(2,1)}, bf16[256,512]{1,0:T(8,128)(2,1)S(1)}, u32[]{:S(2)}) copy-start(bf16[256,512]{1,0:T(8,128)(2,1)S(1)} %pad_maximum_fusion.refs_0_.refs_8_) | copy-start | bytes 786436
  21.8 13.5 %collective-permute-start.16 = (bf16[256,512]{1,0:T(8,128)(2,1)S(1)}, bf16[256,512]{1,0:T(8,128)(2,1)S(1)}, u32[]{:S(2)}, u32[]{:S(2)}) collective-permute-start(bf16[256,512]{1,0:T(8,128)(2,1)S(1)} %pad_maximum_fusion.2.refs_0_.refs_8_), channel_id=1, source_target_pairs={{0,1},{1,0},{2,3},{3,2},{4,5},{5,4},{6,7},{7,6},{8,9},{9,8},{10,11... | collective-permute-start | bytes 786440 | tf_op jit(solution)/shard_map/ppermute | solution.py:48
  21.8 42.3 %copy-start.5 = (bf16[256,512]{1,0:T(8,128)(2,1)}, bf16[256,512]{1,0:T(8,128)(2,1)S(1)}, u32[]{:S(2)}) copy-start(bf16[256,512]{1,0:T(8,128)(2,1)S(1)} %pad_maximum_fusion.1.refs_0_.refs_8_) | copy-start | bytes 786436
  21.9 42.3 %copy-start.10 = (bf16[128,1024]{1,0:T(8,128)(2,1)}, bf16[128,1024]{1,0:T(8,128)(2,1)S(1)}, u32[]{:S(2)}) copy-start(bf16[128,1024]{1,0:T(8,128)(2,1)S(1)} %collective-permute-done.far_q_ref) | copy-start | bytes 786436
  21.9 13.5 %collective-permute-start.2 = (bf16[256,512]{1,0:T(8,128)(2,1)S(1)}, bf16[256,512]{1,0:T(8,128)(2,1)S(1)}, u32[]{:S(2)}, u32[]{:S(2)}) collective-permute-start(bf16[256,512]{1,0:T(8,128)(2,1)S(1)} %pad_maximum_fusion.refs_0_.refs_8_), channel_id=1, source_target_pairs={{0,2},{1,3},{2,4},{3,5},{4,6},{5,7},{8,10},{9,11},{10,12},{11,13},... | collective-permute-start | bytes 786440 | tf_op jit(solution)/shard_map/ppermute | solution.py:37
  24.4 26.2 %copy-start.11 = (bf16[256,512]{1,0:T(8,128)(2,1)}, bf16[256,512]{1,0:T(8,128)(2,1)S(1)}, u32[]{:S(2)}) copy-start(bf16[256,512]{1,0:T(8,128)(2,1)S(1)} %collective-permute-done.21.refs_6_.refs_14_) | copy-start | bytes 786436
  24.4 13.3 %collective-permute-start.14 = (bf16[256,512]{1,0:T(8,128)(2,1)S(1)}, bf16[256,512]{1,0:T(8,128)(2,1)S(1)}, u32[]{:S(2)}, u32[]{:S(2)}) collective-permute-start(bf16[256,512]{1,0:T(8,128)(2,1)S(1)} %pad_maximum_fusion.1.refs_0_.refs_8_), channel_id=1, source_target_pairs={{0,6},{1,7},{8,14},{9,15},{16,22},{17,23},{24,30},{25,31}} | collective-permute-start | bytes 786440 | tf_op jit(solution)/shard_map/ppermute | solution.py:37
  25.7 24.9 %copy-start.12 = (bf16[256,512]{1,0:T(8,128)(2,1)}, bf16[256,512]{1,0:T(8,128)(2,1)S(1)}, u32[]{:S(2)}) copy-start(bf16[256,512]{1,0:T(8,128)(2,1)S(1)} %collective-permute-done.19.refs_4_.refs_12_) | copy-start | bytes 786436
  25.7 17.6 %collective-permute-start.12 = (bf16[256,512]{1,0:T(8,128)(2,1)S(1)}, bf16[256,512]{1,0:T(8,128)(2,1)S(1)}, u32[]{:S(2)}, u32[]{:S(2)}) collective-permute-start(bf16[256,512]{1,0:T(8,128)(2,1)S(1)} %pad_maximum_fusion.1.refs_0_.refs_8_), channel_id=1, source_target_pairs={{0,4},{1,5},{2,6},{3,7},{8,12},{9,13},{10,14},{11,15},{16,20},{17,... | collective-permute-start | bytes 786440 | tf_op jit(solution)/shard_map/ppermute | solution.py:37
  27.0 23.6 %copy-start.17 = (bf16[256,512]{1,0:T(8,128)(2,1)}, bf16[256,512]{1,0:T(8,128)(2,1)S(1)}, u32[]{:S(2)}) copy-start(bf16[256,512]{1,0:T(8,128)(2,1)S(1)} %collective-permute-done.17.refs_2_.refs_10_) | copy-start | bytes 786436
  27.0 21.1 %collective-permute-start.10 = (bf16[256,512]{1,0:T(8,128)(2,1)S(1)}, bf16[256,512]{1,0:T(8,128)(2,1)S(1)}, u32[]{:S(2)}, u32[]{:S(2)}) collective-permute-start(bf16[256,512]{1,0:T(8,128)(2,1)S(1)} %pad_maximum_fusion.1.refs_0_.refs_8_), channel_id=1, source_target_pairs={{0,2},{1,3},{2,4},{3,5},{4,6},{5,7},{8,10},{9,11},{10,12},{11,13},... | collective-permute-start | bytes 786440 | tf_op jit(solution)/shard_map/ppermute | solution.py:37
  35.3 8.0 %copy-start.18 = (bf16[256,512]{1,0:T(8,128)(2,1)}, bf16[256,512]{1,0:T(8,128)(2,1)S(1)}, u32[]{:S(2)}) copy-start(bf16[256,512]{1,0:T(8,128)(2,1)S(1)} %collective-permute-done.16.refs_1_.refs_9_) | copy-start | bytes 786436
  35.3 12.9 %collective-permute-start.22 = (bf16[256,512]{1,0:T(8,128)(2,1)S(1)}, bf16[256,512]{1,0:T(8,128)(2,1)}, u32[]{:S(2)}, u32[]{:S(2)}) collective-permute-start(bf16[256,512]{1,0:T(8,128)(2,1)S(1)} %collective-permute-done.21.refs_6_.refs_14_), channel_id=1, source_target_pairs={{0,1},{1,0},{2,3},{3,2},{4,5},{5,4},{6,7},{7,6},{8,9},{9,8},{10,11... | collective-permute-start | bytes 786440 | tf_op jit(solution)/shard_map/ppermute | solution.py:48
  35.4 29.0 %copy-start.15 = (bf16[256,512]{1,0:T(8,128)(2,1)}, bf16[256,512]{1,0:T(8,128)(2,1)S(1)}, u32[]{:S(2)}) copy-start(bf16[256,512]{1,0:T(8,128)(2,1)S(1)} %collective-permute-done.2.refs_2_.refs_10_) | copy-start | bytes 786436
  35.4 13.3 %collective-permute-start.20 = (bf16[256,512]{1,0:T(8,128)(2,1)S(1)}, bf16[256,512]{1,0:T(8,128)(2,1)}, u32[]{:S(2)}, u32[]{:S(2)}) collective-permute-start(bf16[256,512]{1,0:T(8,128)(2,1)S(1)} %collective-permute-done.19.refs_4_.refs_12_), channel_id=1, source_target_pairs={{0,1},{1,0},{2,3},{3,2},{4,5},{5,4},{6,7},{7,6},{8,9},{9,8},{10,11... | collective-permute-start | bytes 786440 | tf_op jit(solution)/shard_map/ppermute | solution.py:48
  37.7 26.5 %copy-start.13 = (bf16[256,512]{1,0:T(8,128)(2,1)}, bf16[256,512]{1,0:T(8,128)(2,1)S(1)}, u32[]{:S(2)}) copy-start(bf16[256,512]{1,0:T(8,128)(2,1)S(1)} %collective-permute-done.14.refs_6_.refs_14_) | copy-start | bytes 786436
  37.7 11.1 %collective-permute-start.18 = (bf16[256,512]{1,0:T(8,128)(2,1)S(1)}, bf16[256,512]{1,0:T(8,128)(2,1)}, u32[]{:S(2)}, u32[]{:S(2)}) collective-permute-start(bf16[256,512]{1,0:T(8,128)(2,1)S(1)} %collective-permute-done.17.refs_2_.refs_10_), channel_id=1, source_target_pairs={{0,1},{1,0},{2,3},{3,2},{4,5},{5,4},{6,7},{7,6},{8,9},{9,8},{10,11... | collective-permute-start | bytes 786440 | tf_op jit(solution)/shard_map/ppermute | solution.py:48
  43.3 20.9 %copy-start.14 = (bf16[256,512]{1,0:T(8,128)(2,1)}, bf16[256,512]{1,0:T(8,128)(2,1)S(1)}, u32[]{:S(2)}) copy-start(bf16[256,512]{1,0:T(8,128)(2,1)S(1)} %collective-permute-done.12.refs_4_.refs_12_) | copy-start | bytes 786436
  43.3 5.9 %collective-permute-start.4 = (bf16[256,512]{1,0:T(8,128)(2,1)S(1)}, bf16[256,512]{1,0:T(8,128)(2,1)}, u32[]{:S(2)}, u32[]{:S(2)}) collective-permute-start(bf16[256,512]{1,0:T(8,128)(2,1)S(1)} %collective-permute-done.2.refs_2_.refs_10_), channel_id=1, source_target_pairs={{2,4},{3,5},{4,6},{5,7},{10,12},{11,13},{12,14},{13,15},{18,20},{1... | collective-permute-start | bytes 786440 | tf_op jit(solution)/shard_map/ppermute | solution.py:37
  48.2 16.0 %copy-start.16 = (bf16[256,512]{1,0:T(8,128)(2,1)}, bf16[256,512]{1,0:T(8,128)(2,1)S(1)}, u32[]{:S(2)}) copy-start(bf16[256,512]{1,0:T(8,128)(2,1)S(1)} %collective-permute-done.10.refs_2_.refs_10_) | copy-start | bytes 786436
  48.2 16.0 %collective-permute-start.9 = (bf16[256,512]{1,0:T(8,128)(2,1)S(1)}, bf16[256,512]{1,0:T(8,128)(2,1)S(1)}, u32[]{:S(2)}, u32[]{:S(2)}) collective-permute-start(bf16[256,512]{1,0:T(8,128)(2,1)S(1)} %pad_maximum_fusion.1.refs_0_.refs_8_), channel_id=1, source_target_pairs={{0,1},{1,0},{2,3},{3,2},{4,5},{5,4},{6,7},{7,6},{8,9},{9,8},{10,11... | collective-permute-start | bytes 786440 | tf_op jit(solution)/shard_map/ppermute | solution.py:48
  48.2 16.2 %collective-permute-start.15 = (bf16[256,512]{1,0:T(8,128)(2,1)S(1)}, bf16[256,512]{1,0:T(8,128)(2,1)S(1)}, u32[]{:S(2)}, u32[]{:S(2)}) collective-permute-start(bf16[256,512]{1,0:T(8,128)(2,1)S(1)} %collective-permute-done.14.refs_6_.refs_14_), channel_id=1, source_target_pairs={{0,1},{1,0},{2,3},{3,2},{4,5},{5,4},{6,7},{7,6},{8,9},{9,8},{10,11... | collective-permute-start | bytes 786440 | tf_op jit(solution)/shard_map/ppermute | solution.py:48
  48.7 16.2 %collective-permute-start.13 = (bf16[256,512]{1,0:T(8,128)(2,1)S(1)}, bf16[256,512]{1,0:T(8,128)(2,1)S(1)}, u32[]{:S(2)}, u32[]{:S(2)}) collective-permute-start(bf16[256,512]{1,0:T(8,128)(2,1)S(1)} %collective-permute-done.12.refs_4_.refs_12_), channel_id=1, source_target_pairs={{0,1},{1,0},{2,3},{3,2},{4,5},{5,4},{6,7},{7,6},{8,9},{9,8},{10,11... | collective-permute-start | bytes 786440 | tf_op jit(solution)/shard_map/ppermute | solution.py:48
  48.8 16.6 %collective-permute-start.11 = (bf16[256,512]{1,0:T(8,128)(2,1)S(1)}, bf16[256,512]{1,0:T(8,128)(2,1)}, u32[]{:S(2)}, u32[]{:S(2)}) collective-permute-start(bf16[256,512]{1,0:T(8,128)(2,1)S(1)} %collective-permute-done.10.refs_2_.refs_10_), channel_id=1, source_target_pairs={{0,1},{1,0},{2,3},{3,2},{4,5},{5,4},{6,7},{7,6},{8,9},{9,8},{10,11... | collective-permute-start | bytes 786440 | tf_op jit(solution)/shard_map/ppermute | solution.py:48
  49.2 15.7 %collective-permute-start.6 = (bf16[256,512]{1,0:T(8,128)(2,1)}, bf16[256,512]{1,0:T(8,128)(2,1)}, u32[]{:S(2)}, u32[]{:S(2)}) collective-permute-start(bf16[256,512]{1,0:T(8,128)(2,1)} %collective-permute-done.4.refs_4_.refs_12_), channel_id=1, source_target_pairs={{4,6},{5,7},{12,14},{13,15},{20,22},{21,23},{28,30},{29,31}} | collective-permute-start | bytes 786440 | tf_op jit(solution)/shard_map/ppermute | solution.py:37
  64.2 1.2 copy-start.19
  64.2 13.7 %collective-permute-start.1 = (bf16[256,512]{1,0:T(8,128)(2,1)S(1)}, bf16[256,512]{1,0:T(8,128)(2,1)S(1)}, u32[]{:S(2)}, u32[]{:S(2)}) collective-permute-start(bf16[256,512]{1,0:T(8,128)(2,1)S(1)} %pad_maximum_fusion.refs_0_.refs_8_), channel_id=1, source_target_pairs={{0,1},{1,0},{2,3},{3,2},{4,5},{5,4},{6,7},{7,6},{8,9},{9,8},{10,11... | collective-permute-start | bytes 786440 | tf_op jit(solution)/shard_map/ppermute | solution.py:48
  64.4 1.0 copy-start.20
  64.4 13.6 %collective-permute-start.3 = (bf16[256,512]{1,0:T(8,128)(2,1)S(1)}, bf16[256,512]{1,0:T(8,128)(2,1)S(1)}, u32[]{:S(2)}, u32[]{:S(2)}) collective-permute-start(bf16[256,512]{1,0:T(8,128)(2,1)S(1)} %collective-permute-done.2.refs_2_.refs_10_), channel_id=1, source_target_pairs={{0,1},{1,0},{2,3},{3,2},{4,5},{5,4},{6,7},{7,6},{8,9},{9,8},{10,11... | collective-permute-start | bytes 786440 | tf_op jit(solution)/shard_map/ppermute | solution.py:48
  64.9 0.7 copy-start.21
  64.9 13.1 %collective-permute-start.5 = (bf16[256,512]{1,0:T(8,128)(2,1)}, bf16[256,512]{1,0:T(8,128)(2,1)S(1)}, u32[]{:S(2)}, u32[]{:S(2)}) collective-permute-start(bf16[256,512]{1,0:T(8,128)(2,1)} %collective-permute-done.4.refs_4_.refs_12_), channel_id=1, source_target_pairs={{0,1},{1,0},{2,3},{3,2},{4,5},{5,4},{6,7},{7,6},{8,9},{9,8},{10,11... | collective-permute-start | bytes 786440 | tf_op jit(solution)/shard_map/ppermute | solution.py:48
  65.0 13.0 %collective-permute-start.7 = (bf16[256,512]{1,0:T(8,128)(2,1)}, bf16[256,512]{1,0:T(8,128)(2,1)S(1)}, u32[]{:S(2)}, u32[]{:S(2)}) collective-permute-start(bf16[256,512]{1,0:T(8,128)(2,1)} %collective-permute-done.6.refs_6_.refs_14_), channel_id=1, source_target_pairs={{0,1},{1,0},{2,3},{3,2},{4,5},{5,4},{6,7},{7,6},{8,9},{9,8},{10,11... | collective-permute-start | bytes 786440 | tf_op jit(solution)/shard_map/ppermute | solution.py:48
  76.4 28.9 %collective-permute-start.24 = (bf16[128,512]{1,0:T(8,128)(2,1)}, bf16[128,512]{1,0:T(8,128)(2,1)S(1)}, u32[]{:S(2)}, u32[]{:S(2)}) collective-permute-start(bf16[128,512]{1,0:T(8,128)(2,1)} %get-tuple-element.17), channel_id=1, source_target_pairs={{0,8},{8,0},{16,24},{24,16},{1,9},{9,1},{17,25},{25,17},{2,10},{10... | collective-permute-start | bytes 393224 | tf_op jit(solution)/shard_map/ppermute | solution.py:48
  77.9 0.7 copy-start.22
  77.9 31.0 %collective-permute-start.29 = (bf16[4,256,256]{2,1,0:T(8,128)(2,1)}, bf16[4,256,256]{2,1,0:T(8,128)(2,1)S(1)}, u32[]{:S(2)}, u32[]{:S(2)}) collective-permute-start(bf16[4,256,256]{2,1,0:T(8,128)(2,1)} %get-tuple-element.21), channel_id=1, source_target_pairs={{0,1},{1,0},{2,3},{3,2},{4,5},{5,4},{6,7},{7,6},{8,9},{9,8},{10,11... | collective-permute-start | bytes 1572872 | tf_op jit(solution)/shard_map/ppermute | solution.py:48
  78.0 0.8 copy-start.23
  78.0 0.8 copy-start.24
  78.8 0.7 copy-start.25
  93.3 10.8 %copy-start.9 = (f32[1,256]{1,0:T(1,128)S(1)}, f32[1,256]{1,0:T(1,128)}, u32[]{:S(2)}) copy-start(f32[1,256]{1,0:T(1,128)} %get-tuple-element.23) | copy-start | bytes 3076
  93.3 15.6 %copy-start.1 = (f32[4,256,256]{2,1,0:T(8,128)S(1)}, f32[4,256,256]{2,1,0:T(8,128)}, u32[]{:S(2)}) copy-start(f32[4,256,256]{2,1,0:T(8,128)} %get-tuple-element.20) | copy-start | bytes 3145732
  104.8 3.6 %collective-permute-start.35 = (f32[128]{0:T(128)S(1)}, f32[128]{0:T(128)S(1)}, u32[]{:S(2)}, u32[]{:S(2)}) collective-permute-start(f32[128]{0:T(128)S(1)} %fusion.9), channel_id=1, source_target_pairs={{0,8},{8,0},{16,24},{24,16},{1,9},{9,1},{17,25},{25,17},{2,10},{10... | collective-permute-start | bytes 1544 | tf_op jit(solution)/shard_map/ppermute | solution.py:48
  105.4 7.8 %collective-permute-start.23 = (bf16[128,512]{1,0:T(8,128)(2,1)}, bf16[128,512]{1,0:T(8,128)(2,1)S(1)}, u32[]{:S(2)}, u32[]{:S(2)}) collective-permute-start(bf16[128,512]{1,0:T(8,128)(2,1)} %get-tuple-element.16), channel_id=1, source_target_pairs={{0,8},{8,0},{16,24},{24,16},{1,9},{9,1},{17,25},{25,17},{2,10},{10... | collective-permute-start | bytes 393224 | tf_op jit(solution)/shard_map/ppermute | solution.py:48
  106.9 44.2 %collective-permute-start.25 = (bf16[4,256,256]{2,1,0:T(8,128)(2,1)}, bf16[4,256,256]{2,1,0:T(8,128)(2,1)S(1)}, u32[]{:S(2)}, u32[]{:S(2)}) collective-permute-start(bf16[4,256,256]{2,1,0:T(8,128)(2,1)} %get-tuple-element.19), channel_id=1, source_target_pairs={{0,1},{1,0},{2,3},{3,2},{4,5},{5,4},{6,7},{7,6},{8,9},{9,8},{10,11... | collective-permute-start | bytes 1572872 | tf_op jit(solution)/shard_map/ppermute | solution.py:48
  108.9 4.3 %copy-start.2 = (f32[128,512]{1,0:T(8,128)S(1)}, f32[128,512]{1,0:T(8,128)}, u32[]{:S(2)}) copy-start(f32[128,512]{1,0:T(8,128)} %get-tuple-element.15) | copy-start | bytes 786436
  108.9 4.3 %copy-start.3 = (f32[128,512]{1,0:T(8,128)S(1)}, f32[128,512]{1,0:T(8,128)}, u32[]{:S(2)}) copy-start(f32[128,512]{1,0:T(8,128)} %get-tuple-element.14) | copy-start | bytes 786436
  109.1 42.0 %copy-start = (f32[4,256,256]{2,1,0:T(8,128)S(1)}, f32[4,256,256]{2,1,0:T(8,128)}, u32[]{:S(2)}) copy-start(f32[4,256,256]{2,1,0:T(8,128)} %get-tuple-element.18) | copy-start | bytes 3145732
  109.1 22.3 %collective-permute-start.30 = (bf16[256,256]{1,0:T(8,128)(2,1)S(1)}, bf16[256,256]{1,0:T(8,128)(2,1)S(1)}, u32[]{:S(2)}, u32[]{:S(2)}) collective-permute-start(bf16[256,256]{1,0:T(8,128)(2,1)S(1)} %get-tuple-element.31), channel_id=1, source_target_pairs={{2,0},{3,1},{4,2},{5,3},{6,4},{7,5},{10,8},{11,9},{12,10},{13,11},... | collective-permute-start | bytes 393224 | tf_op jit(solution)/shard_map/ppermute | solution.py:43
  110.5 36.2 %collective-permute-start.32 = (bf16[256,256]{1,0:T(8,128)(2,1)S(1)}, bf16[256,256]{1,0:T(8,128)(2,1)S(1)}, u32[]{:S(2)}, u32[]{:S(2)}) collective-permute-start(bf16[256,256]{1,0:T(8,128)(2,1)S(1)} %get-tuple-element.32), channel_id=1, source_target_pairs={{6,0},{7,1},{14,8},{15,9},{22,16},{23,17},{30,24},{31,25}} | collective-permute-start | bytes 393224 | tf_op jit(solution)/shard_map/ppermute | solution.py:43
  111.8 34.9 %collective-permute-start.31 = (bf16[256,256]{1,0:T(8,128)(2,1)S(1)}, bf16[256,256]{1,0:T(8,128)(2,1)S(1)}, u32[]{:S(2)}, u32[]{:S(2)}) collective-permute-start(bf16[256,256]{1,0:T(8,128)(2,1)S(1)} %get-tuple-element.33), channel_id=1, source_target_pairs={{4,0},{5,1},{6,2},{7,3},{12,8},{13,9},{14,10},{15,11},{20,16},{21,... | collective-permute-start | bytes 393224 | tf_op jit(solution)/shard_map/ppermute | solution.py:43
  146.8 4.3 %collective-permute-start.34 = (bf16[128,256]{1,0:T(8,128)(2,1)S(1)}, bf16[128,256]{1,0:T(8,128)(2,1)S(1)}, u32[]{:S(2)}, u32[]{:S(2)}) collective-permute-start(bf16[128,256]{1,0:T(8,128)(2,1)S(1)} %slice.174), channel_id=1, source_target_pairs={{0,8},{8,0},{16,24},{24,16},{1,9},{9,1},{17,25},{25,17},{2,10},{10... | collective-permute-start | bytes 196616 | tf_op jit(solution)/shard_map/ppermute | solution.py:48
  151.4 7.9 %collective-permute-start.26 = (bf16[256,256]{1,0:T(8,128)(2,1)S(1)}, bf16[256,256]{1,0:T(8,128)(2,1)S(1)}, u32[]{:S(2)}, u32[]{:S(2)}) collective-permute-start(bf16[256,256]{1,0:T(8,128)(2,1)S(1)} %get-tuple-element.28), channel_id=1, source_target_pairs={{2,0},{3,1},{4,2},{5,3},{6,4},{7,5},{10,8},{11,9},{12,10},{13,11},... | collective-permute-start | bytes 393224 | tf_op jit(solution)/shard_map/ppermute | solution.py:43
  152.7 8.7 %collective-permute-start.28 = (bf16[256,256]{1,0:T(8,128)(2,1)S(1)}, bf16[256,256]{1,0:T(8,128)(2,1)S(1)}, u32[]{:S(2)}, u32[]{:S(2)}) collective-permute-start(bf16[256,256]{1,0:T(8,128)(2,1)S(1)} %get-tuple-element.29), channel_id=1, source_target_pairs={{6,0},{7,1},{14,8},{15,9},{22,16},{23,17},{30,24},{31,25}} | collective-permute-start | bytes 393224 | tf_op jit(solution)/shard_map/ppermute | solution.py:43
  154.0 11.8 %collective-permute-start.27 = (bf16[256,256]{1,0:T(8,128)(2,1)S(1)}, bf16[256,256]{1,0:T(8,128)(2,1)S(1)}, u32[]{:S(2)}, u32[]{:S(2)}) collective-permute-start(bf16[256,256]{1,0:T(8,128)(2,1)S(1)} %get-tuple-element.30), channel_id=1, source_target_pairs={{4,0},{5,1},{6,2},{7,3},{12,8},{13,9},{14,10},{15,11},{20,16},{21,... | collective-permute-start | bytes 393224 | tf_op jit(solution)/shard_map/ppermute | solution.py:43
  165.8 4.3 %collective-permute-start.33 = (bf16[128,256]{1,0:T(8,128)(2,1)S(1)}, bf16[128,256]{1,0:T(8,128)(2,1)S(1)}, u32[]{:S(2)}, u32[]{:S(2)}) collective-permute-start(bf16[128,256]{1,0:T(8,128)(2,1)S(1)} %slice.175), channel_id=1, source_target_pairs={{0,8},{8,0},{16,24},{24,16},{1,9},{9,1},{17,25},{25,17},{2,10},{10... | collective-permute-start | bytes 196616 | tf_op jit(solution)/shard_map/ppermute | solution.py:48
